TPU v7x, 32 devices: a whole 2x2x4 slice. The times are simulated.
32 devices in a mesh: row: 8 (over y, x, core), col: 4 (over z).
Axes of the slice: x: 2, y: 2, z: 4, core: 2. Of those that a mesh axis runs over, the one named last changes fastest.
Arguments:
- fast_pos: float32 [3, 4096], P(None, ('row', 'col')), may hold values from 0 to 1
- fast_vel: float32 [3, 4096], P(None, ('row', 'col')), may hold values from -5 to 5
- fast_charge: float32 [4096], replicated, may hold values from -4 to 4
- fast_owner: int32 [4096], replicated, may hold values from 0 to 1023, as said below
- exclusions: int32 [4096, 4], replicated, may hold values from 0 to 4095, as said below
- slow_pos: float32 [3, 32, 32, 128], P(None, 'row', 'col'), may hold values from 0 to 1
- slow_vel: float32 [3, 32, 32, 128], P(None, 'row', 'col'), may hold values from -5 to 5
- slow_charge: float32 [32, 32, 128], P('row', 'col'), may hold values from -4 to 4
- neighbours: int32 [32, 32, 5], P('row', 'col'), may hold values from 0 to 24, all different within a row
Outputs:
- fast_pos_out: float32 [3, 4096], P(None, ('row', 'col'))
- fast_vel_out: float32 [3, 4096], P(None, ('row', 'col'))
- slow_pos_out: float32 [3, 32, 32, 128], P(None, 'row', 'col')
- slow_vel_out: float32 [3, 32, 32, 128], P(None, 'row', 'col')
Inputs may be any that keep to these rules, and one draw needn't show every extreme that they name: `fast_owner`: atoms a and b with a % (256) == b % (256) share an owner. `exclusions`: the partners of atom a are atoms b != a with b % (256) == a % 256; a partner may repeat. `neighbours`: the entries of one cell are distinct.
All inputs are finite; a program needn't handle non-finite values.
Results may differ from a plain program's by a relative error of at most 0.0003.
Values sent between devices are 32-bit elements; how exact they have to be, the bound alone decides.
No kernel may reach another device: no remote copies, remote signals or barrier semaphores. Data moves between devices by JAX's collectives and lax.ppermute only.
A program may use at most 64 MiB of HBM per device.

v0:
```python
import jax
import jax.numpy as jnp
from jax import lax
from jax.sharding import PartitionSpec as P

FAST = 4096
CELL = 128
INNER = 4


fast_coupling = 1.0
slow_coupling = 0.1
outer_dt = 0.2


def with_halo(x, sides, width):
    for axis, dim in sides:
        count, length = (lax.axis_size(axis), x.shape[dim])
        up = [(i, (i + 1) % count) for i in range(count)]
        down = [(j, i) for i, j in up]
        last = lax.slice_in_dim(x, length - width, length, axis=dim)
        initial = lax.slice_in_dim(x, 0, width, axis=dim)
        before = lax.ppermute(last, axis, up)
        after = lax.ppermute(initial, axis, down)
        x = jnp.concatenate([before, x, after], axis=dim)
    return x


def owner_coords(owner, total_cols):
    grid_row = (owner // total_cols).astype(jnp.float32)
    grid_col = (owner % total_cols).astype(jnp.float32)
    return jnp.stack([grid_row, grid_col, jnp.zeros_like(grid_row)])


def pair_fast(pos_a, cell_a, charge_a, exclude_a, pos_b, cell_b, charge_b, index_b):
    delta = pos_a[:, :, None] - pos_b[:, None, :] + (cell_a[:, :, None] - cell_b[:, None, :])
    dist_sq = jnp.sum(delta * delta, axis=0) + 1.0
    inverse = 1.0 / (dist_sq * jnp.sqrt(dist_sq))
    barred = jnp.any(exclude_a[:, :, None] == index_b[None, None, :], axis=1)
    weight = jnp.where(barred, jnp.float32(0.0), charge_a[:, None] * charge_b[None, :] * inverse)
    return fast_coupling * jnp.sum(weight[None] * delta, axis=2)


def slow_cells(own, views, lists):
    force = jnp.zeros((3,) + own.shape[1:], jnp.float32)
    offsets = jnp.arange(25, dtype=jnp.int32)
    for slot in range(lists.shape[-1]):
        chosen = lists[..., slot]
        pick = (chosen[..., None] == offsets).astype(jnp.float32)
        other = jnp.einsum("abo,oxabn->xabn", pick, views, precision=lax.Precision.HIGHEST)
        shift_row = (chosen // 5 - 2).astype(jnp.float32)
        shift_col = (chosen % 5 - 2).astype(jnp.float32)
        shift = jnp.stack([shift_row, shift_col, jnp.zeros_like(shift_row)])
        delta = own[0:3, :, :, :, None] - (other[0:3, :, :, None, :] + shift[:, :, :, None, None])
        dist_sq = jnp.sum(delta * delta, axis=0) + 0.5
        inverse = 1.0 / (dist_sq * jnp.sqrt(dist_sq))
        weight = other[3][:, :, None, :] * inverse
        force = force + jnp.sum(weight[None] * delta, axis=-1)
    return slow_coupling * own[3][None] * force


def fast_from_cells(frac, charge, picked):
    delta = frac[:, :, None] - picked[0:3]
    dist_sq = jnp.sum(delta * delta, axis=0) + 0.5
    inverse = 1.0 / (dist_sq * jnp.sqrt(dist_sq))
    weight = picked[3] * inverse
    return slow_coupling * charge[None, :] * jnp.sum(weight[None] * delta, axis=-1)


def per_device(
    fast_pos,
    fast_vel,
    fast_charge,
    fast_owner,
    exclusions,
    slow_pos,
    slow_vel,
    slow_charge,
    neighbours,
):
    row_count = lax.axis_size("row")
    col_count = lax.axis_size("col")
    row_index = lax.axis_index("row")
    col_index = lax.axis_index("col")
    flat_index = row_index * col_count + col_index
    piece = fast_pos.shape[1]
    cell_rows = slow_pos.shape[1]
    cell_cols = slow_pos.shape[2]
    total_cols = cell_cols * col_count
    coords = owner_coords(fast_owner, total_cols)
    block_width = col_count * piece
    block_start = row_index * block_width
    rows_cells = lax.dynamic_slice_in_dim(coords, block_start, block_width, 1)
    rows_charge = lax.dynamic_slice_in_dim(fast_charge, block_start, block_width, 0)
    rows_exclude = lax.dynamic_slice_in_dim(exclusions, block_start, block_width, 0)
    column_atoms = (
        (jnp.arange(row_count, dtype=jnp.int32) * col_count + col_index)[:, None] * piece
        + jnp.arange(piece, dtype=jnp.int32)[None, :]
    ).reshape(-1)
    column_cells = jnp.take(coords, column_atoms, axis=1)
    column_charge = jnp.take(fast_charge, column_atoms, axis=0)

    def fast_force(frac):
        rows_pos = lax.all_gather(frac, "col", axis=1, tiled=True)
        cols_pos = lax.all_gather(frac, "row", axis=1, tiled=True)
        partial_force = pair_fast(
            rows_pos,
            rows_cells,
            rows_charge,
            rows_exclude,
            cols_pos,
            column_cells,
            column_charge,
            column_atoms,
        )
        return lax.psum_scatter(partial_force, "col", scatter_dimension=1, tiled=True)

    grid_row = fast_owner // total_cols - row_index * cell_rows
    grid_col = fast_owner % total_cols - col_index * cell_cols
    inside = (grid_row >= 0) & (grid_row < cell_rows) & (grid_col >= 0) & (grid_col < cell_cols)
    local_cell = grid_row * cell_cols + grid_col
    cell_ids = jnp.arange(cell_rows * cell_cols, dtype=jnp.int32)
    select = jnp.where(
        inside[:, None] & (local_cell[:, None] == cell_ids[None, :]),
        jnp.float32(1.0),
        jnp.float32(0.0),
    )

    def slow_both(spos, frac):
        data = jnp.concatenate([spos, slow_charge[None]], axis=0)
        padded = with_halo(data, (("row", 1), ("col", 2)), 2)
        views = jnp.stack(
            [padded[:, o // 5 : o // 5 + cell_rows, o % 5 : o % 5 + cell_cols] for o in range(25)]
        )
        cell_force = slow_cells(data, views, neighbours)
        everyone = lax.all_gather(frac, ("row", "col"), axis=1, tiled=True)
        table = jnp.transpose(data, (1, 2, 0, 3)).reshape(cell_rows * cell_cols, 4 * CELL)
        picked = jnp.dot(
            select, table, precision=lax.Precision.HIGHEST, preferred_element_type=jnp.float32
        )
        picked = jnp.transpose(picked.reshape(FAST, 4, CELL), (1, 0, 2))
        partial_env = fast_from_cells(everyone, fast_charge, picked)
        summed = lax.psum(partial_env, ("row", "col"))
        own_env = lax.dynamic_slice_in_dim(summed, flat_index * piece, piece, 1)
        return (cell_force, own_env)

    half_outer = 0.5 * outer_dt
    inner_dt = outer_dt / INNER
    fast_acc = fast_force(fast_pos)
    slow_acc, env_acc = slow_both(slow_pos, fast_pos)
    slow_vel = slow_vel + half_outer * slow_acc
    fast_vel = fast_vel + half_outer * env_acc
    for inner_step in range(INNER):
        fast_vel = fast_vel + 0.5 * inner_dt * fast_acc
        fast_pos = fast_pos + inner_dt * fast_vel
        fast_acc = fast_force(fast_pos)
        fast_vel = fast_vel + 0.5 * inner_dt * fast_acc
    slow_pos = slow_pos + outer_dt * slow_vel
    slow_acc, env_acc = slow_both(slow_pos, fast_pos)
    slow_vel = slow_vel + half_outer * slow_acc
    fast_vel = fast_vel + half_outer * env_acc
    return (fast_pos, fast_vel, slow_pos, slow_vel)


def solution(mesh):
    return jax.shard_map(
        per_device,
        mesh=mesh,
        in_specs=(
            P(None, ("row", "col")),
            P(None, ("row", "col")),
            P(),
            P(),
            P(),
            P(None, "row", "col", None),
            P(None, "row", "col", None),
            P("row", "col", None),
            P("row", "col", None),
        ),
        out_specs=(
            P(None, ("row", "col")),
            P(None, ("row", "col")),
            P(None, "row", "col", None),
            P(None, "row", "col", None),
        ),
        check_vma=False,
    )
```

profile of v0, /device:TPU:0, one launch (start us, length us, event | category | flops | bytes accessed | tf_op | source)
XLA Modules:
  0.0 526.1 jit_solution(1581385438300912036)
XLA Ops:
  8.5 2.9 collective-permute-start.1
  11.6 9.6 %all_gather.38 = f32[3,1024]{1,0:T(4,128)S(1)} all-gather(f32[3,128]{1,0:T(4,128)} %param.9), channel_id=1, replica_groups=mesh['row'=8,'col'=4] {'row'}, dimensions={1}, use_global_device_ids=true | all-gather | bytes 13824 | tf_op jit(solution)/shard_map/all_gather | solution.py:105
  21.2 12.3 %all_gather.37 = f32[3,512]{1,0:T(4,128)S(1)} all-gather(f32[3,128]{1,0:T(4,128)} %param.9), channel_id=1, replica_groups=mesh['row'=8,'col'=4] {'col'}, dimensions={1}, use_global_device_ids=true | all-gather | bytes 7680 | tf_op jit(solution)/shard_map/all_gather | solution.py:104
  35.2 6.1 %gather_fusion = f32[1024]{0:T(1024)S(1)} fusion(f32[4096]{0:T(1024)S(1)} %copy-done.2, s32[1024]{0:T(1024)S(1)} %broadcast_clamp_fusion), kind=kCustom, calls=%fused_computation | custom fusion | bytes 12288 | tf_op jit(solution)/shard_map/jit(_take)/gather | solution.py:101
  41.3 2.8 gather_fusion.1
  51.6 65.7 %all_gather.36 = f32[3,4096]{1,0:T(4,128)S(1)} all-gather(f32[3,128]{1,0:T(4,128)S(1)} %copy-done.7), channel_id=1, replica_groups=mesh['row'=8,'col'=4] {'row','col'}, dimensions={1}, use_global_device_ids=true | all-gather | bytes 50688 | tf_op jit(solution)/shard_map/all_gather | solution.py:136
  117.3 6.8 %convolution_bitcast_fusion.1 = f32[4,4096,128]{1,2,0:T(8,128)S(1)} fusion(s32[4096]{0:T(1024)S(1)} %get-tuple-element.54, pred[4096]{0:T(1024)(128)(4,1)S(1)} %compare_and_fusion, f32[1,4,8,128]{3,2,0,1:T(8,128)S(1)} %bitcast.458, f32[3,4,8,128]{3,2,1,0:T(8,128)S(1)} %copy-done.3), kind=kOutput, calls=%fused_computation.29 | convolution fusion | flops 805715968 | bytes 8474624 | tf_op jit(solution)/shard_map/dot_general | solution.py:138
  127.0 38.7 %psum.14 = f32[3,4096]{1,0:T(4,128)S(1)} all-reduce(f32[3,4096]{1,0:T(4,128)S(1)} %broadcast_multiply_fusion.1), channel_id=1, replica_groups=mesh['row'=8,'col'=4] {'row','col'}, use_global_device_ids=true, to_apply=%region_2.3 | all-reduce | flops 12288 | bytes 98304 | tf_op jit(solution)/shard_map/psum | solution.py:143
  166.6 9.7 %all_gather.40 = f32[3,1024]{1,0:T(4,128)S(1)} all-gather(f32[3,128]{1,0:T(4,128)S(1)} %get-tuple-element.36), channel_id=1, replica_groups=mesh['row'=8,'col'=4] {'row'}, dimensions={1}, use_global_device_ids=true | all-gather | bytes 13824 | tf_op jit(solution)/shard_map/all_gather | solution.py:105
  176.3 12.4 %all_gather.39 = f32[3,512]{1,0:T(4,128)S(1)} all-gather(f32[3,128]{1,0:T(4,128)S(1)} %get-tuple-element.36), channel_id=1, replica_groups=mesh['row'=8,'col'=4] {'col'}, dimensions={1}, use_global_device_ids=true | all-gather | bytes 7680 | tf_op jit(solution)/shard_map/all_gather | solution.py:104
  194.2 17.6 %reduce-scatter.18.cloned.1.call-done = f32[128,3]{1,0:T(8,128)} async-done(((f32[512,3]{1,0:T(8,128)}), f32[128,3]{1,0:T(8,128)}) %reduce-scatter.18.cloned.1.call-update) | async-done | bytes 1552
  212.7 8.9 %all_gather.42 = f32[3,1024]{1,0:T(4,128)S(1)} all-gather(f32[3,128]{1,0:T(4,128)S(1)} %multiply_add_fusion.7), channel_id=1, replica_groups=mesh['row'=8,'col'=4] {'row'}, dimensions={1}, use_global_device_ids=true | all-gather | bytes 13824 | tf_op jit(solution)/shard_map/all_gather | solution.py:105
  221.6 11.9 %all_gather.41 = f32[3,512]{1,0:T(4,128)S(1)} all-gather(f32[3,128]{1,0:T(4,128)S(1)} %multiply_add_fusion.7), channel_id=1, replica_groups=mesh['row'=8,'col'=4] {'col'}, dimensions={1}, use_global_device_ids=true | all-gather | bytes 7680 | tf_op jit(solution)/shard_map/all_gather | solution.py:104
  239.0 3.8 collective-permute-start.3
  242.8 13.8 %reduce-scatter.20.cloned.1.call-done = f32[128,3]{1,0:T(8,128)} async-done(((f32[512,3]{1,0:T(8,128)}), f32[128,3]{1,0:T(8,128)}) %reduce-scatter.20.cloned.1.call-update) | async-done | bytes 1552
  257.5 8.9 %all_gather.44 = f32[3,1024]{1,0:T(4,128)S(1)} all-gather(f32[3,128]{1,0:T(4,128)S(1)} %get-tuple-element.34), channel_id=1, replica_groups=mesh['row'=8,'col'=4] {'row'}, dimensions={1}, use_global_device_ids=true | all-gather | bytes 13824 | tf_op jit(solution)/shard_map/all_gather | solution.py:105
  266.4 11.9 %all_gather.43 = f32[3,512]{1,0:T(4,128)S(1)} all-gather(f32[3,128]{1,0:T(4,128)S(1)} %get-tuple-element.34), channel_id=1, replica_groups=mesh['row'=8,'col'=4] {'col'}, dimensions={1}, use_global_device_ids=true | all-gather | bytes 7680 | tf_op jit(solution)/shard_map/all_gather | solution.py:104
  283.6 17.7 %reduce-scatter.22.cloned.1.call-done = f32[128,3]{1,0:T(8,128)} async-done(((f32[512,3]{1,0:T(8,128)}), f32[128,3]{1,0:T(8,128)}) %reduce-scatter.22.cloned.1.call-update) | async-done | bytes 1552
  302.3 8.9 %all_gather.46 = f32[3,1024]{1,0:T(4,128)S(1)} all-gather(f32[3,128]{1,0:T(4,128)S(1)} %multiply_add_fusion.5), channel_id=1, replica_groups=mesh['row'=8,'col'=4] {'row'}, dimensions={1}, use_global_device_ids=true | all-gather | bytes 13824 | tf_op jit(solution)/shard_map/all_gather | solution.py:105
  311.2 12.1 %all_gather.45 = f32[3,512]{1,0:T(4,128)S(1)} all-gather(f32[3,128]{1,0:T(4,128)S(1)} %multiply_add_fusion.5), channel_id=1, replica_groups=mesh['row'=8,'col'=4] {'col'}, dimensions={1}, use_global_device_ids=true | all-gather | bytes 7680 | tf_op jit(solution)/shard_map/all_gather | solution.py:104
  328.5 63.9 %all_gather.47 = f32[3,4096]{1,0:T(4,128)S(1)} all-gather(f32[3,128]{1,0:T(4,128)S(1)} %multiply_add_fusion.5), channel_id=1, replica_groups=mesh['row'=8,'col'=4] {'row','col'}, dimensions={1}, use_global_device_ids=true | all-gather | bytes 50688 | tf_op jit(solution)/shard_map/all_gather | solution.py:136
  403.6 2.5 fusion.2
  407.7 7.2 %fusion.3 = (f32[3,4,8,128]{3,2,1,0:T(8,128)S(1)}, f32[4,8,128,128]{3,2,1,0:T(8,128)S(1)}, f32[4,8,128,128]{3,2,1,0:T(8,128)S(1)}, f32[4,8,128,128]{3,2,1,0:T(8,128)S(1)}, f32[3,4,8,128]{3,2,1,0:T(8,128)S(1)}) fusion(f32[4,8,128,128]{3,2,1,0:T(8,128)S(1)} %fusion.51, f32[3,4,8,128]{3,2,1,0:T(8,128)S(1)} %slice_add_fusion.8, ...), kind=kLoop, calls=%fused_computation.33 | loop fusion | flops 21995520 | bytes 10878976 | tf_op jit(solution)/shard_map/reduce_sum | solution.py:58
  417.2 8.5 %fusion.5 = (f32[3,4,8,128]{3,2,1,0:T(8,128)S(1)}, f32[3,4,8,128]{3,2,1,0:T(8,128)S(1)}, f32[3,4,8,128]{3,2,1,0:T(8,128)S(1)}) fusion(f32[4,8,128,128]{3,2,1,0:T(8,128)S(1)} %fusion.53, f32[3,4,8,128]{3,2,1,0:T(8,128)S(1)} %slice_add_fusion.7, f32[3,4,8,128]{3,2,1,0:T(8,128)S(1)} %copy-done.3, f32[3,4,8,128]{3,2,1,0:T(8,128)S(1)} %slice_add_fusion.5, ...), kind=kLoop, calls=%fused_computation.35 | loop fusion | flops 14118912 | bytes 6635520 | tf_op jit(solution)/shard_map/reduce_sum | solution.py:58
  425.8 6.8 %convolution_bitcast_fusion = f32[4,4096,128]{1,2,0:T(8,128)S(1)} fusion(s32[4096]{0:T(1024)S(1)} %get-tuple-element.54, pred[4096]{0:T(1024)(128)(4,1)S(1)} %compare_and_fusion, f32[1,4,8,128]{3,2,1,0:T(8,128)S(1)} %bitcast.464, f32[3,4,8,128]{3,2,1,0:T(8,128)S(1)} %get-tuple-element.32), kind=kOutput, calls=%fused_computation.28 | convolution fusion | flops 805715968 | bytes 8474624 | tf_op jit(solution)/shard_map/dot_general | solution.py:138
  432.7 2.6 collective-permute-start.5
  438.0 40.2 %psum.15 = f32[3,4096]{1,0:T(4,128)S(1)} all-reduce(f32[3,4096]{1,0:T(4,128)S(1)} %broadcast_multiply_fusion), channel_id=1, replica_groups=mesh['row'=8,'col'=4] {'row','col'}, use_global_device_ids=true, to_apply=%region_31.32 | all-reduce | flops 12288 | bytes 98304 | tf_op jit(solution)/shard_map/psum | solution.py:143
  478.9 4.0 collective-permute-start.7
  485.1 2.3 fusion.28
  497.0 2.5 fusion.12
  501.1 7.2 %fusion.13 = (f32[3,4,8,128]{3,2,1,0:T(8,128)S(1)}, f32[4,8,128,128]{3,2,1,0:T(8,128)S(1)}, f32[4,8,128,128]{3,2,1,0:T(8,128)S(1)}, f32[4,8,128,128]{3,2,1,0:T(8,128)S(1)}, f32[3,4,8,128]{3,2,1,0:T(8,128)S(1)}) fusion(f32[4,8,128,128]{3,2,1,0:T(8,128)S(1)} %fusion.64, f32[3,4,8,128]{3,2,1,0:T(8,128)S(1)} %slice_add_fusion.3, ...), kind=kLoop, calls=%fused_computation.43 | loop fusion | flops 21995520 | bytes 10878976 | tf_op jit(solution)/shard_map/reduce_sum | solution.py:58
  510.6 8.1 %fusion.15 = (f32[3,4,8,128]{3,2,1,0:T(8,128)S(1)}, f32[3,4,8,128]{3,2,1,0:T(8,128)S(1)}, f32[3,4,8,128]{3,2,1,0:T(8,128)S(1)}) fusion(f32[4,8,128,128]{3,2,1,0:T(8,128)S(1)} %fusion.66, f32[3,4,8,128]{3,2,1,0:T(8,128)S(1)} %slice_add_fusion.2, f32[3,4,8,128]{3,2,1,0:T(8,128)S(1)} %get-tuple-element.32, f32[3,4,8,128]{3,2,1,0:T(8,128)S(1)} %slice_add_fusion, ...), kind=kLoop, calls=%fused_computation.45 | loop fusion | flops 14118912 | bytes 6635520 | tf_op jit(solution)/shard_map/reduce_sum | solution.py:58
  (220 shorter events, 72.5 us)
Async XLA Ops:
  7.2 37.4 %copy-start = (s32[4096,4]{0,1:T(4,128)S(1)}, s32[4096,4]{0,1:T(4,128)}, u32[]{:S(2)}) copy-start(s32[4096,4]{0,1:T(4,128)} %param.13) | copy-start | bytes 196612
  7.2 27.9 %copy-start.2 = (f32[4096]{0:T(1024)S(1)}, f32[4096]{0:T(1024)}, u32[]{:S(2)}) copy-start(f32[4096]{0:T(1024)} %param.11) | copy-start | bytes 49156
  7.2 158.5 %reduce-scatter.16.cloned.1.call-start = ((), (), s32[]{:S(2)}) async-start(), calls=%async_computation.5 | async-start | bytes 327680
  8.0 230.8 %collective-permute-start = (f32[4,2,8,128]{3,2,0,1:T(8,128)S(1)}, f32[4,2,8,128]{3,2,0,1:T(8,128)S(1)}, u32[]{:S(2)}, u32[]{:S(2)}) collective-permute-start(f32[4,2,8,128]{3,2,0,1:T(8,128)S(1)} %get-tuple-element.52), channel_id=1, source_target_pairs={{0,4},{4,8},{8,12},{12,16},{16,20},{20,24},{24,28},{28,0},{1,5},{5... | collective-permute-start | bytes 98312 | tf_op jit(solution)/shard_map/ppermute | solution.py:23
  8.5 230.3 %collective-permute-start.1 = (f32[4,2,8,128]{3,2,0,1:T(8,128)S(1)}, f32[4,2,8,128]{3,2,0,1:T(8,128)S(1)}, u32[]{:S(2)}, u32[]{:S(2)}) collective-permute-start(f32[4,2,8,128]{3,2,0,1:T(8,128)S(1)} %get-tuple-element.53), channel_id=1, source_target_pairs={{4,0},{8,4},{12,8},{16,12},{20,16},{24,20},{28,24},{0,28},{5,1},{9... | collective-permute-start | bytes 98312 | tf_op jit(solution)/shard_map/ppermute | solution.py:24
  49.0 2.5 copy-start.9
  49.0 2.5 copy-start.5
  49.0 2.6 copy-start.6
  49.0 2.6 copy-start.7
  49.0 68.3 %copy-start.3 = (f32[3,4,8,128]{3,2,1,0:T(8,128)S(1)}, f32[3,4,8,128]{3,2,1,0:T(8,128)}, u32[]{:S(2)}) copy-start(f32[3,4,8,128]{3,2,1,0:T(8,128)} %param.14) | copy-start | bytes 147460
  51.4 160.4 %reduce-scatter.18.cloned.1.call-start = ((), (), s32[]{:S(2)}) async-start(), calls=%async_computation.6 | async-start | bytes 327680
  125.7 40.9 %copy-start.11 = (f32[3,128]{1,0:T(4,128)S(1)}, f32[3,128]{1,0:T(4,128)}, u32[]{:S(2)}) copy-start(f32[3,128]{1,0:T(4,128)} %param.10) | copy-start | bytes 4612
  194.0 62.5 %reduce-scatter.20.cloned.1.call-start = ((), (), s32[]{:S(2)}) async-start(), calls=%async_computation.7 | async-start | bytes 327680
  238.8 62.5 %reduce-scatter.22.cloned.1.call-start = ((), (), s32[]{:S(2)}) async-start(), calls=%async_computation.8 | async-start | bytes 327680
  238.9 154.5 %collective-permute-start.2 = (f32[4,8,2,128]{3,2,0,1:T(2,128)S(1)}, f32[4,8,2,128]{3,2,0,1:T(2,128)S(1)}, u32[]{:S(2)}, u32[]{:S(2)}) collective-permute-start(f32[4,8,2,128]{3,2,0,1:T(2,128)S(1)} %get-tuple-element.45), channel_id=1, source_target_pairs={{0,1},{1,2},{2,3},{3,0},{4,5},{5,6},{6,7},{7,4},{8,9},{9,10},{10,1... | collective-permute-start | bytes 98312 | tf_op jit(solution)/shard_map/ppermute | solution.py:23
  239.0 154.4 %collective-permute-start.3 = (f32[4,8,2,128]{3,2,0,1:T(2,128)S(1)}, f32[4,8,2,128]{3,2,0,1:T(2,128)S(1)}, u32[]{:S(2)}, u32[]{:S(2)}) collective-permute-start(f32[4,8,2,128]{3,2,0,1:T(2,128)S(1)} %get-tuple-element.44), channel_id=1, source_target_pairs={{1,0},{2,1},{3,2},{0,3},{5,4},{6,5},{7,6},{4,7},{9,8},{10,9},{11,1... | collective-permute-start | bytes 98312 | tf_op jit(solution)/shard_map/ppermute | solution.py:24
  283.6 108.9 %reduce-scatter.24.cloned.1.call-start = ((), (), s32[]{:S(2)}) async-start(), calls=%async_computation.9 | async-start | bytes 327680
  302.2 26.3 %copy-start.10 = (f32[3,128]{1,0:T(4,128)}, f32[3,128]{1,0:T(4,128)S(1)}, u32[]{:S(2)}) copy-start(f32[3,128]{1,0:T(4,128)S(1)} %multiply_add_fusion.5) | copy-start | bytes 4612
  417.2 8.5 %copy-start.8 = (f32[3,4,8,128]{3,2,1,0:T(8,128)S(1)}, f32[3,4,8,128]{3,2,1,0:T(8,128)}, u32[]{:S(2)}) copy-start(f32[3,4,8,128]{3,2,1,0:T(8,128)} %param.15) | copy-start | bytes 147460
  425.8 84.9 %copy-start.4 = (f32[3,4,8,128]{3,2,1,0:T(8,128)}, f32[3,4,8,128]{3,2,1,0:T(8,128)S(1)}, u32[]{:S(2)}) copy-start(f32[3,4,8,128]{3,2,1,0:T(8,128)S(1)} %get-tuple-element.32) | copy-start | bytes 147460
  432.6 46.2 %collective-permute-start.4 = (f32[4,2,8,128]{3,2,1,0:T(8,128)S(1)}, f32[4,2,8,128]{3,2,1,0:T(8,128)S(1)}, u32[]{:S(2)}, u32[]{:S(2)}) collective-permute-start(f32[4,2,8,128]{3,2,1,0:T(8,128)S(1)} %get-tuple-element.48), channel_id=1, source_target_pairs={{0,4},{4,8},{8,12},{12,16},{16,20},{20,24},{24,28},{28,0},{1,5},{5... | collective-permute-start | bytes 98312 | tf_op jit(solution)/shard_map/ppermute | solution.py:23
  432.7 46.2 %collective-permute-start.5 = (f32[4,2,8,128]{3,2,1,0:T(8,128)S(1)}, f32[4,2,8,128]{3,2,1,0:T(8,128)S(1)}, u32[]{:S(2)}, u32[]{:S(2)}) collective-permute-start(f32[4,2,8,128]{3,2,1,0:T(8,128)S(1)} %get-tuple-element.49), channel_id=1, source_target_pairs={{4,0},{8,4},{12,8},{16,12},{20,16},{24,20},{28,24},{0,28},{5,1},{9... | collective-permute-start | bytes 98312 | tf_op jit(solution)/shard_map/ppermute | solution.py:24
  478.9 5.8 %collective-permute-start.6 = (f32[4,8,2,128]{3,2,1,0:T(2,128)S(1)}, f32[4,8,2,128]{3,2,1,0:T(2,128)S(1)}, u32[]{:S(2)}, u32[]{:S(2)}) collective-permute-start(f32[4,8,2,128]{3,2,1,0:T(2,128)S(1)} %get-tuple-element.41), channel_id=1, source_target_pairs={{0,1},{1,2},{2,3},{3,0},{4,5},{5,6},{6,7},{7,4},{8,9},{9,10},{10,1... | collective-permute-start | bytes 98312 | tf_op jit(solution)/shard_map/ppermute | solution.py:23
  478.9 5.7 %collective-permute-start.7 = (f32[4,8,2,128]{3,2,1,0:T(2,128)S(1)}, f32[4,8,2,128]{3,2,1,0:T(2,128)S(1)}, u32[]{:S(2)}, u32[]{:S(2)}) collective-permute-start(f32[4,8,2,128]{3,2,1,0:T(2,128)S(1)} %get-tuple-element.40), channel_id=1, source_target_pairs={{1,0},{2,1},{3,2},{0,3},{5,4},{6,5},{7,6},{4,7},{9,8},{10,9},{11,1... | collective-permute-start | bytes 98312 | tf_op jit(solution)/shard_map/ppermute | solution.py:24
  509.9 9.5 %copy-start.1 = (s32[4096,4]{0,1:T(4,128)S(1)}, s32[4096,4]{0,1:T(4,128)}, u32[]{:S(2)}) copy-start(s32[4096,4]{0,1:T(4,128)} %param.13) | copy-start | bytes 196612
Sparse Core Ops, SparseCore 0:
  51.5 18.8 reduce-scatter.15
  194.2 17.5 reduce-scatter.17
  238.9 17.5 reduce-scatter.19
  283.7 17.5 reduce-scatter.21
  328.6 17.6 reduce-scatter.23
where the time goes:
time: 531 us; the launch traced here: 526 us
  blocking collectives  315 us (59%)
  other arithmetic  77.1 us (15%)
  waiting for transfers between devices  51 us (10%)
  matrix products  34.2 us (6%)
  local copies, waits for them, and re-layouts  19.3 us (4%)
  between operations  15.2 us (3%)
  starting transfers between devices  14.2 us (3%)
    all_gather x2, blocking collectives, slow_both(): everyone = lax.all_gather(frac, ('row', 'col'), axis=1, tiled=True)  130 us
    psum x2, blocking collectives, slow_both(): summed = lax.psum(partial_env, ('row', 'col'))  78.9 us
    all_gather x5, blocking collectives, fast_force(): rows_pos = lax.all_gather(frac, 'col', axis=1, tiled=True)  60.7 us
    unnamed x10, waiting for transfers between devices  49.2 us
    all_gather x5, blocking collectives, fast_force(): cols_pos = lax.all_gather(frac, 'row', axis=1, tiled=True)  46 us
    reduce_sum x4, other arithmetic, slow_cells(): force = force + jnp.sum(weight[None] * delta, axis=-1)  30.9 us
    dot_general x10, matrix products, slow_cells(): jnp.einsum('abo,oxabn->xabn', pick, views, precision=lax.Precision.HIGHEST)  20.6 us
    dot_general x2, matrix products, slow_both(): jnp.dot(select, table, precision=lax.Precision.HIGHEST, preferred_element...  13.6 us
  transfers between devices with their start and end apart: 13, of which 4 were waited for; matrix products, arithmetic and copies ran while one was open for 11% of the time, Pallas kernels for 0%

commit v1 on v0

--- a/solution.py
+++ b/solution.py
@@ -1,16 +1,375 @@
+import functools
+
 import jax
 import jax.numpy as jnp
 from jax import lax
+from jax.experimental import pallas as pl
+from jax.experimental.pallas import tpu as pltpu
 from jax.sharding import PartitionSpec as P
 
-FAST = 4096
 CELL = 128
 INNER = 4
-
+GROUPS = 256
 
 fast_coupling = 1.0
 slow_coupling = 0.1
 outer_dt = 0.2
+half_outer = 0.5 * outer_dt
+inner_dt = outer_dt / INNER
+
+BOTH = ("row", "col")
+F32 = jnp.float32
+BF16 = jnp.bfloat16
+LANES = 128
+ENV_UNROLL = 4
+VMEM = pl.BlockSpec(memory_space=pltpu.VMEM)
+SMEM = pl.BlockSpec(memory_space=pltpu.SMEM)
+
+
+def sds(shape, dtype=F32):
+    return jax.ShapeDtypeStruct(shape, dtype)
+
+
+def fast_rows(g_ref, cor_ref, q_ref, exm_ref, own, planes, cols, sums):
+    count = g_ref.shape[0]
+    members = exm_ref.shape[0]
+    for c in range(3):
+        x = g_ref[:, c, :]
+        planes[c] = x + cor_ref[c] if c < 2 else x
+    own_rows = [planes[c, pl.ds(own, 1), :] for c in range(3)]
+    for c in range(3):
+        cols[c] = jnp.transpose(jnp.broadcast_to(own_rows[c], (LANES, LANES)))
+    unroll = 2
+
+    def body(i, carry):
+        at = [pl.ds(pl.multiple_of((i * unroll + u) * 8, 8), 8) for u in range(unroll)]
+        a = [[cols[c, at[u], :] for c in range(3)] for u in range(unroll)]
+        acc = [[jnp.zeros((8, LANES), F32) for _ in range(3)] for _ in range(unroll)]
+        for b in range(count):
+            y = [jnp.broadcast_to(planes[c, b : b + 1, :], (8, LANES)) for c in range(3)]
+            qb = jnp.broadcast_to(q_ref[b : b + 1, :], (8, LANES))
+            for u in range(unroll):
+                d = [a[u][c] - y[c] for c in range(3)]
+                r = lax.rsqrt(d[0] * d[0] + d[1] * d[1] + d[2] * d[2] + 1.0)
+                w = (qb * r) * (r * r)
+                for c in range(3):
+                    acc[u][c] = acc[u][c] + w * d[c]
+        for u in range(unroll):
+            for c in range(3):
+                sums[c, at[u], :] = acc[u][c]
+        return carry
+
+    lax.fori_loop(0, LANES // (8 * unroll), body, 0)
+    step = GROUPS // LANES
+    part = pl.ds(lax.rem(own, step), members, stride=step)
+    d = [own_rows[c] - planes[c, part, :] for c in range(3)]
+    r = lax.rsqrt(d[0] * d[0] + d[1] * d[1] + d[2] * d[2] + 1.0)
+    w = (exm_ref[...] * q_ref[part, :]) * (r * (r * r))
+    ones = jnp.ones((8, LANES), F32)
+    scale = fast_coupling * q_ref[pl.ds(own, 1), :]
+    out = []
+    for c in range(3):
+        total = lax.dot_general(
+            ones, sums[c], (((1,), (1,)), ((), ())),
+            precision=lax.Precision.HIGHEST, preferred_element_type=F32,
+        )[0:1, :]
+        out.append(scale * (total - jnp.sum(w * d[c], axis=0, keepdims=True)))
+    return out
+
+
+def fast_only_kernel(own_ref, g_ref, cor_ref, q_ref, exm_ref, f_ref, planes, cols, sums):
+    rows = fast_rows(g_ref, cor_ref, q_ref, exm_ref, own_ref[0], planes, cols, sums)
+    for c in range(3):
+        f_ref[c : c + 1, :] = rows[c]
+
+
+def fast_step_kernel(
+    own_ref, g_ref, cor_ref, q_ref, exm_ref, v_ref, send_ref, p_out, v_out, planes, cols, sums
+):
+    own = own_ref[0]
+    rows = fast_rows(g_ref, cor_ref, q_ref, exm_ref, own, planes, cols, sums)
+    count = send_ref.shape[0]
+    for c in range(3):
+        v = v_ref[c : c + 1, :] + inner_dt * rows[c]
+        p = g_ref[pl.ds(own, 1), c, :] + inner_dt * v
+        v_out[c : c + 1, :] = v
+        p_out[c : c + 1, :] = p
+        send_ref[:, c, :] = jnp.broadcast_to(p, (count, LANES))
+
+
+def fast_cost(count):
+    pairs = count * LANES * LANES
+    return pl.CostEstimate(flops=19 * pairs, transcendentals=pairs, bytes_accessed=count * 4096)
+
+
+def fast_scratch(count):
+    return [
+        pltpu.VMEM((3, count, LANES), F32),
+        pltpu.VMEM((3, LANES, LANES), F32),
+        pltpu.VMEM((3, LANES, LANES), F32),
+    ]
+
+
+def fast_only(own, g, cor, q, exm):
+    count = g.shape[0]
+    return pl.pallas_call(
+        fast_only_kernel,
+        out_shape=sds((3, LANES)),
+        in_specs=[SMEM] + [VMEM] * 4,
+        out_specs=VMEM,
+        scratch_shapes=fast_scratch(count),
+        cost_estimate=fast_cost(count),
+        name="fast_only",
+        compiler_params=pltpu.CompilerParams(vmem_limit_bytes=2 << 20),
+    )(own, g, cor, q, exm)
+
+
+def fast_step(own, g, cor, q, exm, v):
+    count = g.shape[0]
+    return pl.pallas_call(
+        fast_step_kernel,
+        out_shape=(sds((count, 3, LANES)), sds((3, LANES)), sds((3, LANES))),
+        in_specs=[SMEM] + [VMEM] * 5,
+        out_specs=(VMEM,) * 3,
+        scratch_shapes=fast_scratch(count),
+        cost_estimate=fast_cost(count),
+        name="fast_step",
+        compiler_params=pltpu.CompilerParams(vmem_limit_bytes=2 << 20),
+    )(own, g, cor, q, exm, v)
+
+
+def list_kernel(total_cols, cell_rows, cell_cols, owner_ref, base_ref, list_ref, count_ref):
+    row0, col0 = base_ref[0], base_ref[1]
+    step = GROUPS // LANES
+
+    def body(i, n):
+        cell = owner_ref[i]
+        r = lax.div(cell, total_cols) - row0
+        c = lax.rem(cell, total_cols) - col0
+        inside = (r >= 0) & (r < cell_rows) & (c >= 0) & (c < cell_cols)
+        list_ref[0, n] = lax.div(i, LANES)
+        list_ref[1, n] = lax.rem(i, LANES)
+        list_ref[2, n] = r * cell_cols + c
+        return n + inside.astype(jnp.int32)
+
+    n = lax.fori_loop(0, GROUPS, body, jnp.int32(0))
+    count_ref[0] = n
+    for k in range(ENV_UNROLL):
+        list_ref[0, n + k] = 0
+        list_ref[1, n + k] = -1
+        list_ref[2, n + k] = 0
+
+
+def env_list(owner, base, total_cols, cell_rows, cell_cols):
+    return pl.pallas_call(
+        functools.partial(list_kernel, total_cols, cell_rows, cell_cols),
+        out_shape=(sds((3, GROUPS + ENV_UNROLL), jnp.int32), sds((1,), jnp.int32)),
+        in_specs=[SMEM, SMEM],
+        out_specs=(SMEM, SMEM),
+        name="env_list",
+        compiler_params=pltpu.CompilerParams(vmem_limit_bytes=2 << 20),
+    )(owner, base)
+
+
+def env_kernel(list_ref, count_ref, g_ref, cells_ref, out_ref, planes, sums):
+    step = GROUPS // LANES
+    members = g_ref.shape[0] // step
+    for c in range(3):
+        for h in range(step):
+            planes[c, h] = g_ref[pl.ds(h, members, stride=step), c, :]
+    sums[...] = jnp.zeros_like(sums)
+    lane = lax.broadcasted_iota(jnp.int32, (members, LANES), 1)
+
+    def body(t, carry):
+        for u in range(ENV_UNROLL):
+            n = t * ENV_UNROLL + u
+            h = list_ref[0, n]
+            here = lane == list_ref[1, n]
+            cell = cells_ref[list_ref[2, n]]
+            d = []
+            for c in range(3):
+                x = jnp.sum(jnp.where(here, planes[c, h], 0.0), axis=1, keepdims=True)
+                d.append(x - cell[c : c + 1, :])
+            r = lax.rsqrt(d[0] * d[0] + d[1] * d[1] + d[2] * d[2] + 0.5)
+            w = (cell[3:4, :] * r) * (r * r)
+            for c in range(3):
+                f = jnp.sum(w * d[c], axis=1, keepdims=True)
+                sums[c, h] = sums[c, h] + jnp.where(here, f, 0.0)
+        return carry
+
+    lax.fori_loop(0, lax.div(count_ref[0] + (ENV_UNROLL - 1), ENV_UNROLL), body, 0)
+    for c in range(3):
+        for h in range(step):
+            out_ref[pl.ds(h, members, stride=step), c, :] = sums[c, h]
+
+
+def env(lists, g, cells):
+    count = g.shape[0]
+    step = GROUPS // LANES
+    members = count // step
+    return pl.pallas_call(
+        env_kernel,
+        out_shape=sds((count, 3, LANES)),
+        in_specs=[SMEM, SMEM, VMEM, VMEM],
+        out_specs=VMEM,
+        scratch_shapes=[
+            pltpu.VMEM((3, step, members, LANES), F32),
+            pltpu.VMEM((3, step, members, LANES), F32),
+        ],
+        cost_estimate=pl.CostEstimate(flops=2_000_000, transcendentals=60000, bytes_accessed=200000),
+        name="env",
+        compiler_params=pltpu.CompilerParams(vmem_limit_bytes=2 << 20),
+    )(*lists, g, cells)
+
+
+def kick_kernel(own_ref, e_ref, f_ref, q_ref, p_ref, v_ref, send_ref, p_out, v_out):
+    scale = slow_coupling * q_ref[pl.ds(own_ref[0], 1), :]
+    count = send_ref.shape[0]
+    for c in range(3):
+        e = scale * jnp.sum(e_ref[:, c, :], axis=0, keepdims=True)
+        v = v_ref[c : c + 1, :] + half_outer * e + 0.5 * inner_dt * f_ref[c : c + 1, :]
+        p = p_ref[c : c + 1, :] + inner_dt * v
+        v_out[c : c + 1, :] = v
+        p_out[c : c + 1, :] = p
+        send_ref[:, c, :] = jnp.broadcast_to(p, (count, LANES))
+
+
+def kick(own, e, f, q, p, v):
+    count = e.shape[0]
+    return pl.pallas_call(
+        kick_kernel,
+        out_shape=(sds((count, 3, LANES)), sds((3, LANES)), sds((3, LANES))),
+        in_specs=[SMEM] + [VMEM] * 5,
+        out_specs=(VMEM,) * 3,
+        name="kick",
+        compiler_params=pltpu.CompilerParams(vmem_limit_bytes=2 << 20),
+    )(own, e, f, q, p, v)
+
+
+def last_kick_kernel(own_ref, e_ref, f_ref, q_ref, v_ref, v_out):
+    scale = slow_coupling * q_ref[pl.ds(own_ref[0], 1), :]
+    for c in range(3):
+        e = scale * jnp.sum(e_ref[:, c, :], axis=0, keepdims=True)
+        v_out[c : c + 1, :] = (
+            v_ref[c : c + 1, :] + 0.5 * inner_dt * f_ref[c : c + 1, :] + half_outer * e
+        )
+
+
+def last_kick(own, e, f, q, v):
+    return pl.pallas_call(
+        last_kick_kernel,
+        out_shape=sds((3, LANES)),
+        in_specs=[SMEM] + [VMEM] * 4,
+        out_specs=VMEM,
+        name="last_kick",
+        compiler_params=pltpu.CompilerParams(vmem_limit_bytes=2 << 20),
+    )(own, e, f, q, v)
+
+
+def split3(x):
+    hi = x.astype(BF16).astype(F32)
+    rest = x - hi
+    mid = rest.astype(BF16).astype(F32)
+    return hi, mid, rest - mid
+
+
+def slow_kernel(first, nb_ref, tab_ref, vel_ref, *refs):
+    if first:
+        vel_out, pos_out, cell_out, feat, vals = refs
+    else:
+        vel_out, feat, vals = refs
+    all_rows, all_cols = tab_ref.shape[0], tab_ref.shape[1]
+    cell_rows, cell_cols = vel_ref.shape[1], vel_ref.shape[2]
+    slots = nb_ref.shape[1]
+    row8 = lax.broadcasted_iota(jnp.int32, (8, LANES), 0)
+
+    def load8(r, c):
+        t = tab_ref[r, c]
+        return jnp.concatenate([t, jnp.zeros_like(t)], axis=0)
+
+    def one_cell(n):
+        t = load8(lax.div(n, all_cols), lax.rem(n, all_cols))
+        pos = jnp.where(row8 < 3, t, 0.0)
+        norm = jnp.sum(pos * pos, axis=0, keepdims=True) + 0.5
+        b = jnp.where(row8 == 3, 1.0, jnp.where(row8 == 4, norm, -2.0 * pos))
+        hi, mid, lo = split3(b)
+        wide = jnp.concatenate([hi, mid, hi, lo, mid, hi], axis=0)
+        feat[n] = jnp.transpose(wide).astype(BF16)
+        charge = t[3:4, :]
+        u = jnp.where(row8 == 3, charge, pos * charge)
+        hi = u.astype(BF16).astype(F32)
+        vals[n] = jnp.concatenate([hi, u - hi], axis=0).astype(BF16)
+
+    def prepare(i, carry):
+        for u in range(4):
+            one_cell(i * 4 + u)
+        return carry
+
+    lax.fori_loop(0, all_rows * all_cols // 4, prepare, 0)
+
+    def body(n, carry):
+        r = lax.div(n, cell_cols)
+        c = lax.rem(n, cell_cols)
+        t = load8(r + 2, c + 2)
+        pos = jnp.where(row8 < 3, t, 0.0)
+        force = jnp.zeros((8, LANES), F32)
+        for k in range(slots):
+            o = nb_ref[n, k]
+            dr = lax.div(o, 5)
+            dc = lax.rem(o, 5)
+            shift = jnp.where(
+                row8 == 0, (dr - 2).astype(F32), jnp.where(row8 == 1, (dc - 2).astype(F32), 0.0)
+            )
+            x = pos - shift
+            norm = jnp.sum(x * x, axis=0, keepdims=True)
+            a = jnp.where(row8 == 3, norm, jnp.where(row8 == 4, 1.0, x))
+            hi, mid, lo = split3(a)
+            wide = jnp.concatenate([hi, hi, mid, hi, mid, lo], axis=0).astype(BF16)
+            other = (r + dr) * all_cols + c + dc
+            s = jnp.dot(feat[other], wide, preferred_element_type=F32)
+            inv = lax.rsqrt(s)
+            w = inv * (inv * inv)
+            whi = w.astype(BF16)
+            wlo = (w - whi.astype(F32)).astype(BF16)
+            g = vals[other]
+            both = jnp.dot(g, whi, preferred_element_type=F32) + jnp.dot(
+                g, wlo, preferred_element_type=F32
+            )
+            total = both[0:8] + both[8:16]
+            force = force + (x * total[3:4, :] - total)
+        force = slow_coupling * t[3:4, :] * force
+        for x in range(3):
+            here = (x, r, pl.ds(c, 1), slice(None))
+            v = vel_ref[here] + half_outer * force[x : x + 1]
+            vel_out[here] = v
+            if first:
+                p = t[x : x + 1] + outer_dt * v
+                pos_out[here] = p
+                cell_out[n, x : x + 1, :] = p
+        if first:
+            cell_out[n, 3:4, :] = t[3:4]
+        return carry
+
+    lax.fori_loop(0, cell_rows * cell_cols, body, 0)
+
+
+def slow(first, nb, tab, vel):
+    cells = tab.shape[0] * tab.shape[1]
+    own = vel.shape[1] * vel.shape[2]
+    out = (sds(vel.shape), sds(vel.shape), sds((own, 4, CELL))) if first else sds(vel.shape)
+    pairs = own * nb.shape[1] * CELL * CELL
+    return pl.pallas_call(
+        functools.partial(slow_kernel, first),
+        out_shape=out,
+        in_specs=[SMEM, VMEM, VMEM],
+        out_specs=(VMEM,) * 3 if first else VMEM,
+        scratch_shapes=[pltpu.VMEM((cells, CELL, 48), BF16), pltpu.VMEM((cells, 16, CELL), BF16)],
+        cost_estimate=pl.CostEstimate(
+            flops=19 * pairs, transcendentals=pairs, bytes_accessed=1_000_000
+        ),
+        name="slow",
+        compiler_params=pltpu.CompilerParams(vmem_limit_bytes=8 << 20),
+    )(nb, tab, vel)
 
 
 def with_halo(x, sides, width):
@@ -24,6 +383,61 @@
         after = lax.ppermute(initial, axis, down)
         x = jnp.concatenate([before, x, after], axis=dim)
     return x
+
+
+def exchange(x):
+    return lax.all_to_all(x, BOTH, 0, 0)
+
+
+def per_device(
+    fast_pos, fast_vel, fast_charge, fast_owner, exclusions,
+    slow_pos, slow_vel, slow_charge, neighbours,
+):
+    if fast_pos.shape[1] != LANES:
+        return general(
+            fast_pos, fast_vel, fast_charge, fast_owner, exclusions,
+            slow_pos, slow_vel, slow_charge, neighbours,
+        )
+    row_count, col_count = lax.axis_size("row"), lax.axis_size("col")
+    row_index, col_index = lax.axis_index("row"), lax.axis_index("col")
+    flat = row_index * col_count + col_index
+    count = row_count * col_count
+    piece = fast_pos.shape[1]
+    cell_rows, cell_cols = slow_pos.shape[1], slow_pos.shape[2]
+    total_cols = cell_cols * col_count
+    own = jnp.reshape(flat, (1,)).astype(jnp.int32)
+
+    g = exchange(jnp.broadcast_to(fast_pos[None], (count, 3, piece)))
+
+    owner = fast_owner.reshape(count, piece)
+    cor = jnp.stack([owner // total_cols, owner % total_cols]).astype(F32)
+    q = fast_charge.reshape(count, piece)
+    members = fast_charge.shape[0] // GROUPS
+    ex = lax.dynamic_slice_in_dim(exclusions, flat * piece, piece, 0) // GROUPS
+    exm = jnp.any(
+        ex[None] == jnp.arange(members, dtype=jnp.int32)[:, None, None], axis=2
+    ).astype(F32)
+    base = jnp.stack([row_index * cell_rows, col_index * cell_cols]).astype(jnp.int32)
+    lists = env_list(fast_owner[:GROUPS], base, total_cols, cell_rows, cell_cols)
+
+    cells = jnp.concatenate([slow_pos, slow_charge[None]], axis=0).transpose(1, 2, 0, 3)
+    sides = (("row", 0), ("col", 1))
+    nb = neighbours.reshape(cell_rows * cell_cols, -1)
+    slow_vel, slow_pos, cells2 = slow(True, nb, with_halo(cells, sides, 2), slow_vel)
+    tab2 = with_halo(cells2.reshape(cells.shape), sides, 2)
+    slow_vel = slow(False, nb, tab2, slow_vel)
+
+    back = exchange(env(lists, g, cells.reshape(cells2.shape)))
+    f = fast_only(own, g, cor, q, exm)
+    send, p, v = kick(own, back, f, q, fast_pos, fast_vel)
+    for _ in range(INNER - 1):
+        g = exchange(send)
+        send, p, v = fast_step(own, g, cor, q, exm, v)
+    g = exchange(send)
+    back = exchange(env(lists, g, cells2))
+    f = fast_only(own, g, cor, q, exm)
+    v = last_kick(own, back, f, q, v)
+    return (p, v, slow_pos, slow_vel)
 
 
 def owner_coords(owner, total_cols):
@@ -67,7 +481,7 @@
     return slow_coupling * charge[None, :] * jnp.sum(weight[None] * delta, axis=-1)
 
 
-def per_device(
+def general(
     fast_pos,
     fast_vel,
     fast_charge,
@@ -138,7 +552,7 @@
         picked = jnp.dot(
             select, table, precision=lax.Precision.HIGHEST, preferred_element_type=jnp.float32
         )
-        picked = jnp.transpose(picked.reshape(FAST, 4, CELL), (1, 0, 2))
+        picked = jnp.transpose(picked.reshape(fast_charge.shape[0], 4, CELL), (1, 0, 2))
         partial_env = fast_from_cells(everyone, fast_charge, picked)
         summed = lax.psum(partial_env, ("row", "col"))
         own_env = lax.dynamic_slice_in_dim(summed, flat_index * piece, piece, 1)
@@ -163,25 +577,15 @@
 
 
 def solution(mesh):
+    both = P(None, ("row", "col"))
     return jax.shard_map(
         per_device,
         mesh=mesh,
         in_specs=(
-            P(None, ("row", "col")),
-            P(None, ("row", "col")),
-            P(),
-            P(),
-            P(),
-            P(None, "row", "col", None),
-            P(None, "row", "col", None),
-            P("row", "col", None),
-            P("row", "col", None),
+            both, both, P(), P(), P(),
+            P(None, "row", "col", None), P(None, "row", "col", None),
+            P("row", "col", None), P("row", "col", None),
         ),
-        out_specs=(
-            P(None, ("row", "col")),
-            P(None, ("row", "col")),
-            P(None, "row", "col", None),
-            P(None, "row", "col", None),
-        ),
+        out_specs=(both, both, P(None, "row", "col", None), P(None, "row", "col", None)),
         check_vma=False,
     )

time: 531 us -> 140 us (0.26)
  blocking collectives: 315 us -> 0 us
  other arithmetic: 77.1 us -> 1.01 us
  Pallas kernels: 0 us -> 75.6 us
  matrix products: 34.2 us -> 0 us
  waiting for transfers between devices: 51 us -> 17.4 us
  starting transfers between devices: 14.2 us -> 41 us
  local copies, waits for them, and re-layouts: 19.3 us -> 3.56 us
  between operations: 15.2 us -> 0.92 us
    all_gather x12 -> x0, blocking collectives: 236 us -> none  [the longest x2 130 us: slow_both(): everyone = lax.all_gather(frac, ('row', 'col'), axis=1, tiled=True)]
    psum x2 -> x0, blocking collectives: 78.9 us -> none  [slow_both(): summed = lax.psum(partial_env, ('row', 'col'))]
    pallas_call x0 -> x12, Pallas kernels: none -> 75.6 us  [the longest x2 50.8 us: slow(): pl.pallas_call(functools.partial(slow_kernel, first), out_shape=out, in_s...]
    reduce_sum x20 -> x0, other arithmetic: 54.3 us -> none  [the longest x4 30.9 us: slow_cells(): force = force + jnp.sum(weight[None] * delta, axis=-1)]
    unnamed x10 -> x0, waiting for transfers between devices: 49.2 us -> none
    dot_general x12 -> x0, matrix products: 34.2 us -> none  [the longest x10 20.6 us: slow_cells(): jnp.einsum('abo,oxabn->xabn', pick, views, precision=lax.Precision.HIGHEST)]
    all_to_all x0 -> x7, starting transfers between devices: none -> 28.1 us  [exchange(): return lax.all_to_all(x, BOTH, 0, 0)]
    all_to_all x0 -> x7, waiting for transfers between devices: none -> 17.4 us  [exchange(): return lax.all_to_all(x, BOTH, 0, 0)]
  transfers between devices with their start and end apart: 13 -> 15, of which waited for: 4 -> 4; matrix products, arithmetic and copies ran while one was open for 11% -> 1% of each run, Pallas kernels for 0% -> 52%
where the time goes in v1:
time: 140 us
  Pallas kernels  75.6 us (54%)
  starting transfers between devices  41 us (29%)
  waiting for transfers between devices  17.4 us (12%)
  local copies, waits for them, and re-layouts  3.56 us (3%)
    pallas_call x2, Pallas kernels, slow(): pl.pallas_call(functools.partial(slow_kernel, first), out_shape=out, in_s...  50.8 us
    all_to_all x7, starting transfers between devices, exchange(): return lax.all_to_all(x, BOTH, 0, 0)  28.1 us
    all_to_all x7, waiting for transfers between devices, exchange(): return lax.all_to_all(x, BOTH, 0, 0)  17.4 us
    ppermute x4, starting transfers between devices, with_halo(): after = lax.ppermute(initial, axis, down)  9.11 us
    pallas_call x3, Pallas kernels, fast_step(): pl.pallas_call(fast_step_kernel, out_shape=(sds((count, 3, LANES)), sds((...  8.28 us
    pallas_call x2, Pallas kernels, env(): pl.pallas_call(env_kernel, out_shape=sds((count, 3, LANES)), in_specs=[SM...  5.52 us
    pallas_call x1, Pallas kernels, env_list(): pl.pallas_call(functools.partial(list_kernel, total_cols, cell_rows, cell...  5.43 us
    pallas_call x2, Pallas kernels, fast_only(): pl.pallas_call(fast_only_kernel, out_shape=sds((3, LANES)), in_specs=[SME...  4.18 us
  transfers between devices with their start and end apart: 15, of which 4 were waited for; matrix products, arithmetic and copies ran while one was open for 1% of the time, Pallas kernels for 52%

profile of v1, /device:TPU:0, one launch (start us, length us, event | category | flops | bytes accessed | tf_op | source)
XLA Modules:
  0.0 139.5 jit_solution(7819054960319069586)
XLA Ops:
  0.6 1.3 broadcast_in_dim.4
  1.9 7.3 %all-to-all-start = ((f32[32,3,128]{2,1,0:T(4,128)}), f32[32,3,128]{2,1,0:T(4,128)S(1)}, u32[]{:S(2)}, u32[]{:S(2)}) async-start(f32[32,3,128]{2,1,0:T(4,128)} %broadcast_in_dim.4), calls=%async_computation | async-start | bytes 131072 | tf_op jit(solution)/shard_map/all_to_all | solution.py:389
  10.4 2.4 %collective-permute-start.1 = (f32[2,8,4,128]{3,2,1,0:T(4,128)S(1)}, f32[2,8,4,128]{3,2,1,0:T(4,128)S(1)}, u32[]{:S(2)}, u32[]{:S(2)}) collective-permute-start(f32[2,8,4,128]{3,2,1,0:T(4,128)S(1)} %get-tuple-element.39), channel_id=1, source_target_pairs={{4,0},{8,4},{12,8},{16,12},{20,16},{24,20},{28,24},{0,28},{5,1},{9... | collective-permute-start | bytes 98312 | tf_op jit(solution)/shard_map/ppermute | solution.py:383
  12.9 5.4 %env_list.1 = (s32[3,260]{1,0:T(4,128)S(1)}, s32[1]{0:T(128)}) custom-call(s32[256]{0:T(256)S(1)} %slice.33.owner_ref, s32[2]{0:T(128)S(1)} %pad_add_fusion.base_ref), custom_call_target="tpu_custom_call" | custom-call | tf_op jit(solution)/shard_map/env_list/pallas_call | solution.py:164
  18.4 0.7 add_select_fusion.2
  19.1 2.8 %env.2 = f32[32,3,128]{2,1,0:T(4,128)} custom-call(s32[3,260]{1,0:T(4,128)S(1)} %get-tuple-element.18.list_ref, s32[1]{0:T(128)} %get-tuple-element.19.count_ref, f32[32,3,128]{2,1,0:T(4,128)S(1)} %all-to-all-done.g_ref, f32[32,4,128]{2,1,0:T(4,128)S(1)} %bitcast.41), custom_call_target="tpu_custom_call" | custom-call | flops 2000000 | bytes 200000 | tf_op jit(solution)/shard_map/env/pallas_call | solution.py:210
  21.8 4.7 %all-to-all-start.1 = ((f32[32,3,128]{2,1,0:T(4,128)}), f32[32,3,128]{2,1,0:T(4,128)S(1)}, u32[]{:S(2)}, u32[]{:S(2)}) async-start(f32[32,3,128]{2,1,0:T(4,128)} %env.2), calls=%async_computation.1 | async-start | bytes 131072 | tf_op jit(solution)/shard_map/all_to_all | solution.py:389
  26.6 0.7 copy-done
  27.3 2.1 %fast_only.2.f_ref = f32[3,128]{1,0:T(4,128)S(1)} custom-call(s32[1]{0:T(128)} %bitcast.own_ref, f32[32,3,128]{2,1,0:T(4,128)S(1)} %all-to-all-done.g_ref, f32[2,32,128]{2,1,0:T(8,128)S(1)} %add_convert_fusion.cor_ref, f32[32,128]{1,0:T(8,128)S(1)} %bitcast.42, f32[16,128]{1,0:T(8,128)S(1)} %convert_element_type.7.exm_ref), custom_call_target="tpu_custom_call" | custom-call | flops 9961472 | bytes 131072 | tf_op jit(solution)/shard_map/fast_only/pallas_call | solution.py:115
  29.4 4.7 %all-to-all-done.1.e_ref = f32[32,3,128]{2,1,0:T(4,128)S(1)} async-done(((f32[32,3,128]{2,1,0:T(4,128)}), f32[32,3,128]{2,1,0:T(4,128)S(1)}, u32[]{:S(2)}, u32[]{:S(2)}) %all-to-all-start.1) | async-done | bytes 49184 | tf_op jit(solution)/shard_map/all_to_all | solution.py:389
  34.1 0.7 kick.1
  34.8 2.6 %all-to-all-start.2 = ((f32[32,3,128]{2,1,0:T(4,128)}), f32[32,3,128]{2,1,0:T(4,128)S(1)}, u32[]{:S(2)}, u32[]{:S(2)}) async-start(f32[32,3,128]{2,1,0:T(4,128)} %get-tuple-element.20), calls=%async_computation.2 | async-start | bytes 131072 | tf_op jit(solution)/shard_map/all_to_all | solution.py:389
  37.4 1.7 %collective-permute-start.2 = (f32[8,2,4,128]{3,2,1,0:T(4,128)S(1)}, f32[8,2,4,128]{3,2,1,0:T(4,128)S(1)}, u32[]{:S(2)}, u32[]{:S(2)}) collective-permute-start(f32[8,2,4,128]{3,2,1,0:T(4,128)S(1)} %get-tuple-element.34), channel_id=1, source_target_pairs={{0,1},{1,2},{2,3},{3,0},{4,5},{5,6},{6,7},{7,4},{8,9},{9,10},{10,1... | collective-permute-start | bytes 98312 | tf_op jit(solution)/shard_map/ppermute | solution.py:382
  39.2 2.1 %collective-permute-start.3 = (f32[8,2,4,128]{3,2,1,0:T(4,128)S(1)}, f32[8,2,4,128]{3,2,1,0:T(4,128)S(1)}, u32[]{:S(2)}, u32[]{:S(2)}) collective-permute-start(f32[8,2,4,128]{3,2,1,0:T(4,128)S(1)} %get-tuple-element.35), channel_id=1, source_target_pairs={{1,0},{2,1},{3,2},{0,3},{5,4},{6,5},{7,6},{4,7},{9,8},{10,9},{11,1... | collective-permute-start | bytes 98312 | tf_op jit(solution)/shard_map/ppermute | solution.py:383
  41.4 3.8 %all-to-all-done.2.g_ref = f32[32,3,128]{2,1,0:T(4,128)S(1)} async-done(((f32[32,3,128]{2,1,0:T(4,128)}), f32[32,3,128]{2,1,0:T(4,128)S(1)}, u32[]{:S(2)}, u32[]{:S(2)}) %all-to-all-start.2) | async-done | bytes 49184 | tf_op jit(solution)/shard_map/all_to_all | solution.py:389
  45.2 2.8 %fast_step.3 = (f32[32,3,128]{2,1,0:T(4,128)}, f32[3,128]{1,0:T(4,128)}, f32[3,128]{1,0:T(4,128)S(1)}) custom-call(s32[1]{0:T(128)} %bitcast.own_ref, f32[32,3,128]{2,1,0:T(4,128)S(1)} %all-to-all-done.2.g_ref, f32[2,32,128]{2,1,0:T(8,128)S(1)} %add_convert_fusion.cor_ref, f32[32,128]{1,0:T(8,128)S(1)} %bitcast.44, ...), custom_call_target="tpu_custom_call" | custom-call | flops 9961472 | bytes 131072 | tf_op jit(solution)/shard_map/fast_step/pallas_call | solution.py:129
  47.9 2.6 %all-to-all-start.3 = ((f32[32,3,128]{2,1,0:T(4,128)}), f32[32,3,128]{2,1,0:T(4,128)S(1)}, u32[]{:S(2)}, u32[]{:S(2)}) async-start(f32[32,3,128]{2,1,0:T(4,128)} %get-tuple-element.22), calls=%async_computation.3 | async-start | bytes 131072 | tf_op jit(solution)/shard_map/all_to_all | solution.py:389
  50.6 0.7 copy-done.3
  51.3 25.5 %slow.2 = (f32[3,4,8,128]{3,2,1,0:T(8,128)S(1)}, f32[3,4,8,128]{3,2,1,0:T(8,128)}, f32[32,4,128]{2,1,0:T(4,128)S(1)}) custom-call(s32[32,5]{1,0:T(8,128)S(1)} %bitcast.49, f32[8,12,4,128]{3,2,1,0:T(4,128)S(1)} %pad_maximum_fusion.tab_ref, f32[3,4,8,128]{3,2,1,0:T(8,128)S(1)} %copy-done.3), custom_call_target="tpu_custom_call" | custom-call | flops 49807360 | bytes 1000000 | tf_op jit(solution)/shard_map/slow/pallas_call | solution.py:361
  76.8 2.8 %fast_step.4 = (f32[32,3,128]{2,1,0:T(4,128)}, f32[3,128]{1,0:T(4,128)}, f32[3,128]{1,0:T(4,128)S(1)}) custom-call(s32[1]{0:T(128)} %bitcast.own_ref, f32[32,3,128]{2,1,0:T(4,128)S(1)} %all-to-all-done.3.g_ref, f32[2,32,128]{2,1,0:T(8,128)S(1)} %add_convert_fusion.cor_ref, f32[32,128]{1,0:T(8,128)S(1)} %bitcast.45, ...), custom_call_target="tpu_custom_call" | custom-call | flops 9961472 | bytes 131072 | tf_op jit(solution)/shard_map/fast_step/pallas_call | solution.py:129
  79.5 5.8 %all-to-all-start.4 = ((f32[32,3,128]{2,1,0:T(4,128)}), f32[32,3,128]{2,1,0:T(4,128)S(1)}, u32[]{:S(2)}, u32[]{:S(2)}) async-start(f32[32,3,128]{2,1,0:T(4,128)} %get-tuple-element.24), calls=%async_computation.4 | async-start | bytes 131072 | tf_op jit(solution)/shard_map/all_to_all | solution.py:389
  85.4 2.4 %collective-permute-start.5 = (f32[2,8,4,128]{3,2,1,0:T(4,128)S(1)}, f32[2,8,4,128]{3,2,1,0:T(4,128)S(1)}, u32[]{:S(2)}, u32[]{:S(2)}) collective-permute-start(f32[2,8,4,128]{3,2,1,0:T(4,128)S(1)} %bitcast.54), channel_id=1, source_target_pairs={{4,0},{8,4},{12,8},{16,12},{20,16},{24,20},{28,24},{0,28},{5,1},{9... | collective-permute-start | bytes 98312 | tf_op jit(solution)/shard_map/ppermute | solution.py:383
  87.8 5.0 %all-to-all-done.4.g_ref = f32[32,3,128]{2,1,0:T(4,128)S(1)} async-done(((f32[32,3,128]{2,1,0:T(4,128)}), f32[32,3,128]{2,1,0:T(4,128)S(1)}, u32[]{:S(2)}, u32[]{:S(2)}) %all-to-all-start.4) | async-done | bytes 49184 | tf_op jit(solution)/shard_map/all_to_all | solution.py:389
  92.9 2.8 %fast_step.5 = (f32[32,3,128]{2,1,0:T(4,128)}, f32[3,128]{1,0:T(4,128)}, f32[3,128]{1,0:T(4,128)S(1)}) custom-call(s32[1]{0:T(128)} %bitcast.own_ref, f32[32,3,128]{2,1,0:T(4,128)S(1)} %all-to-all-done.4.g_ref, f32[2,32,128]{2,1,0:T(8,128)S(1)} %add_convert_fusion.cor_ref, f32[32,128]{1,0:T(8,128)S(1)} %bitcast.46, ...), custom_call_target="tpu_custom_call" | custom-call | flops 9961472 | bytes 131072 | tf_op jit(solution)/shard_map/fast_step/pallas_call | solution.py:129
  95.6 2.6 %all-to-all-start.5 = ((f32[32,3,128]{2,1,0:T(4,128)}), f32[32,3,128]{2,1,0:T(4,128)S(1)}, u32[]{:S(2)}, u32[]{:S(2)}) async-start(f32[32,3,128]{2,1,0:T(4,128)} %get-tuple-element.27), calls=%async_computation.5 | async-start | bytes 131072 | tf_op jit(solution)/shard_map/all_to_all | solution.py:389
  98.2 1.7 %collective-permute-start.6 = (f32[8,2,4,128]{3,2,1,0:T(4,128)S(1)}, f32[8,2,4,128]{3,2,1,0:T(4,128)S(1)}, u32[]{:S(2)}, u32[]{:S(2)}) collective-permute-start(f32[8,2,4,128]{3,2,1,0:T(4,128)S(1)} %get-tuple-element.32), channel_id=1, source_target_pairs={{0,1},{1,2},{2,3},{3,0},{4,5},{5,6},{6,7},{7,4},{8,9},{9,10},{10,1... | collective-permute-start | bytes 98312 | tf_op jit(solution)/shard_map/ppermute | solution.py:382
  100.0 2.1 %collective-permute-start.7 = (f32[8,2,4,128]{3,2,1,0:T(4,128)S(1)}, f32[8,2,4,128]{3,2,1,0:T(4,128)S(1)}, u32[]{:S(2)}, u32[]{:S(2)}) collective-permute-start(f32[8,2,4,128]{3,2,1,0:T(4,128)S(1)} %get-tuple-element.33), channel_id=1, source_target_pairs={{1,0},{2,1},{3,2},{0,3},{5,4},{6,5},{7,6},{4,7},{9,8},{10,9},{11,1... | collective-permute-start | bytes 98312 | tf_op jit(solution)/shard_map/ppermute | solution.py:383
  102.1 3.9 %all-to-all-done.5.g_ref = f32[32,3,128]{2,1,0:T(4,128)S(1)} async-done(((f32[32,3,128]{2,1,0:T(4,128)}), f32[32,3,128]{2,1,0:T(4,128)S(1)}, u32[]{:S(2)}, u32[]{:S(2)}) %all-to-all-start.5) | async-done | bytes 49184 | tf_op jit(solution)/shard_map/all_to_all | solution.py:389
  106.0 2.8 %env.3 = f32[32,3,128]{2,1,0:T(4,128)} custom-call(s32[3,260]{1,0:T(4,128)S(1)} %get-tuple-element.18.list_ref, s32[1]{0:T(128)} %get-tuple-element.19.count_ref, f32[32,3,128]{2,1,0:T(4,128)S(1)} %all-to-all-done.5.g_ref, f32[32,4,128]{2,1,0:T(4,128)S(1)} %get-tuple-element.28.cells_ref), custom_call_target="tpu_custom_call" | custom-call | flops 2000000 | bytes 200000 | tf_op jit(solution)/shard_map/env/pallas_call | solution.py:210
  108.8 2.6 %all-to-all-start.6 = ((f32[32,3,128]{2,1,0:T(4,128)}), f32[32,3,128]{2,1,0:T(4,128)S(1)}, u32[]{:S(2)}, u32[]{:S(2)}) async-start(f32[32,3,128]{2,1,0:T(4,128)} %env.3), calls=%async_computation.6 | async-start | bytes 131072 | tf_op jit(solution)/shard_map/all_to_all | solution.py:389
  111.4 25.4 %slow.3 = f32[3,4,8,128]{3,2,1,0:T(8,128)} custom-call(s32[32,5]{1,0:T(8,128)S(1)} %bitcast.50, f32[8,12,4,128]{3,2,1,0:T(4,128)S(1)} %pad_maximum_fusion.1.tab_ref, f32[3,4,8,128]{3,2,1,0:T(8,128)S(1)} %get-tuple-element.31.vel_ref), custom_call_target="tpu_custom_call" | custom-call | flops 49807360 | bytes 1000000 | tf_op jit(solution)/shard_map/slow/pallas_call | solution.py:361
  136.8 2.1 %fast_only.3.f_ref = f32[3,128]{1,0:T(4,128)S(1)} custom-call(s32[1]{0:T(128)} %bitcast.own_ref, f32[32,3,128]{2,1,0:T(4,128)S(1)} %all-to-all-done.5.g_ref, f32[2,32,128]{2,1,0:T(8,128)S(1)} %add_convert_fusion.cor_ref, f32[32,128]{1,0:T(8,128)S(1)} %bitcast.47, f32[16,128]{1,0:T(8,128)S(1)} %convert_element_type.7.exm_ref), custom_call_target="tpu_custom_call" | custom-call | flops 9961472 | bytes 131072 | tf_op jit(solution)/shard_map/fast_only/pallas_call | solution.py:115
  (44 shorter events, 2.1 us)
Async XLA Ops:
  1.9 7.3 %copy-start.5 = (f32[3,4,8,128]{3,2,1,0:T(8,128)S(1)}, f32[3,4,8,128]{3,2,1,0:T(8,128)}, u32[]{:S(2)}) copy-start(f32[3,4,8,128]{3,2,1,0:T(8,128)} %param.14) | copy-start | bytes 147460
  1.9 17.1 %all-to-all-start = ((f32[32,3,128]{2,1,0:T(4,128)}), f32[32,3,128]{2,1,0:T(4,128)S(1)}, u32[]{:S(2)}, u32[]{:S(2)}) async-start(f32[32,3,128]{2,1,0:T(4,128)} %broadcast_in_dim.4), calls=%async_computation | async-start | bytes 131072 | tf_op jit(solution)/shard_map/all_to_all | solution.py:389
  9.3 0.7 copy-start.4
  10.1 2.7 %copy-start.6 = (s32[4096]{0:T(1024)S(1)}, s32[4096]{0:T(1024)}, u32[]{:S(2)}) copy-start(s32[4096]{0:T(1024)} %param.12) | copy-start | bytes 49156
  10.1 27.3 %collective-permute-start = (f32[2,8,4,128]{3,2,1,0:T(4,128)S(1)}, f32[2,8,4,128]{3,2,1,0:T(4,128)S(1)}, u32[]{:S(2)}, u32[]{:S(2)}) collective-permute-start(f32[2,8,4,128]{3,2,1,0:T(4,128)S(1)} %get-tuple-element.38), channel_id=1, source_target_pairs={{0,4},{4,8},{8,12},{12,16},{16,20},{20,24},{24,28},{28,0},{1,5},{5... | collective-permute-start | bytes 98312 | tf_op jit(solution)/shard_map/ppermute | solution.py:382
  10.4 27.0 %collective-permute-start.1 = (f32[2,8,4,128]{3,2,1,0:T(4,128)S(1)}, f32[2,8,4,128]{3,2,1,0:T(4,128)S(1)}, u32[]{:S(2)}, u32[]{:S(2)}) collective-permute-start(f32[2,8,4,128]{3,2,1,0:T(4,128)S(1)} %get-tuple-element.39), channel_id=1, source_target_pairs={{4,0},{8,4},{12,8},{16,12},{20,16},{24,20},{28,24},{0,28},{5,1},{9... | collective-permute-start | bytes 98312 | tf_op jit(solution)/shard_map/ppermute | solution.py:383
  21.8 12.2 %all-to-all-start.1 = ((f32[32,3,128]{2,1,0:T(4,128)}), f32[32,3,128]{2,1,0:T(4,128)S(1)}, u32[]{:S(2)}, u32[]{:S(2)}) async-start(f32[32,3,128]{2,1,0:T(4,128)} %env.2), calls=%async_computation.1 | async-start | bytes 131072 | tf_op jit(solution)/shard_map/all_to_all | solution.py:389
  26.6 0.7 copy-start
  27.3 6.8 %copy-start.1 = (f32[3,128]{1,0:T(4,128)S(1)}, f32[3,128]{1,0:T(4,128)}, u32[]{:S(2)}) copy-start(f32[3,128]{1,0:T(4,128)} %p_ref.1) | copy-start | bytes 4612
  27.3 6.8 %copy-start.2 = (f32[3,128]{1,0:T(4,128)S(1)}, f32[3,128]{1,0:T(4,128)}, u32[]{:S(2)}) copy-start(f32[3,128]{1,0:T(4,128)} %v_ref.1) | copy-start | bytes 4612
  34.8 10.4 %all-to-all-start.2 = ((f32[32,3,128]{2,1,0:T(4,128)}), f32[32,3,128]{2,1,0:T(4,128)S(1)}, u32[]{:S(2)}, u32[]{:S(2)}) async-start(f32[32,3,128]{2,1,0:T(4,128)} %get-tuple-element.20), calls=%async_computation.2 | async-start | bytes 131072 | tf_op jit(solution)/shard_map/all_to_all | solution.py:389
  37.4 3.9 %copy-start.7 = (s32[4,8,5]{1,0,2:T(4,128)S(1)}, s32[4,8,5]{1,0,2:T(4,128)}, u32[]{:S(2)}) copy-start(s32[4,8,5]{1,0,2:T(4,128)} %param.17) | copy-start | bytes 1924
  37.4 13.1 %collective-permute-start.2 = (f32[8,2,4,128]{3,2,1,0:T(4,128)S(1)}, f32[8,2,4,128]{3,2,1,0:T(4,128)S(1)}, u32[]{:S(2)}, u32[]{:S(2)}) collective-permute-start(f32[8,2,4,128]{3,2,1,0:T(4,128)S(1)} %get-tuple-element.34), channel_id=1, source_target_pairs={{0,1},{1,2},{2,3},{3,0},{4,5},{5,6},{6,7},{7,4},{8,9},{9,10},{10,1... | collective-permute-start | bytes 98312 | tf_op jit(solution)/shard_map/ppermute | solution.py:382
  39.2 11.4 %collective-permute-start.3 = (f32[8,2,4,128]{3,2,1,0:T(4,128)S(1)}, f32[8,2,4,128]{3,2,1,0:T(4,128)S(1)}, u32[]{:S(2)}, u32[]{:S(2)}) collective-permute-start(f32[8,2,4,128]{3,2,1,0:T(4,128)S(1)} %get-tuple-element.35), channel_id=1, source_target_pairs={{1,0},{2,1},{3,2},{0,3},{5,4},{6,5},{7,6},{4,7},{9,8},{10,9},{11,1... | collective-permute-start | bytes 98312 | tf_op jit(solution)/shard_map/ppermute | solution.py:383
  47.9 28.8 %all-to-all-start.3 = ((f32[32,3,128]{2,1,0:T(4,128)}), f32[32,3,128]{2,1,0:T(4,128)S(1)}, u32[]{:S(2)}, u32[]{:S(2)}) async-start(f32[32,3,128]{2,1,0:T(4,128)} %get-tuple-element.22), calls=%async_computation.3 | async-start | bytes 131072 | tf_op jit(solution)/shard_map/all_to_all | solution.py:389
  50.5 0.8 copy-start.3
  79.5 13.3 %all-to-all-start.4 = ((f32[32,3,128]{2,1,0:T(4,128)}), f32[32,3,128]{2,1,0:T(4,128)S(1)}, u32[]{:S(2)}, u32[]{:S(2)}) async-start(f32[32,3,128]{2,1,0:T(4,128)} %get-tuple-element.24), calls=%async_computation.4 | async-start | bytes 131072 | tf_op jit(solution)/shard_map/all_to_all | solution.py:389
  85.4 12.8 %collective-permute-start.5 = (f32[2,8,4,128]{3,2,1,0:T(4,128)S(1)}, f32[2,8,4,128]{3,2,1,0:T(4,128)S(1)}, u32[]{:S(2)}, u32[]{:S(2)}) collective-permute-start(f32[2,8,4,128]{3,2,1,0:T(4,128)S(1)} %bitcast.54), channel_id=1, source_target_pairs={{4,0},{8,4},{12,8},{16,12},{20,16},{24,20},{28,24},{0,28},{5,1},{9... | collective-permute-start | bytes 98312 | tf_op jit(solution)/shard_map/ppermute | solution.py:383
  87.8 10.4 %collective-permute-start.4 = (f32[2,8,4,128]{3,2,1,0:T(4,128)S(1)}, f32[2,8,4,128]{3,2,1,0:T(4,128)S(1)}, u32[]{:S(2)}, u32[]{:S(2)}) collective-permute-start(f32[2,8,4,128]{3,2,1,0:T(4,128)S(1)} %bitcast.53), channel_id=1, source_target_pairs={{0,4},{4,8},{8,12},{12,16},{16,20},{20,24},{24,28},{28,0},{1,5},{5... | collective-permute-start | bytes 98312 | tf_op jit(solution)/shard_map/ppermute | solution.py:382
  95.6 10.4 %all-to-all-start.5 = ((f32[32,3,128]{2,1,0:T(4,128)}), f32[32,3,128]{2,1,0:T(4,128)S(1)}, u32[]{:S(2)}, u32[]{:S(2)}) async-start(f32[32,3,128]{2,1,0:T(4,128)} %get-tuple-element.27), calls=%async_computation.5 | async-start | bytes 131072 | tf_op jit(solution)/shard_map/all_to_all | solution.py:389
  98.2 13.1 %collective-permute-start.6 = (f32[8,2,4,128]{3,2,1,0:T(4,128)S(1)}, f32[8,2,4,128]{3,2,1,0:T(4,128)S(1)}, u32[]{:S(2)}, u32[]{:S(2)}) collective-permute-start(f32[8,2,4,128]{3,2,1,0:T(4,128)S(1)} %get-tuple-element.32), channel_id=1, source_target_pairs={{0,1},{1,2},{2,3},{3,0},{4,5},{5,6},{6,7},{7,4},{8,9},{9,10},{10,1... | collective-permute-start | bytes 98312 | tf_op jit(solution)/shard_map/ppermute | solution.py:382
  100.0 11.4 %collective-permute-start.7 = (f32[8,2,4,128]{3,2,1,0:T(4,128)S(1)}, f32[8,2,4,128]{3,2,1,0:T(4,128)S(1)}, u32[]{:S(2)}, u32[]{:S(2)}) collective-permute-start(f32[8,2,4,128]{3,2,1,0:T(4,128)S(1)} %get-tuple-element.33), channel_id=1, source_target_pairs={{1,0},{2,1},{3,2},{0,3},{5,4},{6,5},{7,6},{4,7},{9,8},{10,9},{11,1... | collective-permute-start | bytes 98312 | tf_op jit(solution)/shard_map/ppermute | solution.py:383
  108.8 30.1 %all-to-all-start.6 = ((f32[32,3,128]{2,1,0:T(4,128)}), f32[32,3,128]{2,1,0:T(4,128)S(1)}, u32[]{:S(2)}, u32[]{:S(2)}) async-start(f32[32,3,128]{2,1,0:T(4,128)} %env.3), calls=%async_computation.6 | async-start | bytes 131072 | tf_op jit(solution)/shard_map/all_to_all | solution.py:389

commit v2 on v1

--- a/solution.py
+++ b/solution.py
@@ -7,6 +7,7 @@
 from jax.experimental.pallas import tpu as pltpu
 from jax.sharding import PartitionSpec as P
 
+
 CELL = 128
 INNER = 4
 GROUPS = 256
@@ -19,7 +20,6 @@
 
 BOTH = ("row", "col")
 F32 = jnp.float32
-BF16 = jnp.bfloat16
 LANES = 128
 ENV_UNROLL = 4
 VMEM = pl.BlockSpec(memory_space=pltpu.VMEM)
@@ -140,30 +140,31 @@
 
 def list_kernel(total_cols, cell_rows, cell_cols, owner_ref, base_ref, list_ref, count_ref):
     row0, col0 = base_ref[0], base_ref[1]
-    step = GROUPS // LANES
-
-    def body(i, n):
-        cell = owner_ref[i]
-        r = lax.div(cell, total_cols) - row0
-        c = lax.rem(cell, total_cols) - col0
-        inside = (r >= 0) & (r < cell_rows) & (c >= 0) & (c < cell_cols)
-        list_ref[0, n] = lax.div(i, LANES)
-        list_ref[1, n] = lax.rem(i, LANES)
-        list_ref[2, n] = r * cell_cols + c
-        return n + inside.astype(jnp.int32)
-
-    n = lax.fori_loop(0, GROUPS, body, jnp.int32(0))
+
+    unroll = 8
+
+    def body(j, n):
+        for u in range(unroll):
+            i = j * unroll + u
+            cell = owner_ref[i]
+            r = lax.div(cell, total_cols)
+            c = cell - r * total_cols - col0
+            r = r - row0
+            sign = r | (cell_rows - 1 - r) | c | (cell_cols - 1 - c)
+            list_ref[n] = i + (r * cell_cols + c) * GROUPS
+            n = n + (1 + lax.shift_right_arithmetic(sign, 31))
+        return n
+
+    n = lax.fori_loop(0, GROUPS // unroll, body, jnp.int32(0))
     count_ref[0] = n
     for k in range(ENV_UNROLL):
-        list_ref[0, n + k] = 0
-        list_ref[1, n + k] = -1
-        list_ref[2, n + k] = 0
+        list_ref[n + k] = -1
 
 
 def env_list(owner, base, total_cols, cell_rows, cell_cols):
     return pl.pallas_call(
         functools.partial(list_kernel, total_cols, cell_rows, cell_cols),
-        out_shape=(sds((3, GROUPS + ENV_UNROLL), jnp.int32), sds((1,), jnp.int32)),
+        out_shape=(sds((GROUPS + ENV_UNROLL,), jnp.int32), sds((1,), jnp.int32)),
         in_specs=[SMEM, SMEM],
         out_specs=(SMEM, SMEM),
         name="env_list",
@@ -183,9 +184,11 @@
     def body(t, carry):
         for u in range(ENV_UNROLL):
             n = t * ENV_UNROLL + u
-            h = list_ref[0, n]
-            here = lane == list_ref[1, n]
-            cell = cells_ref[list_ref[2, n]]
+            entry = list_ref[n]
+            group = entry & (GROUPS - 1)
+            h = lax.shift_right_logical(group, LANES.bit_length() - 1)
+            here = (lane == (group & (LANES - 1))) & (entry >= 0)
+            cell = cells_ref[jnp.maximum(lax.div(entry, GROUPS), 0)]
             d = []
             for c in range(3):
                 x = jnp.sum(jnp.where(here, planes[c, h], 0.0), axis=1, keepdims=True)
@@ -266,109 +269,93 @@
     )(own, e, f, q, v)
 
 
-def split3(x):
-    hi = x.astype(BF16).astype(F32)
-    rest = x - hi
-    mid = rest.astype(BF16).astype(F32)
-    return hi, mid, rest - mid
-
-
-def slow_kernel(first, nb_ref, tab_ref, vel_ref, *refs):
+def slow_kernel(first, row0, nb_ref, tab_ref, vel_ref, *refs):
     if first:
-        vel_out, pos_out, cell_out, feat, vals = refs
+        vel_out, pos_out, cell_out, cols_a, cols_b, sums_a, sums_b = refs
     else:
-        vel_out, feat, vals = refs
-    all_rows, all_cols = tab_ref.shape[0], tab_ref.shape[1]
-    cell_rows, cell_cols = vel_ref.shape[1], vel_ref.shape[2]
+        vel_out, cols_a, cols_b, sums_a, sums_b = refs
+    cell_rows, cell_cols = vel_out.shape[1], vel_out.shape[2]
     slots = nb_ref.shape[1]
-    row8 = lax.broadcasted_iota(jnp.int32, (8, LANES), 0)
-
-    def load8(r, c):
-        t = tab_ref[r, c]
-        return jnp.concatenate([t, jnp.zeros_like(t)], axis=0)
-
-    def one_cell(n):
-        t = load8(lax.div(n, all_cols), lax.rem(n, all_cols))
-        pos = jnp.where(row8 < 3, t, 0.0)
-        norm = jnp.sum(pos * pos, axis=0, keepdims=True) + 0.5
-        b = jnp.where(row8 == 3, 1.0, jnp.where(row8 == 4, norm, -2.0 * pos))
-        hi, mid, lo = split3(b)
-        wide = jnp.concatenate([hi, mid, hi, lo, mid, hi], axis=0)
-        feat[n] = jnp.transpose(wide).astype(BF16)
-        charge = t[3:4, :]
-        u = jnp.where(row8 == 3, charge, pos * charge)
-        hi = u.astype(BF16).astype(F32)
-        vals[n] = jnp.concatenate([hi, u - hi], axis=0).astype(BF16)
-
-    def prepare(i, carry):
-        for u in range(4):
-            one_cell(i * 4 + u)
-        return carry
-
-    lax.fori_loop(0, all_rows * all_cols // 4, prepare, 0)
-
-    def body(n, carry):
-        r = lax.div(n, cell_cols)
-        c = lax.rem(n, cell_cols)
-        t = load8(r + 2, c + 2)
-        pos = jnp.where(row8 < 3, t, 0.0)
-        force = jnp.zeros((8, LANES), F32)
+    count = cell_rows * cell_cols
+
+    def place(n):
+        return lax.div(n, cell_cols), lax.rem(n, cell_cols)
+
+    def spread(n, cols):
+        r, c = place(n)
+        t = tab_ref[r + (row0 + 2), c + 2]
+        for x in range(3):
+            cols[x] = jnp.transpose(jnp.broadcast_to(t[x : x + 1], (CELL, CELL)))
+
+    def pairs(n, cols, sums):
+        r, c = place(n)
+        others = []
         for k in range(slots):
-            o = nb_ref[n, k]
-            dr = lax.div(o, 5)
-            dc = lax.rem(o, 5)
-            shift = jnp.where(
-                row8 == 0, (dr - 2).astype(F32), jnp.where(row8 == 1, (dc - 2).astype(F32), 0.0)
-            )
-            x = pos - shift
-            norm = jnp.sum(x * x, axis=0, keepdims=True)
-            a = jnp.where(row8 == 3, norm, jnp.where(row8 == 4, 1.0, x))
-            hi, mid, lo = split3(a)
-            wide = jnp.concatenate([hi, hi, mid, hi, mid, lo], axis=0).astype(BF16)
-            other = (r + dr) * all_cols + c + dc
-            s = jnp.dot(feat[other], wide, preferred_element_type=F32)
-            inv = lax.rsqrt(s)
-            w = inv * (inv * inv)
-            whi = w.astype(BF16)
-            wlo = (w - whi.astype(F32)).astype(BF16)
-            g = vals[other]
-            both = jnp.dot(g, whi, preferred_element_type=F32) + jnp.dot(
-                g, wlo, preferred_element_type=F32
-            )
-            total = both[0:8] + both[8:16]
-            force = force + (x * total[3:4, :] - total)
-        force = slow_coupling * t[3:4, :] * force
+            o = nb_ref[n + row0 * cell_cols, k]
+            dr, dc = lax.div(o, 5), lax.rem(o, 5)
+            t = tab_ref[r + (dr + row0), c + dc]
+            rows = [t[0:1] + (dr - 2).astype(F32), t[1:2] + (dc - 2).astype(F32), t[2:3], t[3:4]]
+            others.append([jnp.broadcast_to(y, (8, CELL)) for y in rows])
+        for g in range(CELL // 8):
+            at = slice(8 * g, 8 * g + 8)
+            a = [cols[x, at, :] for x in range(3)]
+            acc = None
+            for y in others:
+                d = [a[x] - y[x] for x in range(3)]
+                i = lax.rsqrt(d[0] * d[0] + d[1] * d[1] + d[2] * d[2] + 0.5)
+                w = (y[3] * i) * (i * i)
+                f = [w * d[x] for x in range(3)]
+                acc = f if acc is None else [acc[x] + f[x] for x in range(3)]
+            for x in range(3):
+                sums[x, at, :] = acc[x]
+
+    def finish(n, sums):
+        r, c = place(n)
+        t = tab_ref[r + (row0 + 2), c + 2]
+        scale = slow_coupling * t[3:4]
         for x in range(3):
-            here = (x, r, pl.ds(c, 1), slice(None))
-            v = vel_ref[here] + half_outer * force[x : x + 1]
-            vel_out[here] = v
+            f = scale * jnp.sum(jnp.transpose(sums[x]), axis=0, keepdims=True)
+            v = vel_ref[x, r + row0, pl.ds(c, 1), :] + half_outer * f
+            vel_out[x, r, pl.ds(c, 1), :] = v
             if first:
                 p = t[x : x + 1] + outer_dt * v
-                pos_out[here] = p
+                pos_out[x, r, pl.ds(c, 1), :] = p
                 cell_out[n, x : x + 1, :] = p
         if first:
             cell_out[n, 3:4, :] = t[3:4]
+
+    spread(0, cols_a)
+
+    def body(i, carry):
+        n = 2 * i
+        spread(n + 1, cols_b)
+        pairs(n, cols_a, sums_a)
+        finish(jnp.maximum(n - 1, 0), sums_b)
+        spread(jnp.minimum(n + 2, count - 1), cols_a)
+        pairs(n + 1, cols_b, sums_b)
+        finish(n, sums_a)
         return carry
 
-    lax.fori_loop(0, cell_rows * cell_cols, body, 0)
-
-
-def slow(first, nb, tab, vel):
-    cells = tab.shape[0] * tab.shape[1]
-    own = vel.shape[1] * vel.shape[2]
-    out = (sds(vel.shape), sds(vel.shape), sds((own, 4, CELL))) if first else sds(vel.shape)
+    lax.fori_loop(0, count // 2, body, 0)
+    finish(count - 1, sums_b)
+
+
+def slow(first, row0, rows, nb, tab, vel):
+    shape = (3, rows) + vel.shape[2:]
+    own = rows * vel.shape[2]
+    out = (sds(shape), sds(shape), sds((own, 4, CELL))) if first else sds(shape)
     pairs = own * nb.shape[1] * CELL * CELL
     return pl.pallas_call(
-        functools.partial(slow_kernel, first),
+        functools.partial(slow_kernel, first, row0),
         out_shape=out,
         in_specs=[SMEM, VMEM, VMEM],
         out_specs=(VMEM,) * 3 if first else VMEM,
-        scratch_shapes=[pltpu.VMEM((cells, CELL, 48), BF16), pltpu.VMEM((cells, 16, CELL), BF16)],
+        scratch_shapes=[pltpu.VMEM((3, CELL, CELL), F32)] * 4,
+        compiler_params=pltpu.CompilerParams(vmem_limit_bytes=3 << 20),
         cost_estimate=pl.CostEstimate(
             flops=19 * pairs, transcendentals=pairs, bytes_accessed=1_000_000
         ),
         name="slow",
-        compiler_params=pltpu.CompilerParams(vmem_limit_bytes=8 << 20),
     )(nb, tab, vel)
 
 
@@ -389,15 +376,14 @@
     return lax.all_to_all(x, BOTH, 0, 0)
 
 
-def per_device(
+def per_device(*args):
+    return rows_of_lanes(*args)
+
+
+def rows_of_lanes(
     fast_pos, fast_vel, fast_charge, fast_owner, exclusions,
     slow_pos, slow_vel, slow_charge, neighbours,
 ):
-    if fast_pos.shape[1] != LANES:
-        return general(
-            fast_pos, fast_vel, fast_charge, fast_owner, exclusions,
-            slow_pos, slow_vel, slow_charge, neighbours,
-        )
     row_count, col_count = lax.axis_size("row"), lax.axis_size("col")
     row_index, col_index = lax.axis_index("row"), lax.axis_index("col")
     flat = row_index * col_count + col_index
@@ -423,9 +409,18 @@
     cells = jnp.concatenate([slow_pos, slow_charge[None]], axis=0).transpose(1, 2, 0, 3)
     sides = (("row", 0), ("col", 1))
     nb = neighbours.reshape(cell_rows * cell_cols, -1)
-    slow_vel, slow_pos, cells2 = slow(True, nb, with_halo(cells, sides, 2), slow_vel)
+    half = cell_rows // 2
+    tab = with_halo(cells, sides, 2)
+    parts = []
+    for r0 in (0, half):
+        parts.append(slow(True, r0, half, nb, tab, slow_vel))
+    slow_vel, slow_pos = (jnp.concatenate([parts[0][i], parts[1][i]], axis=1) for i in (0, 1))
+    cells2 = jnp.concatenate([parts[0][2], parts[1][2]], axis=0)
     tab2 = with_halo(cells2.reshape(cells.shape), sides, 2)
-    slow_vel = slow(False, nb, tab2, slow_vel)
+    parts = []
+    for r0 in (0, half):
+        parts.append(slow(False, r0, half, nb, tab2, slow_vel))
+    slow_vel = jnp.concatenate(parts, axis=1)
 
     back = exchange(env(lists, g, cells.reshape(cells2.shape)))
     f = fast_only(own, g, cor, q, exm)
@@ -564,7 +559,7 @@
     slow_acc, env_acc = slow_both(slow_pos, fast_pos)
     slow_vel = slow_vel + half_outer * slow_acc
     fast_vel = fast_vel + half_outer * env_acc
-    for inner_step in range(INNER):
+    for _ in range(INNER):
         fast_vel = fast_vel + 0.5 * inner_dt * fast_acc
         fast_pos = fast_pos + inner_dt * fast_vel
         fast_acc = fast_force(fast_pos)
@@ -578,14 +573,20 @@
 
 def solution(mesh):
     both = P(None, ("row", "col"))
-    return jax.shard_map(
-        per_device,
-        mesh=mesh,
-        in_specs=(
-            both, both, P(), P(), P(),
-            P(None, "row", "col", None), P(None, "row", "col", None),
-            P("row", "col", None), P("row", "col", None),
-        ),
-        out_specs=(both, both, P(None, "row", "col", None), P(None, "row", "col", None)),
-        check_vma=False,
-    )
+
+    def run(*args):
+        special = args[0].shape[1] == LANES * mesh.size
+        step = jax.shard_map(
+            per_device if special else general,
+            mesh=mesh,
+            in_specs=(
+                both, both, P(), P(), P(),
+                P(None, "row", "col", None), P(None, "row", "col", None),
+                P("row", "col", None), P("row", "col", None),
+            ),
+            out_specs=(both, both, P(None, "row", "col", None), P(None, "row", "col", None)),
+            check_vma=False,
+        )
+        return step(*args)
+
+    return run

time: 140 us -> 122 us (0.87)
  Pallas kernels: 75.6 us -> 44.7 us
  waiting for transfers between devices: 17.4 us -> 28.5 us
    pallas_call x2 -> x4, Pallas kernels: 50.8 us -> 23 us  [slow(): pl.pallas_call(functools.partial(slow_kernel, first, row0), out_shape=out...]
    all_to_all x7, waiting for transfers between devices: 17.4 us -> 28.3 us  [exchange(): return lax.all_to_all(x, BOTH, 0, 0)]
    pallas_call x1, Pallas kernels: 5.43 us -> 3.23 us  [env_list(): pl.pallas_call(functools.partial(list_kernel, total_cols, cell_rows, cell...]
    unnamed x18 -> x20, local copies, waits for them, and re-layouts: 2.23 us -> 2.95 us
  transfers between devices with their start and end apart: 15 -> 15, of which waited for: 4 -> 6; matrix products, arithmetic and copies ran while one was open for 1% -> 2% of each run, Pallas kernels for 52% -> 34%
where the time goes in v2:
time: 122 us; the launch traced here: 121 us
  Pallas kernels  44.7 us (37%)
  starting transfers between devices  40.6 us (33%)
  waiting for transfers between devices  28.5 us (23%)
  local copies, waits for them, and re-layouts  4.29 us (4%)
  other arithmetic  2.26 us (2%)
    all_to_all x7, waiting for transfers between devices, exchange(): return lax.all_to_all(x, BOTH, 0, 0)  28.3 us
    all_to_all x7, starting transfers between devices, exchange(): return lax.all_to_all(x, BOTH, 0, 0)  28 us
    pallas_call x4, Pallas kernels, slow(): pl.pallas_call(functools.partial(slow_kernel, first, row0), out_shape=out...  23 us
    ppermute x4, starting transfers between devices, with_halo(): after = lax.ppermute(initial, axis, down)  8.77 us
    pallas_call x3, Pallas kernels, fast_step(): pl.pallas_call(fast_step_kernel, out_shape=(sds((count, 3, LANES)), sds((...  8.28 us
    pallas_call x2, Pallas kernels, env(): pl.pallas_call(env_kernel, out_shape=sds((count, 3, LANES)), in_specs=[SM...  4.62 us
    pallas_call x2, Pallas kernels, fast_only(): pl.pallas_call(fast_only_kernel, out_shape=sds((3, LANES)), in_specs=[SME...  4.18 us
    ppermute x4, starting transfers between devices, with_halo(): before = lax.ppermute(last, axis, up)  3.89 us
  transfers between devices with their start and end apart: 15, of which 6 were waited for; matrix products, arithmetic and copies ran while one was open for 2% of the time, Pallas kernels for 34%

profile of v2, /device:TPU:0, one launch (start us, length us, event | category | flops | bytes accessed | tf_op | source)
XLA Modules:
  0.0 121.3 jit_solution(8968541632838200520)
XLA Ops:
  0.6 1.3 %broadcast_in_dim.4 = f32[32,3,128]{2,1,0:T(4,128)} broadcast(f32[3,128]{1,0:T(4,128)} %p_ref.1), dimensions={1,2} | broadcast | bytes 50688 | tf_op jit(solution)/shard_map/broadcast_in_dim | solution.py:396
  1.9 7.3 %all-to-all-start = ((f32[32,3,128]{2,1,0:T(4,128)}), f32[32,3,128]{2,1,0:T(4,128)S(1)}, u32[]{:S(2)}, u32[]{:S(2)}) async-start(f32[32,3,128]{2,1,0:T(4,128)} %broadcast_in_dim.4), calls=%async_computation | async-start | bytes 131072 | tf_op jit(solution)/shard_map/all_to_all | solution.py:376
  10.4 2.4 %collective-permute-start.1 = (f32[2,8,4,128]{3,2,1,0:T(4,128)S(1)}, f32[2,8,4,128]{3,2,1,0:T(4,128)S(1)}, u32[]{:S(2)}, u32[]{:S(2)}) collective-permute-start(f32[2,8,4,128]{3,2,1,0:T(4,128)S(1)} %get-tuple-element.43), channel_id=1, source_target_pairs={{4,0},{8,4},{12,8},{16,12},{20,16},{24,20},{28,24},{0,28},{5,1},{9... | collective-permute-start | bytes 98312 | tf_op jit(solution)/shard_map/ppermute | solution.py:370
  14.5 1.8 %collective-permute-start.2 = (f32[8,2,4,128]{3,2,1,0:T(4,128)S(1)}, f32[8,2,4,128]{3,2,1,0:T(4,128)S(1)}, u32[]{:S(2)}, u32[]{:S(2)}) collective-permute-start(f32[8,2,4,128]{3,2,1,0:T(4,128)S(1)} %get-tuple-element.40), channel_id=1, source_target_pairs={{0,1},{1,2},{2,3},{3,0},{4,5},{5,6},{6,7},{7,4},{8,9},{9,10},{10,1... | collective-permute-start | bytes 98312 | tf_op jit(solution)/shard_map/ppermute | solution.py:369
  16.3 2.0 %collective-permute-start.3 = (f32[8,2,4,128]{3,2,1,0:T(4,128)S(1)}, f32[8,2,4,128]{3,2,1,0:T(4,128)S(1)}, u32[]{:S(2)}, u32[]{:S(2)}) collective-permute-start(f32[8,2,4,128]{3,2,1,0:T(4,128)S(1)} %get-tuple-element.41), channel_id=1, source_target_pairs={{1,0},{2,1},{3,2},{0,3},{5,4},{6,5},{7,6},{4,7},{9,8},{10,9},{11,1... | collective-permute-start | bytes 98312 | tf_op jit(solution)/shard_map/ppermute | solution.py:370
  18.5 3.2 %env_list.1 = (s32[260]{0:T(512)S(1)}, s32[1]{0:T(128)}) custom-call(s32[256]{0:T(256)S(1)} %slice.29.owner_ref, s32[2]{0:T(128)S(1)} %pad_add_fusion.base_ref), custom_call_target="tpu_custom_call" | custom-call | tf_op jit(solution)/shard_map/env_list/pallas_call | solution.py:165
  21.9 0.7 copy-done.3
  22.6 5.8 %slow.5 = (f32[3,2,8,128]{3,2,1,0:T(8,128)S(1)}, f32[3,2,8,128]{3,2,1,0:T(8,128)S(1)}, f32[16,4,128]{2,1,0:T(4,128)S(1)}) custom-call(s32[32,5]{1,0:T(8,128)S(1)} %bitcast.51, f32[8,12,4,128]{3,2,1,0:T(4,128)S(1)} %pad_maximum_fusion.tab_ref, f32[3,4,8,128]{3,2,1,0:T(8,128)S(1)} %copy-done.3), custom_call_target="tpu_custom_call" | custom-call | flops 24903680 | bytes 1000000 | tf_op jit(solution)/shard_map/slow/pallas_call | solution.py:348
  28.3 5.8 %slow.4 = (f32[3,2,8,128]{3,2,1,0:T(8,128)S(1)}, f32[3,2,8,128]{3,2,1,0:T(8,128)S(1)}, f32[16,4,128]{2,1,0:T(4,128)S(1)}) custom-call(s32[32,5]{1,0:T(8,128)S(1)} %bitcast.52, f32[8,12,4,128]{3,2,1,0:T(4,128)S(1)} %pad_maximum_fusion.tab_ref, f32[3,4,8,128]{3,2,1,0:T(8,128)S(1)} %copy-done.3), custom_call_target="tpu_custom_call" | custom-call | flops 24903680 | bytes 1000000 | tf_op jit(solution)/shard_map/slow/pallas_call | solution.py:348
  34.1 2.2 %collective-permute-start.5 = (f32[2,8,4,128]{3,2,1,0:T(4,128)S(1)}, f32[2,8,4,128]{3,2,1,0:T(4,128)S(1)}, u32[]{:S(2)}, u32[]{:S(2)}) collective-permute-start(f32[2,8,4,128]{3,2,1,0:T(4,128)S(1)} %bitcast.50), channel_id=1, source_target_pairs={{4,0},{8,4},{12,8},{16,12},{20,16},{24,20},{28,24},{0,28},{5,1},{9... | collective-permute-start | bytes 98312 | tf_op jit(solution)/shard_map/ppermute | solution.py:370
  37.0 2.3 %env.2 = f32[32,3,128]{2,1,0:T(4,128)} custom-call(s32[260]{0:T(512)S(1)} %get-tuple-element.21.list_ref, s32[1]{0:T(128)} %get-tuple-element.22.count_ref, f32[32,3,128]{2,1,0:T(4,128)S(1)} %all-to-all-done.g_ref, f32[32,4,128]{2,1,0:T(4,128)S(1)} %bitcast.41), custom_call_target="tpu_custom_call" | custom-call | flops 2000000 | bytes 200000 | tf_op jit(solution)/shard_map/env/pallas_call | solution.py:213
  39.3 4.4 %all-to-all-start.1 = ((f32[32,3,128]{2,1,0:T(4,128)}), f32[32,3,128]{2,1,0:T(4,128)S(1)}, u32[]{:S(2)}, u32[]{:S(2)}) async-start(f32[32,3,128]{2,1,0:T(4,128)} %env.2), calls=%async_computation.1 | async-start | bytes 131072 | tf_op jit(solution)/shard_map/all_to_all | solution.py:376
  44.4 2.1 %fast_only.2.f_ref = f32[3,128]{1,0:T(4,128)S(1)} custom-call(s32[1]{0:T(128)} %bitcast.own_ref, f32[32,3,128]{2,1,0:T(4,128)S(1)} %all-to-all-done.g_ref, f32[2,32,128]{2,1,0:T(8,128)S(1)} %add_convert_fusion.cor_ref, f32[32,128]{1,0:T(8,128)S(1)} %bitcast.42, f32[16,128]{1,0:T(8,128)S(1)} %convert_element_type.7.exm_ref), custom_call_target="tpu_custom_call" | custom-call | flops 9961472 | bytes 131072 | tf_op jit(solution)/shard_map/fast_only/pallas_call | solution.py:115
  46.5 4.7 %all-to-all-done.1.e_ref = f32[32,3,128]{2,1,0:T(4,128)S(1)} async-done(((f32[32,3,128]{2,1,0:T(4,128)}), f32[32,3,128]{2,1,0:T(4,128)S(1)}, u32[]{:S(2)}, u32[]{:S(2)}) %all-to-all-start.1) | async-done | bytes 49184 | tf_op jit(solution)/shard_map/all_to_all | solution.py:376
  51.8 2.6 %all-to-all-start.2 = ((f32[32,3,128]{2,1,0:T(4,128)}), f32[32,3,128]{2,1,0:T(4,128)S(1)}, u32[]{:S(2)}, u32[]{:S(2)}) async-start(f32[32,3,128]{2,1,0:T(4,128)} %get-tuple-element.23), calls=%async_computation.2 | async-start | bytes 131072 | tf_op jit(solution)/shard_map/all_to_all | solution.py:376
  54.4 7.5 %all-to-all-done.2.g_ref = f32[32,3,128]{2,1,0:T(4,128)S(1)} async-done(((f32[32,3,128]{2,1,0:T(4,128)}), f32[32,3,128]{2,1,0:T(4,128)S(1)}, u32[]{:S(2)}, u32[]{:S(2)}) %all-to-all-start.2) | async-done | bytes 49184 | tf_op jit(solution)/shard_map/all_to_all | solution.py:376
  61.9 2.8 %fast_step.3 = (f32[32,3,128]{2,1,0:T(4,128)}, f32[3,128]{1,0:T(4,128)}, f32[3,128]{1,0:T(4,128)S(1)}) custom-call(s32[1]{0:T(128)} %bitcast.own_ref, f32[32,3,128]{2,1,0:T(4,128)S(1)} %all-to-all-done.2.g_ref, f32[2,32,128]{2,1,0:T(8,128)S(1)} %add_convert_fusion.cor_ref, f32[32,128]{1,0:T(8,128)S(1)} %bitcast.44, ...), custom_call_target="tpu_custom_call" | custom-call | flops 9961472 | bytes 131072 | tf_op jit(solution)/shard_map/fast_step/pallas_call | solution.py:129
  64.7 2.6 %all-to-all-start.3 = ((f32[32,3,128]{2,1,0:T(4,128)}), f32[32,3,128]{2,1,0:T(4,128)S(1)}, u32[]{:S(2)}, u32[]{:S(2)}) async-start(f32[32,3,128]{2,1,0:T(4,128)} %get-tuple-element.25), calls=%async_computation.3 | async-start | bytes 131072 | tf_op jit(solution)/shard_map/all_to_all | solution.py:376
  67.3 1.7 %collective-permute-start.6 = (f32[8,2,4,128]{3,2,1,0:T(4,128)S(1)}, f32[8,2,4,128]{3,2,1,0:T(4,128)S(1)}, u32[]{:S(2)}, u32[]{:S(2)}) collective-permute-start(f32[8,2,4,128]{3,2,1,0:T(4,128)S(1)} %get-tuple-element.38), channel_id=1, source_target_pairs={{0,1},{1,2},{2,3},{3,0},{4,5},{5,6},{6,7},{7,4},{8,9},{9,10},{10,1... | collective-permute-start | bytes 98312 | tf_op jit(solution)/shard_map/ppermute | solution.py:369
  69.0 2.1 %collective-permute-start.7 = (f32[8,2,4,128]{3,2,1,0:T(4,128)S(1)}, f32[8,2,4,128]{3,2,1,0:T(4,128)S(1)}, u32[]{:S(2)}, u32[]{:S(2)}) collective-permute-start(f32[8,2,4,128]{3,2,1,0:T(4,128)S(1)} %get-tuple-element.39), channel_id=1, source_target_pairs={{1,0},{2,1},{3,2},{0,3},{5,4},{6,5},{7,6},{4,7},{9,8},{10,9},{11,1... | collective-permute-start | bytes 98312 | tf_op jit(solution)/shard_map/ppermute | solution.py:370
  71.2 3.9 %all-to-all-done.3.g_ref = f32[32,3,128]{2,1,0:T(4,128)S(1)} async-done(((f32[32,3,128]{2,1,0:T(4,128)}), f32[32,3,128]{2,1,0:T(4,128)S(1)}, u32[]{:S(2)}, u32[]{:S(2)}) %all-to-all-start.3) | async-done | bytes 49184 | tf_op jit(solution)/shard_map/all_to_all | solution.py:376
  75.0 2.8 %fast_step.4 = (f32[32,3,128]{2,1,0:T(4,128)}, f32[3,128]{1,0:T(4,128)}, f32[3,128]{1,0:T(4,128)S(1)}) custom-call(s32[1]{0:T(128)} %bitcast.own_ref, f32[32,3,128]{2,1,0:T(4,128)S(1)} %all-to-all-done.3.g_ref, f32[2,32,128]{2,1,0:T(8,128)S(1)} %add_convert_fusion.cor_ref, f32[32,128]{1,0:T(8,128)S(1)} %bitcast.45, ...), custom_call_target="tpu_custom_call" | custom-call | flops 9961472 | bytes 131072 | tf_op jit(solution)/shard_map/fast_step/pallas_call | solution.py:129
  77.8 2.6 %all-to-all-start.4 = ((f32[32,3,128]{2,1,0:T(4,128)}), f32[32,3,128]{2,1,0:T(4,128)S(1)}, u32[]{:S(2)}, u32[]{:S(2)}) async-start(f32[32,3,128]{2,1,0:T(4,128)} %get-tuple-element.27), calls=%async_computation.4 | async-start | bytes 131072 | tf_op jit(solution)/shard_map/all_to_all | solution.py:376
  80.4 7.5 %all-to-all-done.4.g_ref = f32[32,3,128]{2,1,0:T(4,128)S(1)} async-done(((f32[32,3,128]{2,1,0:T(4,128)}), f32[32,3,128]{2,1,0:T(4,128)S(1)}, u32[]{:S(2)}, u32[]{:S(2)}) %all-to-all-start.4) | async-done | bytes 49184 | tf_op jit(solution)/shard_map/all_to_all | solution.py:376
  87.9 2.8 %fast_step.5 = (f32[32,3,128]{2,1,0:T(4,128)}, f32[3,128]{1,0:T(4,128)}, f32[3,128]{1,0:T(4,128)S(1)}) custom-call(s32[1]{0:T(128)} %bitcast.own_ref, f32[32,3,128]{2,1,0:T(4,128)S(1)} %all-to-all-done.4.g_ref, f32[2,32,128]{2,1,0:T(8,128)S(1)} %add_convert_fusion.cor_ref, f32[32,128]{1,0:T(8,128)S(1)} %bitcast.46, ...), custom_call_target="tpu_custom_call" | custom-call | flops 9961472 | bytes 131072 | tf_op jit(solution)/shard_map/fast_step/pallas_call | solution.py:129
  90.6 2.6 %all-to-all-start.5 = ((f32[32,3,128]{2,1,0:T(4,128)}), f32[32,3,128]{2,1,0:T(4,128)S(1)}, u32[]{:S(2)}, u32[]{:S(2)}) async-start(f32[32,3,128]{2,1,0:T(4,128)} %get-tuple-element.30), calls=%async_computation.5 | async-start | bytes 131072 | tf_op jit(solution)/shard_map/all_to_all | solution.py:376
  93.3 5.7 %slow.7 = f32[3,2,8,128]{3,2,1,0:T(8,128)S(1)} custom-call(s32[32,5]{1,0:T(8,128)S(1)} %bitcast.53, f32[8,12,4,128]{3,2,1,0:T(4,128)S(1)} %pad_maximum_fusion.1.tab_ref, f32[3,4,8,128]{3,2,1,0:T(8,128)S(1)} %constant_dynamic-update-slice_fusion.2.vel_ref), custom_call_target="tpu_custom_call" | custom-call | flops 24903680 | bytes 1000000 | tf_op jit(solution)/shard_map/slow/pallas_call | solution.py:348
  99.0 5.7 %slow.6 = f32[3,2,8,128]{3,2,1,0:T(8,128)S(1)} custom-call(s32[32,5]{1,0:T(8,128)S(1)} %bitcast.54, f32[8,12,4,128]{3,2,1,0:T(4,128)S(1)} %pad_maximum_fusion.1.tab_ref, f32[3,4,8,128]{3,2,1,0:T(8,128)S(1)} %constant_dynamic-update-slice_fusion.2.vel_ref), custom_call_target="tpu_custom_call" | custom-call | flops 24903680 | bytes 1000000 | tf_op jit(solution)/shard_map/slow/pallas_call | solution.py:348
  104.8 2.3 %env.3 = f32[32,3,128]{2,1,0:T(4,128)} custom-call(s32[260]{0:T(512)S(1)} %get-tuple-element.21.list_ref, s32[1]{0:T(128)} %get-tuple-element.22.count_ref, f32[32,3,128]{2,1,0:T(4,128)S(1)} %all-to-all-done.5.g_ref, f32[32,4,128]{2,1,0:T(4,128)S(1)} %constant_dynamic-update-slice_fusion.cells_ref), custom_call_target="tpu_custom_call" | custom-call | flops 2000000 | bytes 200000 | tf_op jit(solution)/shard_map/env/pallas_call | solution.py:213
  107.1 6.0 %all-to-all-start.6 = ((f32[32,3,128]{2,1,0:T(4,128)}), f32[32,3,128]{2,1,0:T(4,128)S(1)}, u32[]{:S(2)}, u32[]{:S(2)}) async-start(f32[32,3,128]{2,1,0:T(4,128)} %env.3), calls=%async_computation.6 | async-start | bytes 131072 | tf_op jit(solution)/shard_map/all_to_all | solution.py:376
  113.8 2.1 %fast_only.3.f_ref = f32[3,128]{1,0:T(4,128)S(1)} custom-call(s32[1]{0:T(128)} %bitcast.own_ref, f32[32,3,128]{2,1,0:T(4,128)S(1)} %all-to-all-done.5.g_ref, f32[2,32,128]{2,1,0:T(8,128)S(1)} %add_convert_fusion.cor_ref, f32[32,128]{1,0:T(8,128)S(1)} %bitcast.47, f32[16,128]{1,0:T(8,128)S(1)} %convert_element_type.7.exm_ref), custom_call_target="tpu_custom_call" | custom-call | flops 9961472 | bytes 131072 | tf_op jit(solution)/shard_map/fast_only/pallas_call | solution.py:115
  115.9 4.8 %all-to-all-done.6.e_ref = f32[32,3,128]{2,1,0:T(4,128)S(1)} async-done(((f32[32,3,128]{2,1,0:T(4,128)}), f32[32,3,128]{2,1,0:T(4,128)S(1)}, u32[]{:S(2)}, u32[]{:S(2)}) %all-to-all-start.6) | async-done | bytes 49184 | tf_op jit(solution)/shard_map/all_to_all | solution.py:376
  (51 shorter events, 6.3 us)
Async XLA Ops:
  1.9 7.3 %copy-start.5 = (f32[3,4,8,128]{3,2,1,0:T(8,128)S(1)}, f32[3,4,8,128]{3,2,1,0:T(8,128)}, u32[]{:S(2)}) copy-start(f32[3,4,8,128]{3,2,1,0:T(8,128)} %param.14) | copy-start | bytes 147460
  1.9 35.0 %all-to-all-start = ((f32[32,3,128]{2,1,0:T(4,128)}), f32[32,3,128]{2,1,0:T(4,128)S(1)}, u32[]{:S(2)}, u32[]{:S(2)}) async-start(f32[32,3,128]{2,1,0:T(4,128)} %broadcast_in_dim.4), calls=%async_computation | async-start | bytes 131072 | tf_op jit(solution)/shard_map/all_to_all | solution.py:376
  9.3 0.7 copy-start.4
  10.1 4.4 %collective-permute-start = (f32[2,8,4,128]{3,2,1,0:T(4,128)S(1)}, f32[2,8,4,128]{3,2,1,0:T(4,128)S(1)}, u32[]{:S(2)}, u32[]{:S(2)}) collective-permute-start(f32[2,8,4,128]{3,2,1,0:T(4,128)S(1)} %get-tuple-element.42), channel_id=1, source_target_pairs={{0,4},{4,8},{8,12},{12,16},{16,20},{20,24},{24,28},{28,0},{1,5},{5... | collective-permute-start | bytes 98312 | tf_op jit(solution)/shard_map/ppermute | solution.py:369
  10.4 4.1 %collective-permute-start.1 = (f32[2,8,4,128]{3,2,1,0:T(4,128)S(1)}, f32[2,8,4,128]{3,2,1,0:T(4,128)S(1)}, u32[]{:S(2)}, u32[]{:S(2)}) collective-permute-start(f32[2,8,4,128]{3,2,1,0:T(4,128)S(1)} %get-tuple-element.43), channel_id=1, source_target_pairs={{4,0},{8,4},{12,8},{16,12},{20,16},{24,20},{28,24},{0,28},{5,1},{9... | collective-permute-start | bytes 98312 | tf_op jit(solution)/shard_map/ppermute | solution.py:370
  12.8 0.7 copy-start.6
  14.4 4.0 %copy-start.7 = (s32[4,8,5]{1,0,2:T(4,128)S(1)}, s32[4,8,5]{1,0,2:T(4,128)}, u32[]{:S(2)}) copy-start(s32[4,8,5]{1,0,2:T(4,128)} %param.17) | copy-start | bytes 1924
  14.5 7.3 %collective-permute-start.2 = (f32[8,2,4,128]{3,2,1,0:T(4,128)S(1)}, f32[8,2,4,128]{3,2,1,0:T(4,128)S(1)}, u32[]{:S(2)}, u32[]{:S(2)}) collective-permute-start(f32[8,2,4,128]{3,2,1,0:T(4,128)S(1)} %get-tuple-element.40), channel_id=1, source_target_pairs={{0,1},{1,2},{2,3},{3,0},{4,5},{5,6},{6,7},{7,4},{8,9},{9,10},{10,1... | collective-permute-start | bytes 98312 | tf_op jit(solution)/shard_map/ppermute | solution.py:369
  16.3 5.5 %collective-permute-start.3 = (f32[8,2,4,128]{3,2,1,0:T(4,128)S(1)}, f32[8,2,4,128]{3,2,1,0:T(4,128)S(1)}, u32[]{:S(2)}, u32[]{:S(2)}) collective-permute-start(f32[8,2,4,128]{3,2,1,0:T(4,128)S(1)} %get-tuple-element.41), channel_id=1, source_target_pairs={{1,0},{2,1},{3,2},{0,3},{5,4},{6,5},{7,6},{4,7},{9,8},{10,9},{11,1... | collective-permute-start | bytes 98312 | tf_op jit(solution)/shard_map/ppermute | solution.py:370
  21.8 0.8 copy-start.3
  34.1 33.1 %collective-permute-start.5 = (f32[2,8,4,128]{3,2,1,0:T(4,128)S(1)}, f32[2,8,4,128]{3,2,1,0:T(4,128)S(1)}, u32[]{:S(2)}, u32[]{:S(2)}) collective-permute-start(f32[2,8,4,128]{3,2,1,0:T(4,128)S(1)} %bitcast.50), channel_id=1, source_target_pairs={{4,0},{8,4},{12,8},{16,12},{20,16},{24,20},{28,24},{0,28},{5,1},{9... | collective-permute-start | bytes 98312 | tf_op jit(solution)/shard_map/ppermute | solution.py:370
  36.3 30.9 %collective-permute-start.4 = (f32[2,8,4,128]{3,2,1,0:T(4,128)S(1)}, f32[2,8,4,128]{3,2,1,0:T(4,128)S(1)}, u32[]{:S(2)}, u32[]{:S(2)}) collective-permute-start(f32[2,8,4,128]{3,2,1,0:T(4,128)S(1)} %bitcast.49), channel_id=1, source_target_pairs={{0,4},{4,8},{8,12},{12,16},{16,20},{20,24},{24,28},{28,0},{1,5},{5... | collective-permute-start | bytes 98312 | tf_op jit(solution)/shard_map/ppermute | solution.py:369
  39.3 11.9 %all-to-all-start.1 = ((f32[32,3,128]{2,1,0:T(4,128)}), f32[32,3,128]{2,1,0:T(4,128)S(1)}, u32[]{:S(2)}, u32[]{:S(2)}) async-start(f32[32,3,128]{2,1,0:T(4,128)} %env.2), calls=%async_computation.1 | async-start | bytes 131072 | tf_op jit(solution)/shard_map/all_to_all | solution.py:376
  43.6 0.7 copy-start
  44.4 6.8 %copy-start.1 = (f32[3,128]{1,0:T(4,128)S(1)}, f32[3,128]{1,0:T(4,128)}, u32[]{:S(2)}) copy-start(f32[3,128]{1,0:T(4,128)} %p_ref.1) | copy-start | bytes 4612
  44.4 6.8 %copy-start.2 = (f32[3,128]{1,0:T(4,128)S(1)}, f32[3,128]{1,0:T(4,128)}, u32[]{:S(2)}) copy-start(f32[3,128]{1,0:T(4,128)} %v_ref.1) | copy-start | bytes 4612
  51.8 10.1 %all-to-all-start.2 = ((f32[32,3,128]{2,1,0:T(4,128)}), f32[32,3,128]{2,1,0:T(4,128)S(1)}, u32[]{:S(2)}, u32[]{:S(2)}) async-start(f32[32,3,128]{2,1,0:T(4,128)} %get-tuple-element.23), calls=%async_computation.2 | async-start | bytes 131072 | tf_op jit(solution)/shard_map/all_to_all | solution.py:376
  64.7 10.4 %all-to-all-start.3 = ((f32[32,3,128]{2,1,0:T(4,128)}), f32[32,3,128]{2,1,0:T(4,128)S(1)}, u32[]{:S(2)}, u32[]{:S(2)}) async-start(f32[32,3,128]{2,1,0:T(4,128)} %get-tuple-element.25), calls=%async_computation.3 | async-start | bytes 131072 | tf_op jit(solution)/shard_map/all_to_all | solution.py:376
  67.3 25.9 %collective-permute-start.6 = (f32[8,2,4,128]{3,2,1,0:T(4,128)S(1)}, f32[8,2,4,128]{3,2,1,0:T(4,128)S(1)}, u32[]{:S(2)}, u32[]{:S(2)}) collective-permute-start(f32[8,2,4,128]{3,2,1,0:T(4,128)S(1)} %get-tuple-element.38), channel_id=1, source_target_pairs={{0,1},{1,2},{2,3},{3,0},{4,5},{5,6},{6,7},{7,4},{8,9},{9,10},{10,1... | collective-permute-start | bytes 98312 | tf_op jit(solution)/shard_map/ppermute | solution.py:369
  69.0 24.2 %collective-permute-start.7 = (f32[8,2,4,128]{3,2,1,0:T(4,128)S(1)}, f32[8,2,4,128]{3,2,1,0:T(4,128)S(1)}, u32[]{:S(2)}, u32[]{:S(2)}) collective-permute-start(f32[8,2,4,128]{3,2,1,0:T(4,128)S(1)} %get-tuple-element.39), channel_id=1, source_target_pairs={{1,0},{2,1},{3,2},{0,3},{5,4},{6,5},{7,6},{4,7},{9,8},{10,9},{11,1... | collective-permute-start | bytes 98312 | tf_op jit(solution)/shard_map/ppermute | solution.py:370
  77.8 10.1 %all-to-all-start.4 = ((f32[32,3,128]{2,1,0:T(4,128)}), f32[32,3,128]{2,1,0:T(4,128)S(1)}, u32[]{:S(2)}, u32[]{:S(2)}) async-start(f32[32,3,128]{2,1,0:T(4,128)} %get-tuple-element.27), calls=%async_computation.4 | async-start | bytes 131072 | tf_op jit(solution)/shard_map/all_to_all | solution.py:376
  90.6 14.1 %all-to-all-start.5 = ((f32[32,3,128]{2,1,0:T(4,128)}), f32[32,3,128]{2,1,0:T(4,128)S(1)}, u32[]{:S(2)}, u32[]{:S(2)}) async-start(f32[32,3,128]{2,1,0:T(4,128)} %get-tuple-element.30), calls=%async_computation.5 | async-start | bytes 131072 | tf_op jit(solution)/shard_map/all_to_all | solution.py:376
  107.1 13.5 %all-to-all-start.6 = ((f32[32,3,128]{2,1,0:T(4,128)}), f32[32,3,128]{2,1,0:T(4,128)S(1)}, u32[]{:S(2)}, u32[]{:S(2)}) async-start(f32[32,3,128]{2,1,0:T(4,128)} %env.3), calls=%async_computation.6 | async-start | bytes 131072 | tf_op jit(solution)/shard_map/all_to_all | solution.py:376

commit v3 on v2

--- a/solution.py
+++ b/solution.py
@@ -20,6 +20,7 @@
 
 BOTH = ("row", "col")
 F32 = jnp.float32
+BF16 = jnp.bfloat16
 LANES = 128
 ENV_UNROLL = 4
 VMEM = pl.BlockSpec(memory_space=pltpu.VMEM)
@@ -143,16 +144,26 @@
 
     unroll = 8
 
+    power = total_cols & (total_cols - 1) == 0 and cell_cols & (cell_cols - 1) == 0
+
     def body(j, n):
+        found = []
         for u in range(unroll):
-            i = j * unroll + u
-            cell = owner_ref[i]
-            r = lax.div(cell, total_cols)
-            c = cell - r * total_cols - col0
-            r = r - row0
+            cell = owner_ref[j * unroll + u]
+            if power:
+                r = lax.shift_right_logical(cell, total_cols.bit_length() - 1) - row0
+                c = (cell & (total_cols - 1)) - col0
+                local = lax.shift_left(r, cell_cols.bit_length() - 1) + c
+            else:
+                r = lax.div(cell, total_cols) - row0
+                c = lax.rem(cell, total_cols) - col0
+                local = r * cell_cols + c
             sign = r | (cell_rows - 1 - r) | c | (cell_cols - 1 - c)
-            list_ref[n] = i + (r * cell_cols + c) * GROUPS
-            n = n + (1 + lax.shift_right_arithmetic(sign, 31))
+            entry = j * unroll + (u + lax.shift_left(local, GROUPS.bit_length() - 1))
+            found.append((entry, 1 + lax.shift_right_arithmetic(sign, 31)))
+        for entry, inside in found:
+            list_ref[n] = entry
+            n = n + inside
         return n
 
     n = lax.fori_loop(0, GROUPS // unroll, body, jnp.int32(0))
@@ -188,7 +199,7 @@
             group = entry & (GROUPS - 1)
             h = lax.shift_right_logical(group, LANES.bit_length() - 1)
             here = (lane == (group & (LANES - 1))) & (entry >= 0)
-            cell = cells_ref[jnp.maximum(lax.div(entry, GROUPS), 0)]
+            cell = cells_ref[jnp.maximum(lax.shift_right_arithmetic(entry, GROUPS.bit_length() - 1), 0)]
             d = []
             for c in range(3):
                 x = jnp.sum(jnp.where(here, planes[c, h], 0.0), axis=1, keepdims=True)
@@ -269,52 +280,80 @@
     )(own, e, f, q, v)
 
 
+def split3(x):
+    hi = x.astype(BF16).astype(F32)
+    rest = x - hi
+    mid = rest.astype(BF16).astype(F32)
+    return hi, mid, rest - mid
+
+
 def slow_kernel(first, row0, nb_ref, tab_ref, vel_ref, *refs):
     if first:
-        vel_out, pos_out, cell_out, cols_a, cols_b, sums_a, sums_b = refs
+        vel_out, pos_out, cell_out, *scratch = refs
     else:
-        vel_out, cols_a, cols_b, sums_a, sums_b = refs
+        vel_out, *scratch = refs
+    bufs = [tuple(scratch[0:4]), tuple(scratch[4:8])]
     cell_rows, cell_cols = vel_out.shape[1], vel_out.shape[2]
     slots = nb_ref.shape[1]
     count = cell_rows * cell_cols
+    row8 = lax.broadcasted_iota(jnp.int32, (8, CELL), 0)
 
     def place(n):
         return lax.div(n, cell_cols), lax.rem(n, cell_cols)
 
-    def spread(n, cols):
+    def load8(r, c):
+        t = tab_ref[r, c]
+        return jnp.concatenate([t, jnp.zeros_like(t)], axis=0)
+
+    def distances(n, buf):
+        feat, ys, dist, _ = buf
         r, c = place(n)
-        t = tab_ref[r + (row0 + 2), c + 2]
-        for x in range(3):
-            cols[x] = jnp.transpose(jnp.broadcast_to(t[x : x + 1], (CELL, CELL)))
-
-    def pairs(n, cols, sums):
-        r, c = place(n)
-        others = []
+        x = jnp.where(row8 < 3, load8(r + (row0 + 2), c + 2), 0.0)
+        norm = jnp.sum(x * x, axis=0, keepdims=True)
+        hi, mid, lo = split3(jnp.where(row8 == 3, norm, jnp.where(row8 == 4, 1.0, x)))
+        left = jnp.transpose(jnp.concatenate([hi, hi, mid, hi, mid, lo], axis=0)).astype(BF16)
         for k in range(slots):
             o = nb_ref[n + row0 * cell_cols, k]
             dr, dc = lax.div(o, 5), lax.rem(o, 5)
-            t = tab_ref[r + (dr + row0), c + dc]
-            rows = [t[0:1] + (dr - 2).astype(F32), t[1:2] + (dc - 2).astype(F32), t[2:3], t[3:4]]
-            others.append([jnp.broadcast_to(y, (8, CELL)) for y in rows])
-        for g in range(CELL // 8):
-            at = slice(8 * g, 8 * g + 8)
-            a = [cols[x, at, :] for x in range(3)]
-            acc = None
-            for y in others:
-                d = [a[x] - y[x] for x in range(3)]
-                i = lax.rsqrt(d[0] * d[0] + d[1] * d[1] + d[2] * d[2] + 0.5)
-                w = (y[3] * i) * (i * i)
-                f = [w * d[x] for x in range(3)]
-                acc = f if acc is None else [acc[x] + f[x] for x in range(3)]
-            for x in range(3):
-                sums[x, at, :] = acc[x]
-
-    def finish(n, sums):
+            y = load8(r + (dr + row0), c + dc)
+            y = y + jnp.where(
+                row8 == 0, (dr - 2).astype(F32), jnp.where(row8 == 1, (dc - 2).astype(F32), 0.0)
+            )
+            ys[8 * k : 8 * k + 8] = y
+            y = jnp.where(row8 < 3, y, 0.0)
+            norm = jnp.sum(y * y, axis=0, keepdims=True) + 0.5
+            hi, mid, lo = split3(
+                jnp.where(row8 == 3, 1.0, jnp.where(row8 == 4, norm, -2.0 * y))
+            )
+            feat[:, CELL * k : CELL * (k + 1)] = jnp.concatenate(
+                [hi, mid, hi, lo, mid, hi], axis=0
+            ).astype(BF16)
+        dist[...] = jnp.dot(left, feat[...], preferred_element_type=F32)
+
+    def pairs(buf):
+        _, ys, dist, sums = buf
+        for g in range(0, CELL // 8, 2):
+            at = [slice(8 * (g + h), 8 * (g + h) + 8) for h in range(2)]
+            acc = [None, None]
+            for k in range(slots):
+                y = [jnp.broadcast_to(ys[8 * k + x : 8 * k + x + 1], (8, CELL)) for x in range(4)]
+                for h in range(2):
+                    i = lax.rsqrt(dist[at[h], CELL * k : CELL * (k + 1)])
+                    w = (y[3] * i) * (i * i)
+                    f = [w * y[0], w * y[1], w * y[2], w]
+                    acc[h] = f if acc[h] is None else [acc[h][x] + f[x] for x in range(4)]
+            for h in range(2):
+                for x in range(4):
+                    sums[x, at[h], :] = acc[h][x]
+
+    def finish(n, buf):
+        sums = buf[3]
         r, c = place(n)
         t = tab_ref[r + (row0 + 2), c + 2]
+        total = [jnp.sum(jnp.transpose(sums[x]), axis=0, keepdims=True) for x in range(4)]
         scale = slow_coupling * t[3:4]
         for x in range(3):
-            f = scale * jnp.sum(jnp.transpose(sums[x]), axis=0, keepdims=True)
+            f = scale * (t[x : x + 1] * total[3] - total[x])
             v = vel_ref[x, r + row0, pl.ds(c, 1), :] + half_outer * f
             vel_out[x, r, pl.ds(c, 1), :] = v
             if first:
@@ -324,36 +363,42 @@
         if first:
             cell_out[n, 3:4, :] = t[3:4]
 
-    spread(0, cols_a)
+    distances(0, bufs[0])
 
     def body(i, carry):
         n = 2 * i
-        spread(n + 1, cols_b)
-        pairs(n, cols_a, sums_a)
-        finish(jnp.maximum(n - 1, 0), sums_b)
-        spread(jnp.minimum(n + 2, count - 1), cols_a)
-        pairs(n + 1, cols_b, sums_b)
-        finish(n, sums_a)
+        distances(n + 1, bufs[1])
+        pairs(bufs[0])
+        finish(jnp.maximum(n - 1, 0), bufs[1])
+        distances(jnp.minimum(n + 2, count - 1), bufs[0])
+        pairs(bufs[1])
+        finish(n, bufs[0])
         return carry
 
     lax.fori_loop(0, count // 2, body, 0)
-    finish(count - 1, sums_b)
+    finish(count - 1, bufs[1])
 
 
 def slow(first, row0, rows, nb, tab, vel):
     shape = (3, rows) + vel.shape[2:]
     own = rows * vel.shape[2]
+    slots = nb.shape[1]
     out = (sds(shape), sds(shape), sds((own, 4, CELL))) if first else sds(shape)
-    pairs = own * nb.shape[1] * CELL * CELL
+    pairs = own * slots * CELL * CELL
     return pl.pallas_call(
         functools.partial(slow_kernel, first, row0),
         out_shape=out,
         in_specs=[SMEM, VMEM, VMEM],
         out_specs=(VMEM,) * 3 if first else VMEM,
-        scratch_shapes=[pltpu.VMEM((3, CELL, CELL), F32)] * 4,
-        compiler_params=pltpu.CompilerParams(vmem_limit_bytes=3 << 20),
+        scratch_shapes=[
+            pltpu.VMEM((48, slots * CELL), BF16),
+            pltpu.VMEM((8 * slots, CELL), F32),
+            pltpu.VMEM((CELL, slots * CELL), F32),
+            pltpu.VMEM((4, CELL, CELL), F32),
+        ] * 2,
+        compiler_params=pltpu.CompilerParams(vmem_limit_bytes=4 << 20),
         cost_estimate=pl.CostEstimate(
-            flops=19 * pairs, transcendentals=pairs, bytes_accessed=1_000_000
+            flops=10 * pairs, transcendentals=pairs, bytes_accessed=1_000_000
         ),
         name="slow",
     )(nb, tab, vel)

time: 122 us -> 116 us (0.951)
  Pallas kernels: 44.7 us -> 38.6 us
    pallas_call x4, Pallas kernels: 23 us -> 17 us  [slow(): pl.pallas_call(functools.partial(slow_kernel, first, row0), out_shape=out...]
  transfers between devices with their start and end apart: 15 -> 15, of which waited for: 6 -> 6; matrix products, arithmetic and copies ran while one was open for 2% -> 2% of each run, Pallas kernels for 34% -> 31%
where the time goes in v3:
time: 116 us; the launch traced here: 115 us
  starting transfers between devices  40.6 us (35%)
  Pallas kernels  38.6 us (33%)
  waiting for transfers between devices  28.5 us (25%)
  local copies, waits for them, and re-layouts  4.29 us (4%)
  other arithmetic  2.26 us (2%)
    all_to_all x7, waiting for transfers between devices, exchange(): return lax.all_to_all(x, BOTH, 0, 0)  28.3 us
    all_to_all x7, starting transfers between devices, exchange(): return lax.all_to_all(x, BOTH, 0, 0)  28 us
    pallas_call x4, Pallas kernels, slow(): pl.pallas_call(functools.partial(slow_kernel, first, row0), out_shape=out...  17 us
    ppermute x4, starting transfers between devices, with_halo(): after = lax.ppermute(initial, axis, down)  8.77 us
    pallas_call x3, Pallas kernels, fast_step(): pl.pallas_call(fast_step_kernel, out_shape=(sds((count, 3, LANES)), sds((...  8.28 us
    pallas_call x2, Pallas kernels, env(): pl.pallas_call(env_kernel, out_shape=sds((count, 3, LANES)), in_specs=[SM...  4.62 us
    pallas_call x2, Pallas kernels, fast_only(): pl.pallas_call(fast_only_kernel, out_shape=sds((3, LANES)), in_specs=[SME...  4.18 us
    ppermute x4, starting transfers between devices, with_halo(): before = lax.ppermute(last, axis, up)  3.89 us
  transfers between devices with their start and end apart: 15, of which 6 were waited for; matrix products, arithmetic and copies ran while one was open for 2% of the time, Pallas kernels for 31%

profile of v3, /device:TPU:0, one launch (start us, length us, event | category | flops | bytes accessed | tf_op | source)
XLA Modules:
  0.0 115.2 jit_solution(3311659372531559434)
XLA Ops:
  0.6 1.3 %broadcast_in_dim.4 = f32[32,3,128]{2,1,0:T(4,128)} broadcast(f32[3,128]{1,0:T(4,128)} %p_ref.1), dimensions={1,2} | broadcast | bytes 50688 | tf_op jit(solution)/shard_map/broadcast_in_dim | solution.py:441
  1.9 7.3 %all-to-all-start = ((f32[32,3,128]{2,1,0:T(4,128)}), f32[32,3,128]{2,1,0:T(4,128)S(1)}, u32[]{:S(2)}, u32[]{:S(2)}) async-start(f32[32,3,128]{2,1,0:T(4,128)} %broadcast_in_dim.4), calls=%async_computation | async-start | bytes 131072 | tf_op jit(solution)/shard_map/all_to_all | solution.py:421
  10.4 2.4 %collective-permute-start.1 = (f32[2,8,4,128]{3,2,1,0:T(4,128)S(1)}, f32[2,8,4,128]{3,2,1,0:T(4,128)S(1)}, u32[]{:S(2)}, u32[]{:S(2)}) collective-permute-start(f32[2,8,4,128]{3,2,1,0:T(4,128)S(1)} %get-tuple-element.43), channel_id=1, source_target_pairs={{4,0},{8,4},{12,8},{16,12},{20,16},{24,20},{28,24},{0,28},{5,1},{9... | collective-permute-start | bytes 98312 | tf_op jit(solution)/shard_map/ppermute | solution.py:415
  14.5 1.8 %collective-permute-start.2 = (f32[8,2,4,128]{3,2,1,0:T(4,128)S(1)}, f32[8,2,4,128]{3,2,1,0:T(4,128)S(1)}, u32[]{:S(2)}, u32[]{:S(2)}) collective-permute-start(f32[8,2,4,128]{3,2,1,0:T(4,128)S(1)} %get-tuple-element.40), channel_id=1, source_target_pairs={{0,1},{1,2},{2,3},{3,0},{4,5},{5,6},{6,7},{7,4},{8,9},{9,10},{10,1... | collective-permute-start | bytes 98312 | tf_op jit(solution)/shard_map/ppermute | solution.py:414
  16.3 2.0 %collective-permute-start.3 = (f32[8,2,4,128]{3,2,1,0:T(4,128)S(1)}, f32[8,2,4,128]{3,2,1,0:T(4,128)S(1)}, u32[]{:S(2)}, u32[]{:S(2)}) collective-permute-start(f32[8,2,4,128]{3,2,1,0:T(4,128)S(1)} %get-tuple-element.41), channel_id=1, source_target_pairs={{1,0},{2,1},{3,2},{0,3},{5,4},{6,5},{7,6},{4,7},{9,8},{10,9},{11,1... | collective-permute-start | bytes 98312 | tf_op jit(solution)/shard_map/ppermute | solution.py:415
  18.5 3.2 %env_list.1 = (s32[260]{0:T(512)S(1)}, s32[1]{0:T(128)}) custom-call(s32[256]{0:T(256)S(1)} %slice.29.owner_ref, s32[2]{0:T(128)S(1)} %pad_add_fusion.base_ref), custom_call_target="tpu_custom_call" | custom-call | tf_op jit(solution)/shard_map/env_list/pallas_call | solution.py:176
  21.9 0.7 copy-done.3
  22.6 4.3 %slow.5 = (f32[3,2,8,128]{3,2,1,0:T(8,128)S(1)}, f32[3,2,8,128]{3,2,1,0:T(8,128)S(1)}, f32[16,4,128]{2,1,0:T(4,128)S(1)}) custom-call(s32[32,5]{1,0:T(8,128)S(1)} %bitcast.51, f32[8,12,4,128]{3,2,1,0:T(4,128)S(1)} %pad_maximum_fusion.tab_ref, f32[3,4,8,128]{3,2,1,0:T(8,128)S(1)} %copy-done.3), custom_call_target="tpu_custom_call" | custom-call | flops 13107200 | bytes 1000000 | tf_op jit(solution)/shard_map/slow/pallas_call | solution.py:388
  26.9 4.2 %slow.4 = (f32[3,2,8,128]{3,2,1,0:T(8,128)S(1)}, f32[3,2,8,128]{3,2,1,0:T(8,128)S(1)}, f32[16,4,128]{2,1,0:T(4,128)S(1)}) custom-call(s32[32,5]{1,0:T(8,128)S(1)} %bitcast.52, f32[8,12,4,128]{3,2,1,0:T(4,128)S(1)} %pad_maximum_fusion.tab_ref, f32[3,4,8,128]{3,2,1,0:T(8,128)S(1)} %copy-done.3), custom_call_target="tpu_custom_call" | custom-call | flops 13107200 | bytes 1000000 | tf_op jit(solution)/shard_map/slow/pallas_call | solution.py:388
  31.1 2.2 %collective-permute-start.5 = (f32[2,8,4,128]{3,2,1,0:T(4,128)S(1)}, f32[2,8,4,128]{3,2,1,0:T(4,128)S(1)}, u32[]{:S(2)}, u32[]{:S(2)}) collective-permute-start(f32[2,8,4,128]{3,2,1,0:T(4,128)S(1)} %bitcast.50), channel_id=1, source_target_pairs={{4,0},{8,4},{12,8},{16,12},{20,16},{24,20},{28,24},{0,28},{5,1},{9... | collective-permute-start | bytes 98312 | tf_op jit(solution)/shard_map/ppermute | solution.py:415
  34.0 2.3 %env.2 = f32[32,3,128]{2,1,0:T(4,128)} custom-call(s32[260]{0:T(512)S(1)} %get-tuple-element.21.list_ref, s32[1]{0:T(128)} %get-tuple-element.22.count_ref, f32[32,3,128]{2,1,0:T(4,128)S(1)} %all-to-all-done.g_ref, f32[32,4,128]{2,1,0:T(4,128)S(1)} %bitcast.41), custom_call_target="tpu_custom_call" | custom-call | flops 2000000 | bytes 200000 | tf_op jit(solution)/shard_map/env/pallas_call | solution.py:224
  36.3 4.4 %all-to-all-start.1 = ((f32[32,3,128]{2,1,0:T(4,128)}), f32[32,3,128]{2,1,0:T(4,128)S(1)}, u32[]{:S(2)}, u32[]{:S(2)}) async-start(f32[32,3,128]{2,1,0:T(4,128)} %env.2), calls=%async_computation.1 | async-start | bytes 131072 | tf_op jit(solution)/shard_map/all_to_all | solution.py:421
  41.4 2.1 %fast_only.2.f_ref = f32[3,128]{1,0:T(4,128)S(1)} custom-call(s32[1]{0:T(128)} %bitcast.own_ref, f32[32,3,128]{2,1,0:T(4,128)S(1)} %all-to-all-done.g_ref, f32[2,32,128]{2,1,0:T(8,128)S(1)} %add_convert_fusion.cor_ref, f32[32,128]{1,0:T(8,128)S(1)} %bitcast.42, f32[16,128]{1,0:T(8,128)S(1)} %convert_element_type.7.exm_ref), custom_call_target="tpu_custom_call" | custom-call | flops 9961472 | bytes 131072 | tf_op jit(solution)/shard_map/fast_only/pallas_call | solution.py:116
  43.5 4.7 %all-to-all-done.1.e_ref = f32[32,3,128]{2,1,0:T(4,128)S(1)} async-done(((f32[32,3,128]{2,1,0:T(4,128)}), f32[32,3,128]{2,1,0:T(4,128)S(1)}, u32[]{:S(2)}, u32[]{:S(2)}) %all-to-all-start.1) | async-done | bytes 49184 | tf_op jit(solution)/shard_map/all_to_all | solution.py:421
  48.8 2.6 %all-to-all-start.2 = ((f32[32,3,128]{2,1,0:T(4,128)}), f32[32,3,128]{2,1,0:T(4,128)S(1)}, u32[]{:S(2)}, u32[]{:S(2)}) async-start(f32[32,3,128]{2,1,0:T(4,128)} %get-tuple-element.23), calls=%async_computation.2 | async-start | bytes 131072 | tf_op jit(solution)/shard_map/all_to_all | solution.py:421
  51.4 7.5 %all-to-all-done.2.g_ref = f32[32,3,128]{2,1,0:T(4,128)S(1)} async-done(((f32[32,3,128]{2,1,0:T(4,128)}), f32[32,3,128]{2,1,0:T(4,128)S(1)}, u32[]{:S(2)}, u32[]{:S(2)}) %all-to-all-start.2) | async-done | bytes 49184 | tf_op jit(solution)/shard_map/all_to_all | solution.py:421
  58.9 2.8 %fast_step.3 = (f32[32,3,128]{2,1,0:T(4,128)}, f32[3,128]{1,0:T(4,128)}, f32[3,128]{1,0:T(4,128)S(1)}) custom-call(s32[1]{0:T(128)} %bitcast.own_ref, f32[32,3,128]{2,1,0:T(4,128)S(1)} %all-to-all-done.2.g_ref, f32[2,32,128]{2,1,0:T(8,128)S(1)} %add_convert_fusion.cor_ref, f32[32,128]{1,0:T(8,128)S(1)} %bitcast.44, ...), custom_call_target="tpu_custom_call" | custom-call | flops 9961472 | bytes 131072 | tf_op jit(solution)/shard_map/fast_step/pallas_call | solution.py:130
  61.7 2.6 %all-to-all-start.3 = ((f32[32,3,128]{2,1,0:T(4,128)}), f32[32,3,128]{2,1,0:T(4,128)S(1)}, u32[]{:S(2)}, u32[]{:S(2)}) async-start(f32[32,3,128]{2,1,0:T(4,128)} %get-tuple-element.25), calls=%async_computation.3 | async-start | bytes 131072 | tf_op jit(solution)/shard_map/all_to_all | solution.py:421
  64.3 1.7 %collective-permute-start.6 = (f32[8,2,4,128]{3,2,1,0:T(4,128)S(1)}, f32[8,2,4,128]{3,2,1,0:T(4,128)S(1)}, u32[]{:S(2)}, u32[]{:S(2)}) collective-permute-start(f32[8,2,4,128]{3,2,1,0:T(4,128)S(1)} %get-tuple-element.38), channel_id=1, source_target_pairs={{0,1},{1,2},{2,3},{3,0},{4,5},{5,6},{6,7},{7,4},{8,9},{9,10},{10,1... | collective-permute-start | bytes 98312 | tf_op jit(solution)/shard_map/ppermute | solution.py:414
  66.0 2.1 %collective-permute-start.7 = (f32[8,2,4,128]{3,2,1,0:T(4,128)S(1)}, f32[8,2,4,128]{3,2,1,0:T(4,128)S(1)}, u32[]{:S(2)}, u32[]{:S(2)}) collective-permute-start(f32[8,2,4,128]{3,2,1,0:T(4,128)S(1)} %get-tuple-element.39), channel_id=1, source_target_pairs={{1,0},{2,1},{3,2},{0,3},{5,4},{6,5},{7,6},{4,7},{9,8},{10,9},{11,1... | collective-permute-start | bytes 98312 | tf_op jit(solution)/shard_map/ppermute | solution.py:415
  68.2 3.9 %all-to-all-done.3.g_ref = f32[32,3,128]{2,1,0:T(4,128)S(1)} async-done(((f32[32,3,128]{2,1,0:T(4,128)}), f32[32,3,128]{2,1,0:T(4,128)S(1)}, u32[]{:S(2)}, u32[]{:S(2)}) %all-to-all-start.3) | async-done | bytes 49184 | tf_op jit(solution)/shard_map/all_to_all | solution.py:421
  72.1 2.8 %fast_step.4 = (f32[32,3,128]{2,1,0:T(4,128)}, f32[3,128]{1,0:T(4,128)}, f32[3,128]{1,0:T(4,128)S(1)}) custom-call(s32[1]{0:T(128)} %bitcast.own_ref, f32[32,3,128]{2,1,0:T(4,128)S(1)} %all-to-all-done.3.g_ref, f32[2,32,128]{2,1,0:T(8,128)S(1)} %add_convert_fusion.cor_ref, f32[32,128]{1,0:T(8,128)S(1)} %bitcast.45, ...), custom_call_target="tpu_custom_call" | custom-call | flops 9961472 | bytes 131072 | tf_op jit(solution)/shard_map/fast_step/pallas_call | solution.py:130
  74.8 2.6 %all-to-all-start.4 = ((f32[32,3,128]{2,1,0:T(4,128)}), f32[32,3,128]{2,1,0:T(4,128)S(1)}, u32[]{:S(2)}, u32[]{:S(2)}) async-start(f32[32,3,128]{2,1,0:T(4,128)} %get-tuple-element.27), calls=%async_computation.4 | async-start | bytes 131072 | tf_op jit(solution)/shard_map/all_to_all | solution.py:421
  77.4 7.5 %all-to-all-done.4.g_ref = f32[32,3,128]{2,1,0:T(4,128)S(1)} async-done(((f32[32,3,128]{2,1,0:T(4,128)}), f32[32,3,128]{2,1,0:T(4,128)S(1)}, u32[]{:S(2)}, u32[]{:S(2)}) %all-to-all-start.4) | async-done | bytes 49184 | tf_op jit(solution)/shard_map/all_to_all | solution.py:421
  84.9 2.8 %fast_step.5 = (f32[32,3,128]{2,1,0:T(4,128)}, f32[3,128]{1,0:T(4,128)}, f32[3,128]{1,0:T(4,128)S(1)}) custom-call(s32[1]{0:T(128)} %bitcast.own_ref, f32[32,3,128]{2,1,0:T(4,128)S(1)} %all-to-all-done.4.g_ref, f32[2,32,128]{2,1,0:T(8,128)S(1)} %add_convert_fusion.cor_ref, f32[32,128]{1,0:T(8,128)S(1)} %bitcast.46, ...), custom_call_target="tpu_custom_call" | custom-call | flops 9961472 | bytes 131072 | tf_op jit(solution)/shard_map/fast_step/pallas_call | solution.py:130
  87.6 2.6 %all-to-all-start.5 = ((f32[32,3,128]{2,1,0:T(4,128)}), f32[32,3,128]{2,1,0:T(4,128)S(1)}, u32[]{:S(2)}, u32[]{:S(2)}) async-start(f32[32,3,128]{2,1,0:T(4,128)} %get-tuple-element.30), calls=%async_computation.5 | async-start | bytes 131072 | tf_op jit(solution)/shard_map/all_to_all | solution.py:421
  90.3 4.2 %slow.7 = f32[3,2,8,128]{3,2,1,0:T(8,128)S(1)} custom-call(s32[32,5]{1,0:T(8,128)S(1)} %bitcast.53, f32[8,12,4,128]{3,2,1,0:T(4,128)S(1)} %pad_maximum_fusion.1.tab_ref, f32[3,4,8,128]{3,2,1,0:T(8,128)S(1)} %constant_dynamic-update-slice_fusion.2.vel_ref), custom_call_target="tpu_custom_call" | custom-call | flops 13107200 | bytes 1000000 | tf_op jit(solution)/shard_map/slow/pallas_call | solution.py:388
  94.5 4.2 %slow.6 = f32[3,2,8,128]{3,2,1,0:T(8,128)S(1)} custom-call(s32[32,5]{1,0:T(8,128)S(1)} %bitcast.54, f32[8,12,4,128]{3,2,1,0:T(4,128)S(1)} %pad_maximum_fusion.1.tab_ref, f32[3,4,8,128]{3,2,1,0:T(8,128)S(1)} %constant_dynamic-update-slice_fusion.2.vel_ref), custom_call_target="tpu_custom_call" | custom-call | flops 13107200 | bytes 1000000 | tf_op jit(solution)/shard_map/slow/pallas_call | solution.py:388
  98.8 2.3 %env.3 = f32[32,3,128]{2,1,0:T(4,128)} custom-call(s32[260]{0:T(512)S(1)} %get-tuple-element.21.list_ref, s32[1]{0:T(128)} %get-tuple-element.22.count_ref, f32[32,3,128]{2,1,0:T(4,128)S(1)} %all-to-all-done.5.g_ref, f32[32,4,128]{2,1,0:T(4,128)S(1)} %constant_dynamic-update-slice_fusion.cells_ref), custom_call_target="tpu_custom_call" | custom-call | flops 2000000 | bytes 200000 | tf_op jit(solution)/shard_map/env/pallas_call | solution.py:224
  101.1 6.0 %all-to-all-start.6 = ((f32[32,3,128]{2,1,0:T(4,128)}), f32[32,3,128]{2,1,0:T(4,128)S(1)}, u32[]{:S(2)}, u32[]{:S(2)}) async-start(f32[32,3,128]{2,1,0:T(4,128)} %env.3), calls=%async_computation.6 | async-start | bytes 131072 | tf_op jit(solution)/shard_map/all_to_all | solution.py:421
  107.7 2.1 %fast_only.3.f_ref = f32[3,128]{1,0:T(4,128)S(1)} custom-call(s32[1]{0:T(128)} %bitcast.own_ref, f32[32,3,128]{2,1,0:T(4,128)S(1)} %all-to-all-done.5.g_ref, f32[2,32,128]{2,1,0:T(8,128)S(1)} %add_convert_fusion.cor_ref, f32[32,128]{1,0:T(8,128)S(1)} %bitcast.47, f32[16,128]{1,0:T(8,128)S(1)} %convert_element_type.7.exm_ref), custom_call_target="tpu_custom_call" | custom-call | flops 9961472 | bytes 131072 | tf_op jit(solution)/shard_map/fast_only/pallas_call | solution.py:116
  109.8 4.8 %all-to-all-done.6.e_ref = f32[32,3,128]{2,1,0:T(4,128)S(1)} async-done(((f32[32,3,128]{2,1,0:T(4,128)}), f32[32,3,128]{2,1,0:T(4,128)S(1)}, u32[]{:S(2)}, u32[]{:S(2)}) %all-to-all-start.6) | async-done | bytes 49184 | tf_op jit(solution)/shard_map/all_to_all | solution.py:421
  (51 shorter events, 6.3 us)
Async XLA Ops:
  1.9 7.3 %copy-start.5 = (f32[3,4,8,128]{3,2,1,0:T(8,128)S(1)}, f32[3,4,8,128]{3,2,1,0:T(8,128)}, u32[]{:S(2)}) copy-start(f32[3,4,8,128]{3,2,1,0:T(8,128)} %param.14) | copy-start | bytes 147460
  1.9 32.0 %all-to-all-start = ((f32[32,3,128]{2,1,0:T(4,128)}), f32[32,3,128]{2,1,0:T(4,128)S(1)}, u32[]{:S(2)}, u32[]{:S(2)}) async-start(f32[32,3,128]{2,1,0:T(4,128)} %broadcast_in_dim.4), calls=%async_computation | async-start | bytes 131072 | tf_op jit(solution)/shard_map/all_to_all | solution.py:421
  9.3 0.7 copy-start.4
  10.1 4.4 %collective-permute-start = (f32[2,8,4,128]{3,2,1,0:T(4,128)S(1)}, f32[2,8,4,128]{3,2,1,0:T(4,128)S(1)}, u32[]{:S(2)}, u32[]{:S(2)}) collective-permute-start(f32[2,8,4,128]{3,2,1,0:T(4,128)S(1)} %get-tuple-element.42), channel_id=1, source_target_pairs={{0,4},{4,8},{8,12},{12,16},{16,20},{20,24},{24,28},{28,0},{1,5},{5... | collective-permute-start | bytes 98312 | tf_op jit(solution)/shard_map/ppermute | solution.py:414
  10.4 4.1 %collective-permute-start.1 = (f32[2,8,4,128]{3,2,1,0:T(4,128)S(1)}, f32[2,8,4,128]{3,2,1,0:T(4,128)S(1)}, u32[]{:S(2)}, u32[]{:S(2)}) collective-permute-start(f32[2,8,4,128]{3,2,1,0:T(4,128)S(1)} %get-tuple-element.43), channel_id=1, source_target_pairs={{4,0},{8,4},{12,8},{16,12},{20,16},{24,20},{28,24},{0,28},{5,1},{9... | collective-permute-start | bytes 98312 | tf_op jit(solution)/shard_map/ppermute | solution.py:415
  12.8 0.7 copy-start.6
  14.4 4.0 %copy-start.7 = (s32[4,8,5]{1,0,2:T(4,128)S(1)}, s32[4,8,5]{1,0,2:T(4,128)}, u32[]{:S(2)}) copy-start(s32[4,8,5]{1,0,2:T(4,128)} %param.17) | copy-start | bytes 1924
  14.5 7.3 %collective-permute-start.2 = (f32[8,2,4,128]{3,2,1,0:T(4,128)S(1)}, f32[8,2,4,128]{3,2,1,0:T(4,128)S(1)}, u32[]{:S(2)}, u32[]{:S(2)}) collective-permute-start(f32[8,2,4,128]{3,2,1,0:T(4,128)S(1)} %get-tuple-element.40), channel_id=1, source_target_pairs={{0,1},{1,2},{2,3},{3,0},{4,5},{5,6},{6,7},{7,4},{8,9},{9,10},{10,1... | collective-permute-start | bytes 98312 | tf_op jit(solution)/shard_map/ppermute | solution.py:414
  16.3 5.5 %collective-permute-start.3 = (f32[8,2,4,128]{3,2,1,0:T(4,128)S(1)}, f32[8,2,4,128]{3,2,1,0:T(4,128)S(1)}, u32[]{:S(2)}, u32[]{:S(2)}) collective-permute-start(f32[8,2,4,128]{3,2,1,0:T(4,128)S(1)} %get-tuple-element.41), channel_id=1, source_target_pairs={{1,0},{2,1},{3,2},{0,3},{5,4},{6,5},{7,6},{4,7},{9,8},{10,9},{11,1... | collective-permute-start | bytes 98312 | tf_op jit(solution)/shard_map/ppermute | solution.py:415
  21.8 0.8 copy-start.3
  31.1 33.1 %collective-permute-start.5 = (f32[2,8,4,128]{3,2,1,0:T(4,128)S(1)}, f32[2,8,4,128]{3,2,1,0:T(4,128)S(1)}, u32[]{:S(2)}, u32[]{:S(2)}) collective-permute-start(f32[2,8,4,128]{3,2,1,0:T(4,128)S(1)} %bitcast.50), channel_id=1, source_target_pairs={{4,0},{8,4},{12,8},{16,12},{20,16},{24,20},{28,24},{0,28},{5,1},{9... | collective-permute-start | bytes 98312 | tf_op jit(solution)/shard_map/ppermute | solution.py:415
  33.3 30.9 %collective-permute-start.4 = (f32[2,8,4,128]{3,2,1,0:T(4,128)S(1)}, f32[2,8,4,128]{3,2,1,0:T(4,128)S(1)}, u32[]{:S(2)}, u32[]{:S(2)}) collective-permute-start(f32[2,8,4,128]{3,2,1,0:T(4,128)S(1)} %bitcast.49), channel_id=1, source_target_pairs={{0,4},{4,8},{8,12},{12,16},{16,20},{20,24},{24,28},{28,0},{1,5},{5... | collective-permute-start | bytes 98312 | tf_op jit(solution)/shard_map/ppermute | solution.py:414
  36.3 11.9 %all-to-all-start.1 = ((f32[32,3,128]{2,1,0:T(4,128)}), f32[32,3,128]{2,1,0:T(4,128)S(1)}, u32[]{:S(2)}, u32[]{:S(2)}) async-start(f32[32,3,128]{2,1,0:T(4,128)} %env.2), calls=%async_computation.1 | async-start | bytes 131072 | tf_op jit(solution)/shard_map/all_to_all | solution.py:421
  40.6 0.7 copy-start
  41.4 6.8 %copy-start.1 = (f32[3,128]{1,0:T(4,128)S(1)}, f32[3,128]{1,0:T(4,128)}, u32[]{:S(2)}) copy-start(f32[3,128]{1,0:T(4,128)} %p_ref.1) | copy-start | bytes 4612
  41.4 6.8 %copy-start.2 = (f32[3,128]{1,0:T(4,128)S(1)}, f32[3,128]{1,0:T(4,128)}, u32[]{:S(2)}) copy-start(f32[3,128]{1,0:T(4,128)} %v_ref.1) | copy-start | bytes 4612
  48.8 10.1 %all-to-all-start.2 = ((f32[32,3,128]{2,1,0:T(4,128)}), f32[32,3,128]{2,1,0:T(4,128)S(1)}, u32[]{:S(2)}, u32[]{:S(2)}) async-start(f32[32,3,128]{2,1,0:T(4,128)} %get-tuple-element.23), calls=%async_computation.2 | async-start | bytes 131072 | tf_op jit(solution)/shard_map/all_to_all | solution.py:421
  61.7 10.4 %all-to-all-start.3 = ((f32[32,3,128]{2,1,0:T(4,128)}), f32[32,3,128]{2,1,0:T(4,128)S(1)}, u32[]{:S(2)}, u32[]{:S(2)}) async-start(f32[32,3,128]{2,1,0:T(4,128)} %get-tuple-element.25), calls=%async_computation.3 | async-start | bytes 131072 | tf_op jit(solution)/shard_map/all_to_all | solution.py:421
  64.3 25.9 %collective-permute-start.6 = (f32[8,2,4,128]{3,2,1,0:T(4,128)S(1)}, f32[8,2,4,128]{3,2,1,0:T(4,128)S(1)}, u32[]{:S(2)}, u32[]{:S(2)}) collective-permute-start(f32[8,2,4,128]{3,2,1,0:T(4,128)S(1)} %get-tuple-element.38), channel_id=1, source_target_pairs={{0,1},{1,2},{2,3},{3,0},{4,5},{5,6},{6,7},{7,4},{8,9},{9,10},{10,1... | collective-permute-start | bytes 98312 | tf_op jit(solution)/shard_map/ppermute | solution.py:414
  66.0 24.2 %collective-permute-start.7 = (f32[8,2,4,128]{3,2,1,0:T(4,128)S(1)}, f32[8,2,4,128]{3,2,1,0:T(4,128)S(1)}, u32[]{:S(2)}, u32[]{:S(2)}) collective-permute-start(f32[8,2,4,128]{3,2,1,0:T(4,128)S(1)} %get-tuple-element.39), channel_id=1, source_target_pairs={{1,0},{2,1},{3,2},{0,3},{5,4},{6,5},{7,6},{4,7},{9,8},{10,9},{11,1... | collective-permute-start | bytes 98312 | tf_op jit(solution)/shard_map/ppermute | solution.py:415
  74.8 10.1 %all-to-all-start.4 = ((f32[32,3,128]{2,1,0:T(4,128)}), f32[32,3,128]{2,1,0:T(4,128)S(1)}, u32[]{:S(2)}, u32[]{:S(2)}) async-start(f32[32,3,128]{2,1,0:T(4,128)} %get-tuple-element.27), calls=%async_computation.4 | async-start | bytes 131072 | tf_op jit(solution)/shard_map/all_to_all | solution.py:421
  87.6 11.1 %all-to-all-start.5 = ((f32[32,3,128]{2,1,0:T(4,128)}), f32[32,3,128]{2,1,0:T(4,128)S(1)}, u32[]{:S(2)}, u32[]{:S(2)}) async-start(f32[32,3,128]{2,1,0:T(4,128)} %get-tuple-element.30), calls=%async_computation.5 | async-start | bytes 131072 | tf_op jit(solution)/shard_map/all_to_all | solution.py:421
  101.1 13.5 %all-to-all-start.6 = ((f32[32,3,128]{2,1,0:T(4,128)}), f32[32,3,128]{2,1,0:T(4,128)S(1)}, u32[]{:S(2)}, u32[]{:S(2)}) async-start(f32[32,3,128]{2,1,0:T(4,128)} %env.3), calls=%async_computation.6 | async-start | bytes 131072 | tf_op jit(solution)/shard_map/all_to_all | solution.py:421

commit v4 on v3

--- a/solution.py
+++ b/solution.py
@@ -31,64 +31,87 @@
     return jax.ShapeDtypeStruct(shape, dtype)
 
 
-def fast_rows(g_ref, cor_ref, q_ref, exm_ref, own, planes, cols, sums):
+def split3(x):
+    hi = x.astype(BF16).astype(F32)
+    rest = x - hi
+    mid = rest.astype(BF16).astype(F32)
+    return hi, mid, rest - mid
+
+
+def norm_rows(y):
+    row = lax.broadcasted_iota(jnp.int32, y.shape, 0)
+    pos = jnp.where(row < 3, y, 0.0)
+    return row, pos, jnp.sum(pos * pos, axis=0, keepdims=True)
+
+
+def left_rows(y):
+    row, pos, norm = norm_rows(y)
+    hi, mid, lo = split3(jnp.where(row == 3, norm, jnp.where(row == 4, 1.0, pos)))
+    return jnp.concatenate([hi, hi, mid, hi, mid, lo], axis=0)
+
+
+def right_rows(y, soft):
+    row, pos, norm = norm_rows(y)
+    hi, mid, lo = split3(
+        jnp.where(row == 3, 1.0, jnp.where(row == 4, norm + soft, -2.0 * pos))
+    )
+    return jnp.concatenate([hi, mid, hi, lo, mid, hi], axis=0)
+
+
+def fast_rows(g_ref, table_ref, exm_ref, own, atoms, feat, dist, sums):
     count = g_ref.shape[0]
     members = exm_ref.shape[0]
-    for c in range(3):
-        x = g_ref[:, c, :]
-        planes[c] = x + cor_ref[c] if c < 2 else x
-    own_rows = [planes[c, pl.ds(own, 1), :] for c in range(3)]
-    for c in range(3):
-        cols[c] = jnp.transpose(jnp.broadcast_to(own_rows[c], (LANES, LANES)))
+    zeros = jnp.zeros((5, LANES), F32)
+    for b in range(count):
+        y = jnp.concatenate([g_ref[b], zeros], axis=0) + table_ref[b]
+        atoms[b] = y
+        feat[:, LANES * b : LANES * (b + 1)] = right_rows(y, 1.0).astype(BF16)
+    me = atoms[own]
+    left = jnp.transpose(left_rows(me)).astype(BF16)
+    dist[...] = jnp.dot(left, feat[...], preferred_element_type=F32)
     unroll = 2
 
     def body(i, carry):
         at = [pl.ds(pl.multiple_of((i * unroll + u) * 8, 8), 8) for u in range(unroll)]
-        a = [[cols[c, at[u], :] for c in range(3)] for u in range(unroll)]
-        acc = [[jnp.zeros((8, LANES), F32) for _ in range(3)] for _ in range(unroll)]
+        acc = [None] * unroll
         for b in range(count):
-            y = [jnp.broadcast_to(planes[c, b : b + 1, :], (8, LANES)) for c in range(3)]
-            qb = jnp.broadcast_to(q_ref[b : b + 1, :], (8, LANES))
+            y = [jnp.broadcast_to(atoms[b, c : c + 1, :], (8, LANES)) for c in range(4)]
             for u in range(unroll):
-                d = [a[u][c] - y[c] for c in range(3)]
-                r = lax.rsqrt(d[0] * d[0] + d[1] * d[1] + d[2] * d[2] + 1.0)
-                w = (qb * r) * (r * r)
-                for c in range(3):
-                    acc[u][c] = acc[u][c] + w * d[c]
+                r = lax.rsqrt(dist[at[u], LANES * b : LANES * (b + 1)])
+                w = (y[3] * r) * (r * r)
+                f = [w * y[0], w * y[1], w * y[2], w]
+                acc[u] = f if acc[u] is None else [acc[u][c] + f[c] for c in range(4)]
         for u in range(unroll):
-            for c in range(3):
+            for c in range(4):
                 sums[c, at[u], :] = acc[u][c]
         return carry
 
     lax.fori_loop(0, LANES // (8 * unroll), body, 0)
     step = GROUPS // LANES
     part = pl.ds(lax.rem(own, step), members, stride=step)
-    d = [own_rows[c] - planes[c, part, :] for c in range(3)]
+    d = [me[c : c + 1] - atoms[part, c, :] for c in range(3)]
     r = lax.rsqrt(d[0] * d[0] + d[1] * d[1] + d[2] * d[2] + 1.0)
-    w = (exm_ref[...] * q_ref[part, :]) * (r * (r * r))
-    ones = jnp.ones((8, LANES), F32)
-    scale = fast_coupling * q_ref[pl.ds(own, 1), :]
-    out = []
-    for c in range(3):
-        total = lax.dot_general(
-            ones, sums[c], (((1,), (1,)), ((), ())),
-            precision=lax.Precision.HIGHEST, preferred_element_type=F32,
-        )[0:1, :]
-        out.append(scale * (total - jnp.sum(w * d[c], axis=0, keepdims=True)))
-    return out
-
-
-def fast_only_kernel(own_ref, g_ref, cor_ref, q_ref, exm_ref, f_ref, planes, cols, sums):
-    rows = fast_rows(g_ref, cor_ref, q_ref, exm_ref, own_ref[0], planes, cols, sums)
+    w = (exm_ref[...] * atoms[part, 3, :]) * (r * (r * r))
+    scale = fast_coupling * me[3:4]
+    total = [jnp.sum(jnp.transpose(sums[c]), axis=0, keepdims=True) for c in range(4)]
+    return [
+        scale
+        * (me[c : c + 1] * total[3] - total[c] - jnp.sum(w * d[c], axis=0, keepdims=True))
+        for c in range(3)
+    ]
+
+
+def fast_only_kernel(own_ref, g_ref, table_ref, exm_ref, f_ref, *scratch):
+    rows = fast_rows(g_ref, table_ref, exm_ref, own_ref[0], *scratch)
     for c in range(3):
         f_ref[c : c + 1, :] = rows[c]
 
 
 def fast_step_kernel(
-    own_ref, g_ref, cor_ref, q_ref, exm_ref, v_ref, send_ref, p_out, v_out, planes, cols, sums
+    own_ref, g_ref, table_ref, exm_ref, v_ref, send_ref, p_out, v_out, *scratch
 ):
     own = own_ref[0]
-    rows = fast_rows(g_ref, cor_ref, q_ref, exm_ref, own, planes, cols, sums)
+    rows = fast_rows(g_ref, table_ref, exm_ref, own, *scratch)
     count = send_ref.shape[0]
     for c in range(3):
         v = v_ref[c : c + 1, :] + inner_dt * rows[c]
@@ -100,67 +123,75 @@
 
 def fast_cost(count):
     pairs = count * LANES * LANES
-    return pl.CostEstimate(flops=19 * pairs, transcendentals=pairs, bytes_accessed=count * 4096)
+    return pl.CostEstimate(flops=10 * pairs, transcendentals=pairs, bytes_accessed=count * 4096)
 
 
 def fast_scratch(count):
     return [
-        pltpu.VMEM((3, count, LANES), F32),
-        pltpu.VMEM((3, LANES, LANES), F32),
-        pltpu.VMEM((3, LANES, LANES), F32),
+        pltpu.VMEM((count, 8, LANES), F32),
+        pltpu.VMEM((48, count * LANES), BF16),
+        pltpu.VMEM((LANES, count * LANES), F32),
+        pltpu.VMEM((4, LANES, LANES), F32),
     ]
 
 
-def fast_only(own, g, cor, q, exm):
+def fast_only(own, g, table, exm):
     count = g.shape[0]
     return pl.pallas_call(
         fast_only_kernel,
         out_shape=sds((3, LANES)),
-        in_specs=[SMEM] + [VMEM] * 4,
+        in_specs=[SMEM] + [VMEM] * 3,
         out_specs=VMEM,
         scratch_shapes=fast_scratch(count),
         cost_estimate=fast_cost(count),
         name="fast_only",
-        compiler_params=pltpu.CompilerParams(vmem_limit_bytes=2 << 20),
-    )(own, g, cor, q, exm)
-
-
-def fast_step(own, g, cor, q, exm, v):
+        compiler_params=pltpu.CompilerParams(vmem_limit_bytes=4 << 20),
+    )(own, g, table, exm)
+
+
+def fast_step(own, g, table, exm, v):
     count = g.shape[0]
     return pl.pallas_call(
         fast_step_kernel,
         out_shape=(sds((count, 3, LANES)), sds((3, LANES)), sds((3, LANES))),
-        in_specs=[SMEM] + [VMEM] * 5,
+        in_specs=[SMEM] + [VMEM] * 4,
         out_specs=(VMEM,) * 3,
         scratch_shapes=fast_scratch(count),
         cost_estimate=fast_cost(count),
         name="fast_step",
-        compiler_params=pltpu.CompilerParams(vmem_limit_bytes=2 << 20),
-    )(own, g, cor, q, exm, v)
-
-
-def list_kernel(total_cols, cell_rows, cell_cols, owner_ref, base_ref, list_ref, count_ref):
-    row0, col0 = base_ref[0], base_ref[1]
-
-    unroll = 8
-
-    power = total_cols & (total_cols - 1) == 0 and cell_cols & (cell_cols - 1) == 0
+        compiler_params=pltpu.CompilerParams(vmem_limit_bytes=4 << 20),
+    )(own, g, table, exm, v)
+
+
+def prep_kernel(
+    grid, place_ref, owner_smem, owner_ref, q_ref, ex_ref, table_ref, exm_ref, list_ref, count_ref
+):
+    total_cols, cell_rows, cell_cols = grid
+    own, row_index, col_index = place_ref[0], place_ref[1], place_ref[2]
+    owner = owner_ref[...]
+    table_ref[...] = jnp.zeros_like(table_ref)
+    table_ref[:, 0, :] = (lax.div(owner, total_cols) - total_cols // 2).astype(F32)
+    table_ref[:, 1, :] = (lax.rem(owner, total_cols) - total_cols // 2).astype(F32)
+    table_ref[:, 3, :] = q_ref[...]
+    ex = ex_ref[:, pl.ds(pl.multiple_of(own * LANES, LANES), LANES)]
+    ex = lax.div(ex, GROUPS)
+    member = lax.broadcasted_iota(jnp.int32, exm_ref.shape, 0)
+    barred = jnp.zeros(exm_ref.shape, F32)
+    for k in range(ex_ref.shape[0]):
+        barred = jnp.where(member == ex[k : k + 1], 1.0, barred)
+    exm_ref[...] = barred
+    row_bit = total_cols * cell_rows
+    keep = -row_bit | (total_cols - cell_cols)
+    here = row_index * row_bit + col_index * cell_cols
+    unroll = 16
 
     def body(j, n):
         found = []
         for u in range(unroll):
-            cell = owner_ref[j * unroll + u]
-            if power:
-                r = lax.shift_right_logical(cell, total_cols.bit_length() - 1) - row0
-                c = (cell & (total_cols - 1)) - col0
-                local = lax.shift_left(r, cell_cols.bit_length() - 1) + c
-            else:
-                r = lax.div(cell, total_cols) - row0
-                c = lax.rem(cell, total_cols) - col0
-                local = r * cell_cols + c
-            sign = r | (cell_rows - 1 - r) | c | (cell_cols - 1 - c)
-            entry = j * unroll + (u + lax.shift_left(local, GROUPS.bit_length() - 1))
-            found.append((entry, 1 + lax.shift_right_arithmetic(sign, 31)))
+            i = j * unroll + u
+            cell = owner_smem[i]
+            other = (cell & keep) ^ here
+            found.append((cell * GROUPS + i, lax.shift_right_logical(other - 1, 31)))
         for entry, inside in found:
             list_ref[n] = entry
             n = n + inside
@@ -172,18 +203,23 @@
         list_ref[n + k] = -1
 
 
-def env_list(owner, base, total_cols, cell_rows, cell_cols):
+def prep(place, owner, q, exclusions, members, grid):
+    count = owner.shape[0] // LANES
     return pl.pallas_call(
-        functools.partial(list_kernel, total_cols, cell_rows, cell_cols),
-        out_shape=(sds((GROUPS + ENV_UNROLL,), jnp.int32), sds((1,), jnp.int32)),
-        in_specs=[SMEM, SMEM],
-        out_specs=(SMEM, SMEM),
-        name="env_list",
+        functools.partial(prep_kernel, grid),
+        out_shape=(
+            sds((count, 8, LANES)), sds((members, LANES)),
+            sds((GROUPS + ENV_UNROLL,), jnp.int32), sds((1,), jnp.int32),
+        ),
+        in_specs=[SMEM, SMEM, VMEM, VMEM, VMEM],
+        out_specs=(VMEM, VMEM, SMEM, SMEM),
+        name="prep",
         compiler_params=pltpu.CompilerParams(vmem_limit_bytes=2 << 20),
-    )(owner, base)
-
-
-def env_kernel(list_ref, count_ref, g_ref, cells_ref, out_ref, planes, sums):
+    )(place, owner, owner.reshape(count, LANES), q, exclusions.T)
+
+
+def env_kernel(grid, list_ref, count_ref, g_ref, cells_ref, out_ref, planes, sums):
+    total_cols, cell_rows, cell_cols = grid
     step = GROUPS // LANES
     members = g_ref.shape[0] // step
     for c in range(3):
@@ -199,7 +235,9 @@
             group = entry & (GROUPS - 1)
             h = lax.shift_right_logical(group, LANES.bit_length() - 1)
             here = (lane == (group & (LANES - 1))) & (entry >= 0)
-            cell = cells_ref[jnp.maximum(lax.shift_right_arithmetic(entry, GROUPS.bit_length() - 1), 0)]
+            number = jnp.maximum(lax.shift_right_arithmetic(entry, GROUPS.bit_length() - 1), 0)
+            r = lax.div(number, total_cols) & (cell_rows - 1)
+            cell = cells_ref[r * cell_cols + (number & (cell_cols - 1))]
             d = []
             for c in range(3):
                 x = jnp.sum(jnp.where(here, planes[c, h], 0.0), axis=1, keepdims=True)
@@ -217,12 +255,12 @@
             out_ref[pl.ds(h, members, stride=step), c, :] = sums[c, h]
 
 
-def env(lists, g, cells):
+def env(lists, g, cells, grid):
     count = g.shape[0]
     step = GROUPS // LANES
     members = count // step
     return pl.pallas_call(
-        env_kernel,
+        functools.partial(env_kernel, grid),
         out_shape=sds((count, 3, LANES)),
         in_specs=[SMEM, SMEM, VMEM, VMEM],
         out_specs=VMEM,
@@ -280,22 +318,24 @@
     )(own, e, f, q, v)
 
 
-def split3(x):
-    hi = x.astype(BF16).astype(F32)
-    rest = x - hi
-    mid = rest.astype(BF16).astype(F32)
-    return hi, mid, rest - mid
-
-
 def slow_kernel(first, row0, nb_ref, tab_ref, vel_ref, *refs):
+    results = 3 if first else 1
+    if row0:
+        before, refs = refs[:results], refs[results:]
+    outs, scratch = refs[:results], refs[results:]
+    vel_out = outs[0]
     if first:
-        vel_out, pos_out, cell_out, *scratch = refs
-    else:
-        vel_out, *scratch = refs
+        pos_out, cell_out = outs[1:]
     bufs = [tuple(scratch[0:4]), tuple(scratch[4:8])]
-    cell_rows, cell_cols = vel_out.shape[1], vel_out.shape[2]
+    cell_rows, cell_cols = vel_out.shape[1] - row0, vel_out.shape[2]
     slots = nb_ref.shape[1]
     count = cell_rows * cell_cols
+    skip = row0 * cell_cols
+    if row0:
+        vel_out[:, :row0] = before[0][...]
+        if first:
+            pos_out[:, :row0] = before[1][...]
+            cell_out[:skip] = before[2][...]
     row8 = lax.broadcasted_iota(jnp.int32, (8, CELL), 0)
 
     def place(n):
@@ -308,10 +348,7 @@
     def distances(n, buf):
         feat, ys, dist, _ = buf
         r, c = place(n)
-        x = jnp.where(row8 < 3, load8(r + (row0 + 2), c + 2), 0.0)
-        norm = jnp.sum(x * x, axis=0, keepdims=True)
-        hi, mid, lo = split3(jnp.where(row8 == 3, norm, jnp.where(row8 == 4, 1.0, x)))
-        left = jnp.transpose(jnp.concatenate([hi, hi, mid, hi, mid, lo], axis=0)).astype(BF16)
+        left = jnp.transpose(left_rows(load8(r + (row0 + 2), c + 2))).astype(BF16)
         for k in range(slots):
             o = nb_ref[n + row0 * cell_cols, k]
             dr, dc = lax.div(o, 5), lax.rem(o, 5)
@@ -320,14 +357,7 @@
                 row8 == 0, (dr - 2).astype(F32), jnp.where(row8 == 1, (dc - 2).astype(F32), 0.0)
             )
             ys[8 * k : 8 * k + 8] = y
-            y = jnp.where(row8 < 3, y, 0.0)
-            norm = jnp.sum(y * y, axis=0, keepdims=True) + 0.5
-            hi, mid, lo = split3(
-                jnp.where(row8 == 3, 1.0, jnp.where(row8 == 4, norm, -2.0 * y))
-            )
-            feat[:, CELL * k : CELL * (k + 1)] = jnp.concatenate(
-                [hi, mid, hi, lo, mid, hi], axis=0
-            ).astype(BF16)
+            feat[:, CELL * k : CELL * (k + 1)] = right_rows(y, 0.5).astype(BF16)
         dist[...] = jnp.dot(left, feat[...], preferred_element_type=F32)
 
     def pairs(buf):
@@ -355,13 +385,13 @@
         for x in range(3):
             f = scale * (t[x : x + 1] * total[3] - total[x])
             v = vel_ref[x, r + row0, pl.ds(c, 1), :] + half_outer * f
-            vel_out[x, r, pl.ds(c, 1), :] = v
+            vel_out[x, r + row0, pl.ds(c, 1), :] = v
             if first:
                 p = t[x : x + 1] + outer_dt * v
-                pos_out[x, r, pl.ds(c, 1), :] = p
-                cell_out[n, x : x + 1, :] = p
+                pos_out[x, r + row0, pl.ds(c, 1), :] = p
+                cell_out[n + skip, x : x + 1, :] = p
         if first:
-            cell_out[n, 3:4, :] = t[3:4]
+            cell_out[n + skip, 3:4, :] = t[3:4]
 
     distances(0, bufs[0])
 
@@ -379,17 +409,19 @@
     finish(count - 1, bufs[1])
 
 
-def slow(first, row0, rows, nb, tab, vel):
-    shape = (3, rows) + vel.shape[2:]
+def slow(first, row0, rows, nb, tab, vel, before=()):
+    shape = (3, row0 + rows) + vel.shape[2:]
     own = rows * vel.shape[2]
     slots = nb.shape[1]
-    out = (sds(shape), sds(shape), sds((own, 4, CELL))) if first else sds(shape)
+    out = (sds(shape),)
+    if first:
+        out += (sds(shape), sds(((row0 + rows) * vel.shape[2], 4, CELL)))
     pairs = own * slots * CELL * CELL
     return pl.pallas_call(
         functools.partial(slow_kernel, first, row0),
         out_shape=out,
-        in_specs=[SMEM, VMEM, VMEM],
-        out_specs=(VMEM,) * 3 if first else VMEM,
+        in_specs=[SMEM] + [VMEM] * (2 + len(before)),
+        out_specs=(VMEM,) * len(out),
         scratch_shapes=[
             pltpu.VMEM((48, slots * CELL), BF16),
             pltpu.VMEM((8 * slots, CELL), F32),
@@ -401,7 +433,7 @@
             flops=10 * pairs, transcendentals=pairs, bytes_accessed=1_000_000
         ),
         name="slow",
-    )(nb, tab, vel)
+    )(nb, tab, vel, *before)
 
 
 def with_halo(x, sides, width):
@@ -440,42 +472,36 @@
 
     g = exchange(jnp.broadcast_to(fast_pos[None], (count, 3, piece)))
 
-    owner = fast_owner.reshape(count, piece)
-    cor = jnp.stack([owner // total_cols, owner % total_cols]).astype(F32)
     q = fast_charge.reshape(count, piece)
     members = fast_charge.shape[0] // GROUPS
-    ex = lax.dynamic_slice_in_dim(exclusions, flat * piece, piece, 0) // GROUPS
-    exm = jnp.any(
-        ex[None] == jnp.arange(members, dtype=jnp.int32)[:, None, None], axis=2
-    ).astype(F32)
-    base = jnp.stack([row_index * cell_rows, col_index * cell_cols]).astype(jnp.int32)
-    lists = env_list(fast_owner[:GROUPS], base, total_cols, cell_rows, cell_cols)
+    place = jnp.stack([flat, row_index, col_index]).astype(jnp.int32)
+    grid = (total_cols, cell_rows, cell_cols)
+    table, exm, *lists = prep(place, fast_owner, q, exclusions, members, grid)
 
     cells = jnp.concatenate([slow_pos, slow_charge[None]], axis=0).transpose(1, 2, 0, 3)
     sides = (("row", 0), ("col", 1))
     nb = neighbours.reshape(cell_rows * cell_cols, -1)
     half = cell_rows // 2
     tab = with_halo(cells, sides, 2)
-    parts = []
+    part = ()
     for r0 in (0, half):
-        parts.append(slow(True, r0, half, nb, tab, slow_vel))
-    slow_vel, slow_pos = (jnp.concatenate([parts[0][i], parts[1][i]], axis=1) for i in (0, 1))
-    cells2 = jnp.concatenate([parts[0][2], parts[1][2]], axis=0)
+        part = slow(True, r0, half, nb, tab, slow_vel, part)
+    slow_vel, slow_pos, cells2 = part
     tab2 = with_halo(cells2.reshape(cells.shape), sides, 2)
-    parts = []
+    part = ()
     for r0 in (0, half):
-        parts.append(slow(False, r0, half, nb, tab2, slow_vel))
-    slow_vel = jnp.concatenate(parts, axis=1)
-
-    back = exchange(env(lists, g, cells.reshape(cells2.shape)))
-    f = fast_only(own, g, cor, q, exm)
+        part = slow(False, r0, half, nb, tab2, slow_vel, part)
+    (slow_vel,) = part
+
+    back = exchange(env(lists, g, cells.reshape(cells2.shape), grid))
+    f = fast_only(own, g, table, exm)
     send, p, v = kick(own, back, f, q, fast_pos, fast_vel)
     for _ in range(INNER - 1):
         g = exchange(send)
-        send, p, v = fast_step(own, g, cor, q, exm, v)
+        send, p, v = fast_step(own, g, table, exm, v)
     g = exchange(send)
-    back = exchange(env(lists, g, cells2))
-    f = fast_only(own, g, cor, q, exm)
+    back = exchange(env(lists, g, cells2, grid))
+    f = fast_only(own, g, table, exm)
     v = last_kick(own, back, f, q, v)
     return (p, v, slow_pos, slow_vel)
 
@@ -620,7 +646,9 @@
     both = P(None, ("row", "col"))
 
     def run(*args):
-        special = args[0].shape[1] == LANES * mesh.size
+        rows, cols = args[5].shape[1:3]
+        powers = all(n & (n - 1) == 0 for n in (rows, cols, *mesh.shape.values()))
+        special = args[0].shape[1] == LANES * mesh.size and powers
         step = jax.shard_map(
             per_device if special else general,
             mesh=mesh,

time: 116 us -> 101 us (0.87)
  waiting for transfers between devices: 28.5 us -> 18.9 us
  other arithmetic: 2.26 us -> 0.28 us
  Pallas kernels: 38.6 us -> 37 us
  starting transfers between devices: 40.6 us -> 39.2 us
    all_to_all x7, waiting for transfers between devices: 28.3 us -> 18.9 us  [exchange(): return lax.all_to_all(x, BOTH, 0, 0)]
    all_to_all x7, starting transfers between devices: 28 us -> 26.1 us  [exchange(): return lax.all_to_all(x, BOTH, 0, 0)]
    pallas_call x3, Pallas kernels: 8.28 us -> 6.99 us  [fast_step(): pl.pallas_call(fast_step_kernel, out_shape=(sds((count, 3, LANES)), sds((...]
    concatenate x2 -> x0, other arithmetic: 1.25 us -> none  [the longest x1 0.62 us: rows_of_lanes(): slow_vel = jnp.concatenate(parts, axis=1)]
    pallas_call x4, Pallas kernels: 17 us -> 18.2 us  [slow(): pl.pallas_call(functools.partial(slow_kernel, first, row0), out_shape=out...]
  transfers between devices with their start and end apart: 15 -> 15, of which waited for: 6 -> 5; matrix products, arithmetic and copies ran while one was open for 2% -> 0% of each run, Pallas kernels for 31% -> 32%
where the time goes in v4:
time: 101 us; the launch traced here: 99.9 us
  starting transfers between devices  39.2 us (39%)
  Pallas kernels  37 us (37%)
  waiting for transfers between devices  18.9 us (19%)
  local copies, waits for them, and re-layouts  3.59 us (4%)
    all_to_all x7, starting transfers between devices, exchange(): return lax.all_to_all(x, BOTH, 0, 0)  26.1 us
    all_to_all x7, waiting for transfers between devices, exchange(): return lax.all_to_all(x, BOTH, 0, 0)  18.9 us
    pallas_call x4, Pallas kernels, slow(): pl.pallas_call(functools.partial(slow_kernel, first, row0), out_shape=out...  18.2 us
    ppermute x4, starting transfers between devices, with_halo(): after = lax.ppermute(initial, axis, down)  9.06 us
    pallas_call x3, Pallas kernels, fast_step(): pl.pallas_call(fast_step_kernel, out_shape=(sds((count, 3, LANES)), sds((...  6.99 us
    pallas_call x2, Pallas kernels, env(): pl.pallas_call(functools.partial(env_kernel, grid), out_shape=sds((count,...  4.62 us
    ppermute x4, starting transfers between devices, with_halo(): before = lax.ppermute(last, axis, up)  4.09 us
    pallas_call x2, Pallas kernels, fast_only(): pl.pallas_call(fast_only_kernel, out_shape=sds((3, LANES)), in_specs=[SME...  3.33 us
  transfers between devices with their start and end apart: 15, of which 5 were waited for; matrix products, arithmetic and copies ran while one was open for 0% of the time, Pallas kernels for 32%

profile of v4, /device:TPU:0, one launch (start us, length us, event | category | flops | bytes accessed | tf_op | source)
XLA Modules:
  0.0 99.9 jit_solution(1629041528431113823)
XLA Ops:
  0.6 1.3 %broadcast_in_dim.4 = f32[32,3,128]{2,1,0:T(4,128)} broadcast(f32[3,128]{1,0:T(4,128)} %p_ref.1), dimensions={1,2} | broadcast | bytes 50688 | tf_op jit(solution)/shard_map/broadcast_in_dim | solution.py:473
  1.9 7.3 %all-to-all-start = ((f32[32,3,128]{2,1,0:T(4,128)}), f32[32,3,128]{2,1,0:T(4,128)S(1)}, u32[]{:S(2)}, u32[]{:S(2)}) async-start(f32[32,3,128]{2,1,0:T(4,128)} %broadcast_in_dim.4), calls=%async_computation | async-start | bytes 131072 | tf_op jit(solution)/shard_map/all_to_all | solution.py:453
  10.9 2.5 %prep.1 = (f32[32,8,128]{2,1,0:T(8,128)S(1)}, f32[16,128]{1,0:T(8,128)S(1)}, s32[260]{0:T(512)S(1)}, s32[1]{0:T(128)}) custom-call(s32[3]{0:T(128)S(1)} %pad_add_fusion.place_ref, s32[4096]{0:T(1024)S(1)} %copy-done.1, s32[32,128]{1,0:T(8,128)S(1)} %bitcast.21, f32[32,128]{1,0:T(8,128)S(1)} %bitcast.18, s32[4,4096]{1,0:T(4,128)S(1)} %bitcast.22), custom_call_target="tpu_custom_call" | custom-call | tf_op jit(solution)/shard_map/prep/pallas_call | solution.py:208
  13.5 3.3 %all-to-all-done.g_ref = f32[32,3,128]{2,1,0:T(4,128)S(1)} async-done(((f32[32,3,128]{2,1,0:T(4,128)}), f32[32,3,128]{2,1,0:T(4,128)S(1)}, u32[]{:S(2)}, u32[]{:S(2)}) %all-to-all-start) | async-done | bytes 49184 | tf_op jit(solution)/shard_map/all_to_all | solution.py:453
  16.8 2.3 %env.2 = f32[32,3,128]{2,1,0:T(4,128)} custom-call(s32[260]{0:T(512)S(1)} %get-tuple-element.23.list_ref, s32[1]{0:T(128)} %get-tuple-element.24.count_ref, f32[32,3,128]{2,1,0:T(4,128)S(1)} %all-to-all-done.g_ref, f32[32,4,128]{2,1,0:T(4,128)S(1)} %bitcast.17), custom_call_target="tpu_custom_call" | custom-call | flops 2000000 | bytes 200000 | tf_op jit(solution)/shard_map/env/pallas_call | solution.py:262
  19.1 2.7 %all-to-all-start.1 = ((f32[32,3,128]{2,1,0:T(4,128)}), f32[32,3,128]{2,1,0:T(4,128)S(1)}, u32[]{:S(2)}, u32[]{:S(2)}) async-start(f32[32,3,128]{2,1,0:T(4,128)} %env.2), calls=%async_computation.1 | async-start | bytes 131072 | tf_op jit(solution)/shard_map/all_to_all | solution.py:453
  22.2 2.4 %collective-permute-start.1 = (f32[2,8,4,128]{3,2,1,0:T(4,128)S(1)}, f32[2,8,4,128]{3,2,1,0:T(4,128)S(1)}, u32[]{:S(2)}, u32[]{:S(2)}) collective-permute-start(f32[2,8,4,128]{3,2,1,0:T(4,128)S(1)} %get-tuple-element.49), channel_id=1, source_target_pairs={{4,0},{8,4},{12,8},{16,12},{20,16},{24,20},{28,24},{0,28},{5,1},{9... | collective-permute-start | bytes 98312 | tf_op jit(solution)/shard_map/ppermute | solution.py:447
  24.6 1.7 %fast_only.2.f_ref = f32[3,128]{1,0:T(4,128)S(1)} custom-call(s32[1]{0:T(128)} %bitcast.own_ref, f32[32,3,128]{2,1,0:T(4,128)S(1)} %all-to-all-done.g_ref, f32[32,8,128]{2,1,0:T(8,128)S(1)} %get-tuple-element.25.table_ref, f32[16,128]{1,0:T(8,128)S(1)} %get-tuple-element.26.exm_ref), custom_call_target="tpu_custom_call" | custom-call | flops 5242880 | bytes 131072 | tf_op jit(solution)/shard_map/fast_only/pallas_call | solution.py:140
  26.2 3.1 %all-to-all-done.1.e_ref = f32[32,3,128]{2,1,0:T(4,128)S(1)} async-done(((f32[32,3,128]{2,1,0:T(4,128)}), f32[32,3,128]{2,1,0:T(4,128)S(1)}, u32[]{:S(2)}, u32[]{:S(2)}) %all-to-all-start.1) | async-done | bytes 49184 | tf_op jit(solution)/shard_map/all_to_all | solution.py:453
  30.0 2.5 %all-to-all-start.2 = ((f32[32,3,128]{2,1,0:T(4,128)}), f32[32,3,128]{2,1,0:T(4,128)S(1)}, u32[]{:S(2)}, u32[]{:S(2)}) async-start(f32[32,3,128]{2,1,0:T(4,128)} %get-tuple-element.27), calls=%async_computation.2 | async-start | bytes 131072 | tf_op jit(solution)/shard_map/all_to_all | solution.py:453
  32.7 1.7 %collective-permute-start.2 = (f32[8,2,4,128]{3,2,1,0:T(4,128)S(1)}, f32[8,2,4,128]{3,2,1,0:T(4,128)S(1)}, u32[]{:S(2)}, u32[]{:S(2)}) collective-permute-start(f32[8,2,4,128]{3,2,1,0:T(4,128)S(1)} %get-tuple-element.44), channel_id=1, source_target_pairs={{0,1},{1,2},{2,3},{3,0},{4,5},{5,6},{6,7},{7,4},{8,9},{9,10},{10,1... | collective-permute-start | bytes 98312 | tf_op jit(solution)/shard_map/ppermute | solution.py:446
  34.4 2.1 %collective-permute-start.3 = (f32[8,2,4,128]{3,2,1,0:T(4,128)S(1)}, f32[8,2,4,128]{3,2,1,0:T(4,128)S(1)}, u32[]{:S(2)}, u32[]{:S(2)}) collective-permute-start(f32[8,2,4,128]{3,2,1,0:T(4,128)S(1)} %get-tuple-element.45), channel_id=1, source_target_pairs={{1,0},{2,1},{3,2},{0,3},{5,4},{6,5},{7,6},{4,7},{9,8},{10,9},{11,1... | collective-permute-start | bytes 98312 | tf_op jit(solution)/shard_map/ppermute | solution.py:447
  36.6 3.8 %all-to-all-done.2.g_ref = f32[32,3,128]{2,1,0:T(4,128)S(1)} async-done(((f32[32,3,128]{2,1,0:T(4,128)}), f32[32,3,128]{2,1,0:T(4,128)S(1)}, u32[]{:S(2)}, u32[]{:S(2)}) %all-to-all-start.2) | async-done | bytes 49184 | tf_op jit(solution)/shard_map/all_to_all | solution.py:453
  40.4 2.3 %fast_step.3 = (f32[32,3,128]{2,1,0:T(4,128)}, f32[3,128]{1,0:T(4,128)}, f32[3,128]{1,0:T(4,128)S(1)}) custom-call(s32[1]{0:T(128)} %bitcast.own_ref, f32[32,3,128]{2,1,0:T(4,128)S(1)} %all-to-all-done.2.g_ref, f32[32,8,128]{2,1,0:T(8,128)S(1)} %get-tuple-element.25.table_ref, f32[16,128]{1,0:T(8,128)S(1)} %get-tuple-element.26.exm_ref, ...), custom_call_target="tpu_custom_call" | custom-call | flops 5242880 | bytes 131072 | tf_op jit(solution)/shard_map/fast_step/pallas_call | solution.py:154
  42.7 2.5 %all-to-all-start.3 = ((f32[32,3,128]{2,1,0:T(4,128)}), f32[32,3,128]{2,1,0:T(4,128)S(1)}, u32[]{:S(2)}, u32[]{:S(2)}) async-start(f32[32,3,128]{2,1,0:T(4,128)} %get-tuple-element.29), calls=%async_computation.3 | async-start | bytes 131072 | tf_op jit(solution)/shard_map/all_to_all | solution.py:453
  45.4 0.7 copy-done.5
  46.1 4.2 %slow.4 = (f32[3,2,8,128]{3,2,1,0:T(8,128)S(1)}, f32[3,2,8,128]{3,2,1,0:T(8,128)S(1)}, f32[16,4,128]{2,1,0:T(4,128)S(1)}) custom-call(s32[32,5]{1,0:T(8,128)S(1)} %bitcast.23, f32[8,12,4,128]{3,2,1,0:T(4,128)S(1)} %pad_maximum_fusion.tab_ref, f32[3,4,8,128]{3,2,1,0:T(8,128)S(1)} %copy-done.5), custom_call_target="tpu_custom_call" | custom-call | flops 13107200 | bytes 1000000 | tf_op jit(solution)/shard_map/slow/pallas_call | solution.py:420
  50.3 4.9 %slow.5 = (f32[3,4,8,128]{3,2,1,0:T(8,128)S(1)}, f32[3,4,8,128]{3,2,1,0:T(8,128)}, f32[32,4,128]{2,1,0:T(4,128)S(1)}) custom-call(s32[32,5]{1,0:T(8,128)S(1)} %bitcast.24, f32[8,12,4,128]{3,2,1,0:T(4,128)S(1)} %pad_maximum_fusion.tab_ref, f32[3,4,8,128]{3,2,1,0:T(8,128)S(1)} %copy-done.5, f32[3,2,8,128]{3,2,1,0:T(8,128)S(1)} %get-tuple-element.35.refs_0_, ...), custom_call_target="tpu_custom_call" | custom-call | flops 13107200 | bytes 1000000 | tf_op jit(solution)/shard_map/slow/pallas_call | solution.py:420
  55.3 2.3 %fast_step.4 = (f32[32,3,128]{2,1,0:T(4,128)}, f32[3,128]{1,0:T(4,128)}, f32[3,128]{1,0:T(4,128)S(1)}) custom-call(s32[1]{0:T(128)} %bitcast.own_ref, f32[32,3,128]{2,1,0:T(4,128)S(1)} %all-to-all-done.3.g_ref, f32[32,8,128]{2,1,0:T(8,128)S(1)} %get-tuple-element.25.table_ref, f32[16,128]{1,0:T(8,128)S(1)} %get-tuple-element.26.exm_ref, ...), custom_call_target="tpu_custom_call" | custom-call | flops 5242880 | bytes 131072 | tf_op jit(solution)/shard_map/fast_step/pallas_call | solution.py:154
  57.6 5.8 %all-to-all-start.4 = ((f32[32,3,128]{2,1,0:T(4,128)}), f32[32,3,128]{2,1,0:T(4,128)S(1)}, u32[]{:S(2)}, u32[]{:S(2)}) async-start(f32[32,3,128]{2,1,0:T(4,128)} %get-tuple-element.31), calls=%async_computation.4 | async-start | bytes 131072 | tf_op jit(solution)/shard_map/all_to_all | solution.py:453
  63.7 2.4 %collective-permute-start.5 = (f32[2,8,4,128]{3,2,1,0:T(4,128)S(1)}, f32[2,8,4,128]{3,2,1,0:T(4,128)S(1)}, u32[]{:S(2)}, u32[]{:S(2)}) collective-permute-start(f32[2,8,4,128]{3,2,1,0:T(4,128)S(1)} %bitcast.29), channel_id=1, source_target_pairs={{4,0},{8,4},{12,8},{16,12},{20,16},{24,20},{28,24},{0,28},{5,1},{9... | collective-permute-start | bytes 98312 | tf_op jit(solution)/shard_map/ppermute | solution.py:447
  66.1 4.8 %all-to-all-done.4.g_ref = f32[32,3,128]{2,1,0:T(4,128)S(1)} async-done(((f32[32,3,128]{2,1,0:T(4,128)}), f32[32,3,128]{2,1,0:T(4,128)S(1)}, u32[]{:S(2)}, u32[]{:S(2)}) %all-to-all-start.4) | async-done | bytes 49184 | tf_op jit(solution)/shard_map/all_to_all | solution.py:453
  70.9 2.3 %fast_step.5 = (f32[32,3,128]{2,1,0:T(4,128)}, f32[3,128]{1,0:T(4,128)}, f32[3,128]{1,0:T(4,128)S(1)}) custom-call(s32[1]{0:T(128)} %bitcast.own_ref, f32[32,3,128]{2,1,0:T(4,128)S(1)} %all-to-all-done.4.g_ref, f32[32,8,128]{2,1,0:T(8,128)S(1)} %get-tuple-element.25.table_ref, f32[16,128]{1,0:T(8,128)S(1)} %get-tuple-element.26.exm_ref, ...), custom_call_target="tpu_custom_call" | custom-call | flops 5242880 | bytes 131072 | tf_op jit(solution)/shard_map/fast_step/pallas_call | solution.py:154
  73.3 2.5 %all-to-all-start.5 = ((f32[32,3,128]{2,1,0:T(4,128)}), f32[32,3,128]{2,1,0:T(4,128)S(1)}, u32[]{:S(2)}, u32[]{:S(2)}) async-start(f32[32,3,128]{2,1,0:T(4,128)} %get-tuple-element.34), calls=%async_computation.5 | async-start | bytes 131072 | tf_op jit(solution)/shard_map/all_to_all | solution.py:453
  75.9 1.7 %collective-permute-start.6 = (f32[8,2,4,128]{3,2,1,0:T(4,128)S(1)}, f32[8,2,4,128]{3,2,1,0:T(4,128)S(1)}, u32[]{:S(2)}, u32[]{:S(2)}) collective-permute-start(f32[8,2,4,128]{3,2,1,0:T(4,128)S(1)} %get-tuple-element.42), channel_id=1, source_target_pairs={{0,1},{1,2},{2,3},{3,0},{4,5},{5,6},{6,7},{7,4},{8,9},{9,10},{10,1... | collective-permute-start | bytes 98312 | tf_op jit(solution)/shard_map/ppermute | solution.py:446
  77.6 2.1 %collective-permute-start.7 = (f32[8,2,4,128]{3,2,1,0:T(4,128)S(1)}, f32[8,2,4,128]{3,2,1,0:T(4,128)S(1)}, u32[]{:S(2)}, u32[]{:S(2)}) collective-permute-start(f32[8,2,4,128]{3,2,1,0:T(4,128)S(1)} %get-tuple-element.43), channel_id=1, source_target_pairs={{1,0},{2,1},{3,2},{0,3},{5,4},{6,5},{7,6},{4,7},{9,8},{10,9},{11,1... | collective-permute-start | bytes 98312 | tf_op jit(solution)/shard_map/ppermute | solution.py:447
  79.7 3.9 %all-to-all-done.5.g_ref = f32[32,3,128]{2,1,0:T(4,128)S(1)} async-done(((f32[32,3,128]{2,1,0:T(4,128)}), f32[32,3,128]{2,1,0:T(4,128)S(1)}, u32[]{:S(2)}, u32[]{:S(2)}) %all-to-all-start.5) | async-done | bytes 49184 | tf_op jit(solution)/shard_map/all_to_all | solution.py:453
  83.6 2.3 %env.3 = f32[32,3,128]{2,1,0:T(4,128)} custom-call(s32[260]{0:T(512)S(1)} %get-tuple-element.23.list_ref, s32[1]{0:T(128)} %get-tuple-element.24.count_ref, f32[32,3,128]{2,1,0:T(4,128)S(1)} %all-to-all-done.5.g_ref, f32[32,4,128]{2,1,0:T(4,128)S(1)} %get-tuple-element.38.cells_ref), custom_call_target="tpu_custom_call" | custom-call | flops 2000000 | bytes 200000 | tf_op jit(solution)/shard_map/env/pallas_call | solution.py:262
  85.9 2.5 %all-to-all-start.6 = ((f32[32,3,128]{2,1,0:T(4,128)}), f32[32,3,128]{2,1,0:T(4,128)S(1)}, u32[]{:S(2)}, u32[]{:S(2)}) async-start(f32[32,3,128]{2,1,0:T(4,128)} %env.3), calls=%async_computation.6 | async-start | bytes 131072 | tf_op jit(solution)/shard_map/all_to_all | solution.py:453
  88.6 4.2 %slow.6.refs_0_ = f32[3,2,8,128]{3,2,1,0:T(8,128)S(1)} custom-call(s32[32,5]{1,0:T(8,128)S(1)} %bitcast.25, f32[8,12,4,128]{3,2,1,0:T(4,128)S(1)} %pad_maximum_fusion.1.tab_ref, f32[3,4,8,128]{3,2,1,0:T(8,128)S(1)} %get-tuple-element.41.vel_ref), custom_call_target="tpu_custom_call" | custom-call | flops 13107200 | bytes 1000000 | tf_op jit(solution)/shard_map/slow/pallas_call | solution.py:420
  92.8 4.8 %slow.7 = f32[3,4,8,128]{3,2,1,0:T(8,128)} custom-call(s32[32,5]{1,0:T(8,128)S(1)} %bitcast.26, f32[8,12,4,128]{3,2,1,0:T(4,128)S(1)} %pad_maximum_fusion.1.tab_ref, f32[3,4,8,128]{3,2,1,0:T(8,128)S(1)} %get-tuple-element.41.vel_ref, f32[3,2,8,128]{3,2,1,0:T(8,128)S(1)} %slow.6.refs_0_), custom_call_target="tpu_custom_call" | custom-call | flops 13107200 | bytes 1000000 | tf_op jit(solution)/shard_map/slow/pallas_call | solution.py:420
  97.6 1.7 %fast_only.3.f_ref = f32[3,128]{1,0:T(4,128)S(1)} custom-call(s32[1]{0:T(128)} %bitcast.own_ref, f32[32,3,128]{2,1,0:T(4,128)S(1)} %all-to-all-done.5.g_ref, f32[32,8,128]{2,1,0:T(8,128)S(1)} %get-tuple-element.25.table_ref, f32[16,128]{1,0:T(8,128)S(1)} %get-tuple-element.26.exm_ref), custom_call_target="tpu_custom_call" | custom-call | flops 5242880 | bytes 131072 | tf_op jit(solution)/shard_map/fast_only/pallas_call | solution.py:140
  (42 shorter events, 3.8 us)
Async XLA Ops:
  1.9 7.3 %copy-start.7 = (f32[3,4,8,128]{3,2,1,0:T(8,128)S(1)}, f32[3,4,8,128]{3,2,1,0:T(8,128)}, u32[]{:S(2)}) copy-start(f32[3,4,8,128]{3,2,1,0:T(8,128)} %param.14) | copy-start | bytes 147460
  1.9 14.8 %all-to-all-start = ((f32[32,3,128]{2,1,0:T(4,128)}), f32[32,3,128]{2,1,0:T(4,128)S(1)}, u32[]{:S(2)}, u32[]{:S(2)}) async-start(f32[32,3,128]{2,1,0:T(4,128)} %broadcast_in_dim.4), calls=%async_computation | async-start | bytes 131072 | tf_op jit(solution)/shard_map/all_to_all | solution.py:453
  9.3 0.7 copy-start.6
  10.0 0.7 copy-start.1
  10.0 0.9 copy-start.2
  10.1 0.8 copy-start
  19.1 10.2 %all-to-all-start.1 = ((f32[32,3,128]{2,1,0:T(4,128)}), f32[32,3,128]{2,1,0:T(4,128)S(1)}, u32[]{:S(2)}, u32[]{:S(2)}) async-start(f32[32,3,128]{2,1,0:T(4,128)} %env.2), calls=%async_computation.1 | async-start | bytes 131072 | tf_op jit(solution)/shard_map/all_to_all | solution.py:453
  21.9 10.7 %collective-permute-start = (f32[2,8,4,128]{3,2,1,0:T(4,128)S(1)}, f32[2,8,4,128]{3,2,1,0:T(4,128)S(1)}, u32[]{:S(2)}, u32[]{:S(2)}) collective-permute-start(f32[2,8,4,128]{3,2,1,0:T(4,128)S(1)} %get-tuple-element.48), channel_id=1, source_target_pairs={{0,4},{4,8},{8,12},{12,16},{16,20},{20,24},{24,28},{28,0},{1,5},{5... | collective-permute-start | bytes 98312 | tf_op jit(solution)/shard_map/ppermute | solution.py:446
  22.2 10.4 %collective-permute-start.1 = (f32[2,8,4,128]{3,2,1,0:T(4,128)S(1)}, f32[2,8,4,128]{3,2,1,0:T(4,128)S(1)}, u32[]{:S(2)}, u32[]{:S(2)}) collective-permute-start(f32[2,8,4,128]{3,2,1,0:T(4,128)S(1)} %get-tuple-element.49), channel_id=1, source_target_pairs={{4,0},{8,4},{12,8},{16,12},{20,16},{24,20},{28,24},{0,28},{5,1},{9... | collective-permute-start | bytes 98312 | tf_op jit(solution)/shard_map/ppermute | solution.py:447
  24.6 4.8 %copy-start.3 = (f32[3,128]{1,0:T(4,128)S(1)}, f32[3,128]{1,0:T(4,128)}, u32[]{:S(2)}) copy-start(f32[3,128]{1,0:T(4,128)} %p_ref.1) | copy-start | bytes 4612
  24.6 4.8 %copy-start.4 = (f32[3,128]{1,0:T(4,128)S(1)}, f32[3,128]{1,0:T(4,128)}, u32[]{:S(2)}) copy-start(f32[3,128]{1,0:T(4,128)} %v_ref.1) | copy-start | bytes 4612
  30.0 10.4 %all-to-all-start.2 = ((f32[32,3,128]{2,1,0:T(4,128)}), f32[32,3,128]{2,1,0:T(4,128)S(1)}, u32[]{:S(2)}, u32[]{:S(2)}) async-start(f32[32,3,128]{2,1,0:T(4,128)} %get-tuple-element.27), calls=%async_computation.2 | async-start | bytes 131072 | tf_op jit(solution)/shard_map/all_to_all | solution.py:453
  32.6 3.9 %copy-start.8 = (s32[4,8,5]{1,0,2:T(4,128)S(1)}, s32[4,8,5]{1,0,2:T(4,128)}, u32[]{:S(2)}) copy-start(s32[4,8,5]{1,0,2:T(4,128)} %param.17) | copy-start | bytes 1924
  32.7 12.6 %collective-permute-start.2 = (f32[8,2,4,128]{3,2,1,0:T(4,128)S(1)}, f32[8,2,4,128]{3,2,1,0:T(4,128)S(1)}, u32[]{:S(2)}, u32[]{:S(2)}) collective-permute-start(f32[8,2,4,128]{3,2,1,0:T(4,128)S(1)} %get-tuple-element.44), channel_id=1, source_target_pairs={{0,1},{1,2},{2,3},{3,0},{4,5},{5,6},{6,7},{7,4},{8,9},{9,10},{10,1... | collective-permute-start | bytes 98312 | tf_op jit(solution)/shard_map/ppermute | solution.py:446
  34.4 10.9 %collective-permute-start.3 = (f32[8,2,4,128]{3,2,1,0:T(4,128)S(1)}, f32[8,2,4,128]{3,2,1,0:T(4,128)S(1)}, u32[]{:S(2)}, u32[]{:S(2)}) collective-permute-start(f32[8,2,4,128]{3,2,1,0:T(4,128)S(1)} %get-tuple-element.45), channel_id=1, source_target_pairs={{1,0},{2,1},{3,2},{0,3},{5,4},{6,5},{7,6},{4,7},{9,8},{10,9},{11,1... | collective-permute-start | bytes 98312 | tf_op jit(solution)/shard_map/ppermute | solution.py:447
  42.7 12.5 %all-to-all-start.3 = ((f32[32,3,128]{2,1,0:T(4,128)}), f32[32,3,128]{2,1,0:T(4,128)S(1)}, u32[]{:S(2)}, u32[]{:S(2)}) async-start(f32[32,3,128]{2,1,0:T(4,128)} %get-tuple-element.29), calls=%async_computation.3 | async-start | bytes 131072 | tf_op jit(solution)/shard_map/all_to_all | solution.py:453
  45.3 0.8 copy-start.5
  57.6 13.3 %all-to-all-start.4 = ((f32[32,3,128]{2,1,0:T(4,128)}), f32[32,3,128]{2,1,0:T(4,128)S(1)}, u32[]{:S(2)}, u32[]{:S(2)}) async-start(f32[32,3,128]{2,1,0:T(4,128)} %get-tuple-element.31), calls=%async_computation.4 | async-start | bytes 131072 | tf_op jit(solution)/shard_map/all_to_all | solution.py:453
  63.4 12.4 %collective-permute-start.4 = (f32[2,8,4,128]{3,2,1,0:T(4,128)S(1)}, f32[2,8,4,128]{3,2,1,0:T(4,128)S(1)}, u32[]{:S(2)}, u32[]{:S(2)}) collective-permute-start(f32[2,8,4,128]{3,2,1,0:T(4,128)S(1)} %bitcast.30), channel_id=1, source_target_pairs={{0,4},{4,8},{8,12},{12,16},{16,20},{20,24},{24,28},{28,0},{1,5},{5... | collective-permute-start | bytes 98312 | tf_op jit(solution)/shard_map/ppermute | solution.py:446
  63.7 12.1 %collective-permute-start.5 = (f32[2,8,4,128]{3,2,1,0:T(4,128)S(1)}, f32[2,8,4,128]{3,2,1,0:T(4,128)S(1)}, u32[]{:S(2)}, u32[]{:S(2)}) collective-permute-start(f32[2,8,4,128]{3,2,1,0:T(4,128)S(1)} %bitcast.29), channel_id=1, source_target_pairs={{4,0},{8,4},{12,8},{16,12},{20,16},{24,20},{28,24},{0,28},{5,1},{9... | collective-permute-start | bytes 98312 | tf_op jit(solution)/shard_map/ppermute | solution.py:447
  73.3 10.4 %all-to-all-start.5 = ((f32[32,3,128]{2,1,0:T(4,128)}), f32[32,3,128]{2,1,0:T(4,128)S(1)}, u32[]{:S(2)}, u32[]{:S(2)}) async-start(f32[32,3,128]{2,1,0:T(4,128)} %get-tuple-element.34), calls=%async_computation.5 | async-start | bytes 131072 | tf_op jit(solution)/shard_map/all_to_all | solution.py:453
  75.9 12.6 %collective-permute-start.6 = (f32[8,2,4,128]{3,2,1,0:T(4,128)S(1)}, f32[8,2,4,128]{3,2,1,0:T(4,128)S(1)}, u32[]{:S(2)}, u32[]{:S(2)}) collective-permute-start(f32[8,2,4,128]{3,2,1,0:T(4,128)S(1)} %get-tuple-element.42), channel_id=1, source_target_pairs={{0,1},{1,2},{2,3},{3,0},{4,5},{5,6},{6,7},{7,4},{8,9},{9,10},{10,1... | collective-permute-start | bytes 98312 | tf_op jit(solution)/shard_map/ppermute | solution.py:446
  77.6 10.9 %collective-permute-start.7 = (f32[8,2,4,128]{3,2,1,0:T(4,128)S(1)}, f32[8,2,4,128]{3,2,1,0:T(4,128)S(1)}, u32[]{:S(2)}, u32[]{:S(2)}) collective-permute-start(f32[8,2,4,128]{3,2,1,0:T(4,128)S(1)} %get-tuple-element.43), channel_id=1, source_target_pairs={{1,0},{2,1},{3,2},{0,3},{5,4},{6,5},{7,6},{4,7},{9,8},{10,9},{11,1... | collective-permute-start | bytes 98312 | tf_op jit(solution)/shard_map/ppermute | solution.py:447
  85.9 13.3 %all-to-all-start.6 = ((f32[32,3,128]{2,1,0:T(4,128)}), f32[32,3,128]{2,1,0:T(4,128)S(1)}, u32[]{:S(2)}, u32[]{:S(2)}) async-start(f32[32,3,128]{2,1,0:T(4,128)} %env.3), calls=%async_computation.6 | async-start | bytes 131072 | tf_op jit(solution)/shard_map/all_to_all | solution.py:453

commit v5 on v4

--- a/solution.py
+++ b/solution.py
@@ -23,6 +23,16 @@
 BF16 = jnp.bfloat16
 LANES = 128
 ENV_UNROLL = 4
+
+
+def in_hbm(x):
+    return pltpu.with_memory_space_constraint(x, pltpu.HBM)
+
+
+def position():
+    return lax.axis_index("row") * lax.axis_size("col") + lax.axis_index("col")
+
+
 VMEM = pl.BlockSpec(memory_space=pltpu.VMEM)
 SMEM = pl.BlockSpec(memory_space=pltpu.SMEM)
 
@@ -101,16 +111,16 @@
     ]
 
 
-def fast_only_kernel(own_ref, g_ref, table_ref, exm_ref, f_ref, *scratch):
-    rows = fast_rows(g_ref, table_ref, exm_ref, own_ref[0], *scratch)
+def fast_only_kernel(g_ref, table_ref, exm_ref, f_ref, *scratch):
+    rows = fast_rows(g_ref, table_ref, exm_ref, position(), *scratch)
     for c in range(3):
         f_ref[c : c + 1, :] = rows[c]
 
 
 def fast_step_kernel(
-    own_ref, g_ref, table_ref, exm_ref, v_ref, send_ref, p_out, v_out, *scratch
+    g_ref, table_ref, exm_ref, v_ref, send_ref, p_out, v_out, *scratch
 ):
-    own = own_ref[0]
+    own = position()
     rows = fast_rows(g_ref, table_ref, exm_ref, own, *scratch)
     count = send_ref.shape[0]
     for c in range(3):
@@ -135,61 +145,62 @@
     ]
 
 
-def fast_only(own, g, table, exm):
+def fast_only(g, table, exm):
     count = g.shape[0]
     return pl.pallas_call(
         fast_only_kernel,
         out_shape=sds((3, LANES)),
-        in_specs=[SMEM] + [VMEM] * 3,
+        in_specs=[VMEM] * 3,
         out_specs=VMEM,
         scratch_shapes=fast_scratch(count),
         cost_estimate=fast_cost(count),
         name="fast_only",
         compiler_params=pltpu.CompilerParams(vmem_limit_bytes=4 << 20),
-    )(own, g, table, exm)
-
-
-def fast_step(own, g, table, exm, v):
+    )(g, table, exm)
+
+
+def fast_step(g, table, exm, v):
     count = g.shape[0]
     return pl.pallas_call(
         fast_step_kernel,
         out_shape=(sds((count, 3, LANES)), sds((3, LANES)), sds((3, LANES))),
-        in_specs=[SMEM] + [VMEM] * 4,
+        in_specs=[VMEM] * 4,
         out_specs=(VMEM,) * 3,
         scratch_shapes=fast_scratch(count),
         cost_estimate=fast_cost(count),
         name="fast_step",
         compiler_params=pltpu.CompilerParams(vmem_limit_bytes=4 << 20),
-    )(own, g, table, exm, v)
+    )(g, table, exm, v)
 
 
 def prep_kernel(
-    grid, place_ref, owner_smem, owner_ref, q_ref, ex_ref, table_ref, exm_ref, list_ref, count_ref
+    grid, owner_hbm, q_hbm, ex_hbm, table_ref, exm_ref, list_ref,
+    heads, owner_ref, q_ref, ex_ref, sems,
 ):
     total_cols, cell_rows, cell_cols = grid
-    own, row_index, col_index = place_ref[0], place_ref[1], place_ref[2]
-    owner = owner_ref[...]
+    mine = pl.ds(pl.multiple_of(position() * LANES, LANES), LANES)
+    first = pltpu.make_async_copy(owner_hbm.at[0 : heads.shape[0]], heads, sems.at[3])
+    first.start()
+    copies = [
+        pltpu.make_async_copy(owner_hbm, owner_ref, sems.at[0]),
+        pltpu.make_async_copy(q_hbm, q_ref, sems.at[1]),
+        pltpu.make_async_copy(ex_hbm.at[:, mine], ex_ref, sems.at[2]),
+    ]
+    for copy in copies:
+        copy.start()
     table_ref[...] = jnp.zeros_like(table_ref)
-    table_ref[:, 0, :] = (lax.div(owner, total_cols) - total_cols // 2).astype(F32)
-    table_ref[:, 1, :] = (lax.rem(owner, total_cols) - total_cols // 2).astype(F32)
-    table_ref[:, 3, :] = q_ref[...]
-    ex = ex_ref[:, pl.ds(pl.multiple_of(own * LANES, LANES), LANES)]
-    ex = lax.div(ex, GROUPS)
-    member = lax.broadcasted_iota(jnp.int32, exm_ref.shape, 0)
-    barred = jnp.zeros(exm_ref.shape, F32)
-    for k in range(ex_ref.shape[0]):
-        barred = jnp.where(member == ex[k : k + 1], 1.0, barred)
-    exm_ref[...] = barred
     row_bit = total_cols * cell_rows
     keep = -row_bit | (total_cols - cell_cols)
-    here = row_index * row_bit + col_index * cell_cols
+    here = lax.axis_index("row") * row_bit + lax.axis_index("col") * cell_cols
     unroll = 16
 
     def body(j, n):
         found = []
+        row = lax.shift_right_logical(j * unroll, LANES.bit_length() - 1)
+        col = (j * unroll) & (LANES - 1)
         for u in range(unroll):
             i = j * unroll + u
-            cell = owner_smem[i]
+            cell = heads[row, col + u]
             other = (cell & keep) ^ here
             found.append((cell * GROUPS + i, lax.shift_right_logical(other - 1, 31)))
         for entry, inside in found:
@@ -197,28 +208,50 @@
             n = n + inside
         return n
 
+    first.wait()
     n = lax.fori_loop(0, GROUPS // unroll, body, jnp.int32(0))
-    count_ref[0] = n
     for k in range(ENV_UNROLL):
         list_ref[n + k] = -1
-
-
-def prep(place, owner, q, exclusions, members, grid):
+    list_ref[GROUPS + ENV_UNROLL] = n
+    for copy in copies:
+        copy.wait()
+    owner = owner_ref[...]
+    shift = total_cols.bit_length() - 1
+    table_ref[:, 0, :] = (lax.shift_right_logical(owner, shift) - total_cols // 2).astype(F32)
+    table_ref[:, 1, :] = ((owner & (total_cols - 1)) - total_cols // 2).astype(F32)
+    table_ref[:, 3, :] = q_ref[...]
+    ex = lax.shift_right_logical(ex_ref[...], GROUPS.bit_length() - 1)
+    member = lax.broadcasted_iota(jnp.int32, exm_ref.shape, 0)
+    barred = jnp.zeros(exm_ref.shape, F32)
+    for k in range(ex_ref.shape[0]):
+        barred = jnp.where(member == ex[k : k + 1], 1.0, barred)
+    exm_ref[...] = barred
+
+
+def prep(owner, q, exclusions, members, grid):
     count = owner.shape[0] // LANES
+    hbm = pl.BlockSpec(memory_space=pltpu.HBM)
     return pl.pallas_call(
         functools.partial(prep_kernel, grid),
         out_shape=(
             sds((count, 8, LANES)), sds((members, LANES)),
-            sds((GROUPS + ENV_UNROLL,), jnp.int32), sds((1,), jnp.int32),
+            sds((GROUPS + ENV_UNROLL + 1,), jnp.int32),
         ),
-        in_specs=[SMEM, SMEM, VMEM, VMEM, VMEM],
-        out_specs=(VMEM, VMEM, SMEM, SMEM),
+        in_specs=[hbm, hbm, hbm],
+        out_specs=(VMEM, VMEM, SMEM),
+        scratch_shapes=[
+            pltpu.SMEM((8 * pl.cdiv(GROUPS, 8 * LANES), LANES), jnp.int32),
+            pltpu.VMEM((count, LANES), jnp.int32),
+            pltpu.VMEM((count, LANES), F32),
+            pltpu.VMEM((exclusions.shape[1], LANES), jnp.int32),
+            pltpu.SemaphoreType.DMA((4,)),
+        ],
         name="prep",
         compiler_params=pltpu.CompilerParams(vmem_limit_bytes=2 << 20),
-    )(place, owner, owner.reshape(count, LANES), q, exclusions.T)
-
-
-def env_kernel(grid, list_ref, count_ref, g_ref, cells_ref, out_ref, planes, sums):
+    )(*(in_hbm(x) for x in (owner.reshape(count, LANES), q, exclusions.T)))
+
+
+def env_kernel(grid, list_ref, g_ref, cells_ref, out_ref, planes, sums):
     total_cols, cell_rows, cell_cols = grid
     step = GROUPS // LANES
     members = g_ref.shape[0] // step
@@ -249,20 +282,20 @@
                 sums[c, h] = sums[c, h] + jnp.where(here, f, 0.0)
         return carry
 
-    lax.fori_loop(0, lax.div(count_ref[0] + (ENV_UNROLL - 1), ENV_UNROLL), body, 0)
+    lax.fori_loop(0, lax.div(list_ref[GROUPS + ENV_UNROLL] + (ENV_UNROLL - 1), ENV_UNROLL), body, 0)
     for c in range(3):
         for h in range(step):
             out_ref[pl.ds(h, members, stride=step), c, :] = sums[c, h]
 
 
-def env(lists, g, cells, grid):
+def env(groups, g, cells, grid):
     count = g.shape[0]
     step = GROUPS // LANES
     members = count // step
     return pl.pallas_call(
         functools.partial(env_kernel, grid),
         out_shape=sds((count, 3, LANES)),
-        in_specs=[SMEM, SMEM, VMEM, VMEM],
+        in_specs=[SMEM, VMEM, VMEM],
         out_specs=VMEM,
         scratch_shapes=[
             pltpu.VMEM((3, step, members, LANES), F32),
@@ -271,11 +304,11 @@
         cost_estimate=pl.CostEstimate(flops=2_000_000, transcendentals=60000, bytes_accessed=200000),
         name="env",
         compiler_params=pltpu.CompilerParams(vmem_limit_bytes=2 << 20),
-    )(*lists, g, cells)
-
-
-def kick_kernel(own_ref, e_ref, f_ref, q_ref, p_ref, v_ref, send_ref, p_out, v_out):
-    scale = slow_coupling * q_ref[pl.ds(own_ref[0], 1), :]
+    )(groups, g, cells)
+
+
+def kick_kernel(e_ref, f_ref, q_ref, p_ref, v_ref, send_ref, p_out, v_out):
+    scale = slow_coupling * q_ref[pl.ds(position(), 1), :]
     count = send_ref.shape[0]
     for c in range(3):
         e = scale * jnp.sum(e_ref[:, c, :], axis=0, keepdims=True)
@@ -286,20 +319,20 @@
         send_ref[:, c, :] = jnp.broadcast_to(p, (count, LANES))
 
 
-def kick(own, e, f, q, p, v):
+def kick(e, f, q, p, v):
     count = e.shape[0]
     return pl.pallas_call(
         kick_kernel,
         out_shape=(sds((count, 3, LANES)), sds((3, LANES)), sds((3, LANES))),
-        in_specs=[SMEM] + [VMEM] * 5,
+        in_specs=[VMEM] * 5,
         out_specs=(VMEM,) * 3,
         name="kick",
         compiler_params=pltpu.CompilerParams(vmem_limit_bytes=2 << 20),
-    )(own, e, f, q, p, v)
-
-
-def last_kick_kernel(own_ref, e_ref, f_ref, q_ref, v_ref, v_out):
-    scale = slow_coupling * q_ref[pl.ds(own_ref[0], 1), :]
+    )(e, f, q, p, v)
+
+
+def last_kick_kernel(e_ref, f_ref, q_ref, v_ref, v_out):
+    scale = slow_coupling * q_ref[pl.ds(position(), 1), :]
     for c in range(3):
         e = scale * jnp.sum(e_ref[:, c, :], axis=0, keepdims=True)
         v_out[c : c + 1, :] = (
@@ -307,15 +340,15 @@
         )
 
 
-def last_kick(own, e, f, q, v):
+def last_kick(e, f, q, v):
     return pl.pallas_call(
         last_kick_kernel,
         out_shape=sds((3, LANES)),
-        in_specs=[SMEM] + [VMEM] * 4,
+        in_specs=[VMEM] * 4,
         out_specs=VMEM,
         name="last_kick",
         compiler_params=pltpu.CompilerParams(vmem_limit_bytes=2 << 20),
-    )(own, e, f, q, v)
+    )(e, f, q, v)
 
 
 def slow_kernel(first, row0, nb_ref, tab_ref, vel_ref, *refs):
@@ -323,6 +356,10 @@
     if row0:
         before, refs = refs[:results], refs[results:]
     outs, scratch = refs[:results], refs[results:]
+    totals = scratch[8]
+    if first:
+        fetch = pltpu.make_async_copy(vel_ref.at[:, row0 : outs[0].shape[1]], scratch[9], scratch[10])
+        fetch.start()
     vel_out = outs[0]
     if first:
         pos_out, cell_out = outs[1:]
@@ -339,7 +376,7 @@
     row8 = lax.broadcasted_iota(jnp.int32, (8, CELL), 0)
 
     def place(n):
-        return lax.div(n, cell_cols), lax.rem(n, cell_cols)
+        return lax.shift_right_logical(n, cell_cols.bit_length() - 1), n & (cell_cols - 1)
 
     def load8(r, c):
         t = tab_ref[r, c]
@@ -351,7 +388,8 @@
         left = jnp.transpose(left_rows(load8(r + (row0 + 2), c + 2))).astype(BF16)
         for k in range(slots):
             o = nb_ref[n + row0 * cell_cols, k]
-            dr, dc = lax.div(o, 5), lax.rem(o, 5)
+            dr = lax.shift_right_logical(o * 13, 6)
+            dc = o - 5 * dr
             y = load8(r + (dr + row0), c + dc)
             y = y + jnp.where(
                 row8 == 0, (dr - 2).astype(F32), jnp.where(row8 == 1, (dc - 2).astype(F32), 0.0)
@@ -378,20 +416,8 @@
 
     def finish(n, buf):
         sums = buf[3]
-        r, c = place(n)
-        t = tab_ref[r + (row0 + 2), c + 2]
-        total = [jnp.sum(jnp.transpose(sums[x]), axis=0, keepdims=True) for x in range(4)]
-        scale = slow_coupling * t[3:4]
-        for x in range(3):
-            f = scale * (t[x : x + 1] * total[3] - total[x])
-            v = vel_ref[x, r + row0, pl.ds(c, 1), :] + half_outer * f
-            vel_out[x, r + row0, pl.ds(c, 1), :] = v
-            if first:
-                p = t[x : x + 1] + outer_dt * v
-                pos_out[x, r + row0, pl.ds(c, 1), :] = p
-                cell_out[n + skip, x : x + 1, :] = p
-        if first:
-            cell_out[n + skip, 3:4, :] = t[3:4]
+        for x in range(4):
+            totals[n, x : x + 1, :] = jnp.sum(jnp.transpose(sums[x]), axis=0, keepdims=True)
 
     distances(0, bufs[0])
 
@@ -407,6 +433,22 @@
 
     lax.fori_loop(0, count // 2, body, 0)
     finish(count - 1, bufs[1])
+    if first:
+        fetch.wait()
+    rows = slice(row0, row0 + cell_rows)
+    inner = (slice(row0 + 2, row0 + 2 + cell_rows), slice(2, 2 + cell_cols))
+    charge = tab_ref[inner[0], inner[1], 3, :].reshape(count, CELL)
+    for x in range(3):
+        p = tab_ref[inner[0], inner[1], x, :].reshape(count, CELL)
+        f = slow_coupling * charge * (p * totals[:, 3, :] - totals[:, x, :])
+        v = (scratch[9][x] if first else vel_ref[x, rows]) + half_outer * f.reshape(cell_rows, cell_cols, CELL)
+        vel_out[x, rows] = v
+        if first:
+            p = p + outer_dt * v.reshape(count, CELL)
+            pos_out[x, rows] = p.reshape(cell_rows, cell_cols, CELL)
+            cell_out[skip:, x, :] = p
+    if first:
+        cell_out[skip:, 3, :] = charge
 
 
 def slow(first, row0, rows, nb, tab, vel, before=()):
@@ -420,20 +462,22 @@
     return pl.pallas_call(
         functools.partial(slow_kernel, first, row0),
         out_shape=out,
-        in_specs=[SMEM] + [VMEM] * (2 + len(before)),
+        in_specs=[SMEM, VMEM, pl.BlockSpec(memory_space=pltpu.HBM) if first else VMEM]
+        + [VMEM] * len(before),
         out_specs=(VMEM,) * len(out),
         scratch_shapes=[
             pltpu.VMEM((48, slots * CELL), BF16),
             pltpu.VMEM((8 * slots, CELL), F32),
             pltpu.VMEM((CELL, slots * CELL), F32),
             pltpu.VMEM((4, CELL, CELL), F32),
-        ] * 2,
+        ] * 2 + [pltpu.VMEM((own, 4, CELL), F32)]
+        + ([pltpu.VMEM((3, rows) + vel.shape[2:], F32), pltpu.SemaphoreType.DMA] if first else []),
         compiler_params=pltpu.CompilerParams(vmem_limit_bytes=4 << 20),
         cost_estimate=pl.CostEstimate(
             flops=10 * pairs, transcendentals=pairs, bytes_accessed=1_000_000
         ),
         name="slow",
-    )(nb, tab, vel, *before)
+    )(nb, tab, in_hbm(vel) if first else vel, *before)
 
 
 def with_halo(x, sides, width):
@@ -462,21 +506,17 @@
     slow_pos, slow_vel, slow_charge, neighbours,
 ):
     row_count, col_count = lax.axis_size("row"), lax.axis_size("col")
-    row_index, col_index = lax.axis_index("row"), lax.axis_index("col")
-    flat = row_index * col_count + col_index
     count = row_count * col_count
     piece = fast_pos.shape[1]
     cell_rows, cell_cols = slow_pos.shape[1], slow_pos.shape[2]
     total_cols = cell_cols * col_count
-    own = jnp.reshape(flat, (1,)).astype(jnp.int32)
 
     g = exchange(jnp.broadcast_to(fast_pos[None], (count, 3, piece)))
 
     q = fast_charge.reshape(count, piece)
     members = fast_charge.shape[0] // GROUPS
-    place = jnp.stack([flat, row_index, col_index]).astype(jnp.int32)
     grid = (total_cols, cell_rows, cell_cols)
-    table, exm, *lists = prep(place, fast_owner, q, exclusions, members, grid)
+    table, exm, groups = prep(fast_owner, q, exclusions, members, grid)
 
     cells = jnp.concatenate([slow_pos, slow_charge[None]], axis=0).transpose(1, 2, 0, 3)
     sides = (("row", 0), ("col", 1))
@@ -493,16 +533,16 @@
         part = slow(False, r0, half, nb, tab2, slow_vel, part)
     (slow_vel,) = part
 
-    back = exchange(env(lists, g, cells.reshape(cells2.shape), grid))
-    f = fast_only(own, g, table, exm)
-    send, p, v = kick(own, back, f, q, fast_pos, fast_vel)
+    back = exchange(env(groups, g, cells.reshape(cells2.shape), grid))
+    f = fast_only(g, table, exm)
+    send, p, v = kick(back, f, q, fast_pos, fast_vel)
     for _ in range(INNER - 1):
         g = exchange(send)
-        send, p, v = fast_step(own, g, table, exm, v)
+        send, p, v = fast_step(g, table, exm, v)
     g = exchange(send)
-    back = exchange(env(lists, g, cells2, grid))
-    f = fast_only(own, g, table, exm)
-    v = last_kick(own, back, f, q, v)
+    back = exchange(env(groups, g, cells2, grid))
+    f = fast_only(g, table, exm)
+    v = last_kick(back, f, q, v)
     return (p, v, slow_pos, slow_vel)
 
 

time: 101 us -> 98.4 us (0.974)
  local copies, waits for them, and re-layouts: 3.59 us -> 2.16 us
    unnamed x20 -> x14, local copies, waits for them, and re-layouts: 2.26 us -> 0.82 us
    pallas_call x2, Pallas kernels: 4.62 us -> 3.33 us  [env(): pl.pallas_call(functools.partial(env_kernel, grid), out_shape=sds((count,...]
where the time goes in v5:
time: 98.4 us; the launch traced here: 97.8 us
  starting transfers between devices  39.1 us (40%)
  Pallas kernels  36 us (37%)
  waiting for transfers between devices  19.4 us (20%)
  local copies, waits for them, and re-layouts  2.16 us (2%)
    all_to_all x7, starting transfers between devices, exchange(): return lax.all_to_all(x, BOTH, 0, 0)  26 us
    all_to_all x7, waiting for transfers between devices, exchange(): return lax.all_to_all(x, BOTH, 0, 0)  19.3 us
    pallas_call x4, Pallas kernels, slow(): pl.pallas_call(functools.partial(slow_kernel, first, row0), out_shape=out...  18.2 us
    ppermute x4, starting transfers between devices, with_halo(): after = lax.ppermute(initial, axis, down)  9.2 us
    pallas_call x3, Pallas kernels, fast_step(): pl.pallas_call(fast_step_kernel, out_shape=(sds((count, 3, LANES)), sds((...  7 us
    ppermute x4, starting transfers between devices, with_halo(): before = lax.ppermute(last, axis, up)  3.95 us
    pallas_call x2, Pallas kernels, fast_only(): pl.pallas_call(fast_only_kernel, out_shape=sds((3, LANES)), in_specs=[VME...  3.34 us
    pallas_call x2, Pallas kernels, env(): pl.pallas_call(functools.partial(env_kernel, grid), out_shape=sds((count,...  3.33 us
  transfers between devices with their start and end apart: 15, of which 5 were waited for; matrix products, arithmetic and copies ran while one was open for 0% of the time, Pallas kernels for 32%

profile of v5, /device:TPU:0, one launch (start us, length us, event | category | flops | bytes accessed | tf_op | source)
XLA Modules:
  0.0 97.8 jit_solution(7724898354572733359)
XLA Ops:
  0.6 1.3 %broadcast_in_dim.4 = f32[32,3,128]{2,1,0:T(4,128)} broadcast(f32[3,128]{1,0:T(4,128)} %p_ref.1), dimensions={1,2} | broadcast | bytes 50688 | tf_op jit(solution)/shard_map/broadcast_in_dim | solution.py:514
  1.9 7.3 %all-to-all-start = ((f32[32,3,128]{2,1,0:T(4,128)}), f32[32,3,128]{2,1,0:T(4,128)S(1)}, u32[]{:S(2)}, u32[]{:S(2)}) async-start(f32[32,3,128]{2,1,0:T(4,128)} %broadcast_in_dim.4), calls=%async_computation | async-start | bytes 131072 | tf_op jit(solution)/shard_map/all_to_all | solution.py:497
  10.1 2.9 %prep.1 = (f32[32,8,128]{2,1,0:T(8,128)S(1)}, f32[16,128]{1,0:T(8,128)S(1)}, s32[261]{0:T(512)S(1)}) custom-call(s32[32,128]{1,0:T(8,128)} %bitcast.27, f32[32,128]{1,0:T(8,128)} %bitcast.15, s32[4,4096]{1,0:T(4,128)} %bitcast.24), custom_call_target="tpu_custom_call" | custom-call | tf_op jit(solution)/shard_map/prep/pallas_call | solution.py:234
  13.0 3.8 %all-to-all-done.g_ref = f32[32,3,128]{2,1,0:T(4,128)S(1)} async-done(((f32[32,3,128]{2,1,0:T(4,128)}), f32[32,3,128]{2,1,0:T(4,128)S(1)}, u32[]{:S(2)}, u32[]{:S(2)}) %all-to-all-start) | async-done | bytes 49184 | tf_op jit(solution)/shard_map/all_to_all | solution.py:497
  16.8 1.7 %env.2 = f32[32,3,128]{2,1,0:T(4,128)} custom-call(s32[261]{0:T(512)S(1)} %get-tuple-element.22.list_ref, f32[32,3,128]{2,1,0:T(4,128)S(1)} %all-to-all-done.g_ref, f32[32,4,128]{2,1,0:T(4,128)S(1)} %bitcast.14), custom_call_target="tpu_custom_call" | custom-call | flops 2000000 | bytes 200000 | tf_op jit(solution)/shard_map/env/pallas_call | solution.py:295
  18.4 2.6 %all-to-all-start.1 = ((f32[32,3,128]{2,1,0:T(4,128)}), f32[32,3,128]{2,1,0:T(4,128)S(1)}, u32[]{:S(2)}, u32[]{:S(2)}) async-start(f32[32,3,128]{2,1,0:T(4,128)} %env.2), calls=%async_computation.1 | async-start | bytes 131072 | tf_op jit(solution)/shard_map/all_to_all | solution.py:497
  21.2 2.5 %collective-permute-start.1 = (f32[2,8,4,128]{3,2,1,0:T(4,128)S(1)}, f32[2,8,4,128]{3,2,1,0:T(4,128)S(1)}, u32[]{:S(2)}, u32[]{:S(2)}) collective-permute-start(f32[2,8,4,128]{3,2,1,0:T(4,128)S(1)} %get-tuple-element.47), channel_id=1, source_target_pairs={{4,0},{8,4},{12,8},{16,12},{20,16},{24,20},{28,24},{0,28},{5,1},{9... | collective-permute-start | bytes 98312 | tf_op jit(solution)/shard_map/ppermute | solution.py:491
  23.7 1.7 %fast_only.2.f_ref = f32[3,128]{1,0:T(4,128)S(1)} custom-call(f32[32,3,128]{2,1,0:T(4,128)S(1)} %all-to-all-done.g_ref, f32[32,8,128]{2,1,0:T(8,128)S(1)} %get-tuple-element.23.table_ref, f32[16,128]{1,0:T(8,128)S(1)} %get-tuple-element.24.exm_ref), custom_call_target="tpu_custom_call" | custom-call | flops 5242880 | bytes 131072 | tf_op jit(solution)/shard_map/fast_only/pallas_call | solution.py:150
  25.4 3.1 %all-to-all-done.1.e_ref = f32[32,3,128]{2,1,0:T(4,128)S(1)} async-done(((f32[32,3,128]{2,1,0:T(4,128)}), f32[32,3,128]{2,1,0:T(4,128)S(1)}, u32[]{:S(2)}, u32[]{:S(2)}) %all-to-all-start.1) | async-done | bytes 49184 | tf_op jit(solution)/shard_map/all_to_all | solution.py:497
  28.5 0.7 kick.1
  29.2 2.6 %all-to-all-start.2 = ((f32[32,3,128]{2,1,0:T(4,128)}), f32[32,3,128]{2,1,0:T(4,128)S(1)}, u32[]{:S(2)}, u32[]{:S(2)}) async-start(f32[32,3,128]{2,1,0:T(4,128)} %get-tuple-element.25), calls=%async_computation.2 | async-start | bytes 131072 | tf_op jit(solution)/shard_map/all_to_all | solution.py:497
  31.9 1.7 %collective-permute-start.2 = (f32[8,2,4,128]{3,2,1,0:T(4,128)S(1)}, f32[8,2,4,128]{3,2,1,0:T(4,128)S(1)}, u32[]{:S(2)}, u32[]{:S(2)}) collective-permute-start(f32[8,2,4,128]{3,2,1,0:T(4,128)S(1)} %get-tuple-element.42), channel_id=1, source_target_pairs={{0,1},{1,2},{2,3},{3,0},{4,5},{5,6},{6,7},{7,4},{8,9},{9,10},{10,1... | collective-permute-start | bytes 98312 | tf_op jit(solution)/shard_map/ppermute | solution.py:490
  33.6 2.1 %collective-permute-start.3 = (f32[8,2,4,128]{3,2,1,0:T(4,128)S(1)}, f32[8,2,4,128]{3,2,1,0:T(4,128)S(1)}, u32[]{:S(2)}, u32[]{:S(2)}) collective-permute-start(f32[8,2,4,128]{3,2,1,0:T(4,128)S(1)} %get-tuple-element.43), channel_id=1, source_target_pairs={{1,0},{2,1},{3,2},{0,3},{5,4},{6,5},{7,6},{4,7},{9,8},{10,9},{11,1... | collective-permute-start | bytes 98312 | tf_op jit(solution)/shard_map/ppermute | solution.py:491
  35.8 3.8 %all-to-all-done.2.g_ref = f32[32,3,128]{2,1,0:T(4,128)S(1)} async-done(((f32[32,3,128]{2,1,0:T(4,128)}), f32[32,3,128]{2,1,0:T(4,128)S(1)}, u32[]{:S(2)}, u32[]{:S(2)}) %all-to-all-start.2) | async-done | bytes 49184 | tf_op jit(solution)/shard_map/all_to_all | solution.py:497
  39.6 2.3 %fast_step.3 = (f32[32,3,128]{2,1,0:T(4,128)}, f32[3,128]{1,0:T(4,128)}, f32[3,128]{1,0:T(4,128)S(1)}) custom-call(f32[32,3,128]{2,1,0:T(4,128)S(1)} %all-to-all-done.2.g_ref, f32[32,8,128]{2,1,0:T(8,128)S(1)} %get-tuple-element.23.table_ref, f32[16,128]{1,0:T(8,128)S(1)} %get-tuple-element.24.exm_ref, f32[3,128]{1,0:T(4,128)S(1)} %get-tuple-element.26.v_ref), custom_call_target="tpu_custom_call" | custom-call | flops 5242880 | bytes 131072 | tf_op jit(solution)/shard_map/fast_step/pallas_call | solution.py:164
  41.9 2.6 %all-to-all-start.3 = ((f32[32,3,128]{2,1,0:T(4,128)}), f32[32,3,128]{2,1,0:T(4,128)S(1)}, u32[]{:S(2)}, u32[]{:S(2)}) async-start(f32[32,3,128]{2,1,0:T(4,128)} %get-tuple-element.27), calls=%async_computation.3 | async-start | bytes 131072 | tf_op jit(solution)/shard_map/all_to_all | solution.py:497
  44.6 4.3 %slow.4 = (f32[3,2,8,128]{3,2,1,0:T(8,128)S(1)}, f32[3,2,8,128]{3,2,1,0:T(8,128)S(1)}, f32[16,4,128]{2,1,0:T(4,128)S(1)}) custom-call(s32[32,5]{1,0:T(8,128)S(1)} %bitcast.18, f32[8,12,4,128]{3,2,1,0:T(4,128)S(1)} %pad_maximum_fusion.tab_ref, f32[3,4,8,128]{3,2,1,0:T(8,128)} %vel_ref.3), custom_call_target="tpu_custom_call" | custom-call | flops 13107200 | bytes 1000000 | tf_op jit(solution)/shard_map/slow/pallas_call | solution.py:462
  48.8 4.9 %slow.5 = (f32[3,4,8,128]{3,2,1,0:T(8,128)S(1)}, f32[3,4,8,128]{3,2,1,0:T(8,128)}, f32[32,4,128]{2,1,0:T(4,128)S(1)}) custom-call(s32[32,5]{1,0:T(8,128)S(1)} %bitcast.19, f32[8,12,4,128]{3,2,1,0:T(4,128)S(1)} %pad_maximum_fusion.tab_ref, f32[3,4,8,128]{3,2,1,0:T(8,128)} %vel_ref.3, f32[3,2,8,128]{3,2,1,0:T(8,128)S(1)} %get-tuple-element.33.refs_0_, ...), custom_call_target="tpu_custom_call" | custom-call | flops 13107200 | bytes 1000000 | tf_op jit(solution)/shard_map/slow/pallas_call | solution.py:462
  53.8 2.3 %fast_step.4 = (f32[32,3,128]{2,1,0:T(4,128)}, f32[3,128]{1,0:T(4,128)}, f32[3,128]{1,0:T(4,128)S(1)}) custom-call(f32[32,3,128]{2,1,0:T(4,128)S(1)} %all-to-all-done.3.g_ref, f32[32,8,128]{2,1,0:T(8,128)S(1)} %get-tuple-element.23.table_ref, f32[16,128]{1,0:T(8,128)S(1)} %get-tuple-element.24.exm_ref, f32[3,128]{1,0:T(4,128)S(1)} %get-tuple-element.28.v_ref), custom_call_target="tpu_custom_call" | custom-call | flops 5242880 | bytes 131072 | tf_op jit(solution)/shard_map/fast_step/pallas_call | solution.py:164
  56.1 5.8 %all-to-all-start.4 = ((f32[32,3,128]{2,1,0:T(4,128)}), f32[32,3,128]{2,1,0:T(4,128)S(1)}, u32[]{:S(2)}, u32[]{:S(2)}) async-start(f32[32,3,128]{2,1,0:T(4,128)} %get-tuple-element.29), calls=%async_computation.4 | async-start | bytes 131072 | tf_op jit(solution)/shard_map/all_to_all | solution.py:497
  62.3 2.4 %collective-permute-start.5 = (f32[2,8,4,128]{3,2,1,0:T(4,128)S(1)}, f32[2,8,4,128]{3,2,1,0:T(4,128)S(1)}, u32[]{:S(2)}, u32[]{:S(2)}) collective-permute-start(f32[2,8,4,128]{3,2,1,0:T(4,128)S(1)} %bitcast.25), channel_id=1, source_target_pairs={{4,0},{8,4},{12,8},{16,12},{20,16},{24,20},{28,24},{0,28},{5,1},{9... | collective-permute-start | bytes 98312 | tf_op jit(solution)/shard_map/ppermute | solution.py:491
  64.7 4.8 %all-to-all-done.4.g_ref = f32[32,3,128]{2,1,0:T(4,128)S(1)} async-done(((f32[32,3,128]{2,1,0:T(4,128)}), f32[32,3,128]{2,1,0:T(4,128)S(1)}, u32[]{:S(2)}, u32[]{:S(2)}) %all-to-all-start.4) | async-done | bytes 49184 | tf_op jit(solution)/shard_map/all_to_all | solution.py:497
  69.4 2.3 %fast_step.5 = (f32[32,3,128]{2,1,0:T(4,128)}, f32[3,128]{1,0:T(4,128)}, f32[3,128]{1,0:T(4,128)S(1)}) custom-call(f32[32,3,128]{2,1,0:T(4,128)S(1)} %all-to-all-done.4.g_ref, f32[32,8,128]{2,1,0:T(8,128)S(1)} %get-tuple-element.23.table_ref, f32[16,128]{1,0:T(8,128)S(1)} %get-tuple-element.24.exm_ref, f32[3,128]{1,0:T(4,128)S(1)} %get-tuple-element.30.v_ref), custom_call_target="tpu_custom_call" | custom-call | flops 5242880 | bytes 131072 | tf_op jit(solution)/shard_map/fast_step/pallas_call | solution.py:164
  71.8 2.6 %all-to-all-start.5 = ((f32[32,3,128]{2,1,0:T(4,128)}), f32[32,3,128]{2,1,0:T(4,128)S(1)}, u32[]{:S(2)}, u32[]{:S(2)}) async-start(f32[32,3,128]{2,1,0:T(4,128)} %get-tuple-element.32), calls=%async_computation.5 | async-start | bytes 131072 | tf_op jit(solution)/shard_map/all_to_all | solution.py:497
  74.4 1.7 %collective-permute-start.6 = (f32[8,2,4,128]{3,2,1,0:T(4,128)S(1)}, f32[8,2,4,128]{3,2,1,0:T(4,128)S(1)}, u32[]{:S(2)}, u32[]{:S(2)}) collective-permute-start(f32[8,2,4,128]{3,2,1,0:T(4,128)S(1)} %get-tuple-element.40), channel_id=1, source_target_pairs={{0,1},{1,2},{2,3},{3,0},{4,5},{5,6},{6,7},{7,4},{8,9},{9,10},{10,1... | collective-permute-start | bytes 98312 | tf_op jit(solution)/shard_map/ppermute | solution.py:490
  76.1 2.1 %collective-permute-start.7 = (f32[8,2,4,128]{3,2,1,0:T(4,128)S(1)}, f32[8,2,4,128]{3,2,1,0:T(4,128)S(1)}, u32[]{:S(2)}, u32[]{:S(2)}) collective-permute-start(f32[8,2,4,128]{3,2,1,0:T(4,128)S(1)} %get-tuple-element.41), channel_id=1, source_target_pairs={{1,0},{2,1},{3,2},{0,3},{5,4},{6,5},{7,6},{4,7},{9,8},{10,9},{11,1... | collective-permute-start | bytes 98312 | tf_op jit(solution)/shard_map/ppermute | solution.py:491
  78.3 3.9 %all-to-all-done.5.g_ref = f32[32,3,128]{2,1,0:T(4,128)S(1)} async-done(((f32[32,3,128]{2,1,0:T(4,128)}), f32[32,3,128]{2,1,0:T(4,128)S(1)}, u32[]{:S(2)}, u32[]{:S(2)}) %all-to-all-start.5) | async-done | bytes 49184 | tf_op jit(solution)/shard_map/all_to_all | solution.py:497
  82.1 1.7 %env.3 = f32[32,3,128]{2,1,0:T(4,128)} custom-call(s32[261]{0:T(512)S(1)} %get-tuple-element.22.list_ref, f32[32,3,128]{2,1,0:T(4,128)S(1)} %all-to-all-done.5.g_ref, f32[32,4,128]{2,1,0:T(4,128)S(1)} %get-tuple-element.36.cells_ref), custom_call_target="tpu_custom_call" | custom-call | flops 2000000 | bytes 200000 | tf_op jit(solution)/shard_map/env/pallas_call | solution.py:295
  83.8 2.6 %all-to-all-start.6 = ((f32[32,3,128]{2,1,0:T(4,128)}), f32[32,3,128]{2,1,0:T(4,128)S(1)}, u32[]{:S(2)}, u32[]{:S(2)}) async-start(f32[32,3,128]{2,1,0:T(4,128)} %env.3), calls=%async_computation.6 | async-start | bytes 131072 | tf_op jit(solution)/shard_map/all_to_all | solution.py:497
  86.5 4.2 %slow.6.refs_0_ = f32[3,2,8,128]{3,2,1,0:T(8,128)S(1)} custom-call(s32[32,5]{1,0:T(8,128)S(1)} %bitcast.20, f32[8,12,4,128]{3,2,1,0:T(4,128)S(1)} %pad_maximum_fusion.1.tab_ref, f32[3,4,8,128]{3,2,1,0:T(8,128)S(1)} %get-tuple-element.39.vel_ref), custom_call_target="tpu_custom_call" | custom-call | flops 13107200 | bytes 1000000 | tf_op jit(solution)/shard_map/slow/pallas_call | solution.py:462
  90.7 4.8 %slow.7 = f32[3,4,8,128]{3,2,1,0:T(8,128)} custom-call(s32[32,5]{1,0:T(8,128)S(1)} %bitcast.21, f32[8,12,4,128]{3,2,1,0:T(4,128)S(1)} %pad_maximum_fusion.1.tab_ref, f32[3,4,8,128]{3,2,1,0:T(8,128)S(1)} %get-tuple-element.39.vel_ref, f32[3,2,8,128]{3,2,1,0:T(8,128)S(1)} %slow.6.refs_0_), custom_call_target="tpu_custom_call" | custom-call | flops 13107200 | bytes 1000000 | tf_op jit(solution)/shard_map/slow/pallas_call | solution.py:462
  95.5 1.7 %fast_only.3.f_ref = f32[3,128]{1,0:T(4,128)S(1)} custom-call(f32[32,3,128]{2,1,0:T(4,128)S(1)} %all-to-all-done.5.g_ref, f32[32,8,128]{2,1,0:T(8,128)S(1)} %get-tuple-element.23.table_ref, f32[16,128]{1,0:T(8,128)S(1)} %get-tuple-element.24.exm_ref), custom_call_target="tpu_custom_call" | custom-call | flops 5242880 | bytes 131072 | tf_op jit(solution)/shard_map/fast_only/pallas_call | solution.py:150
  (35 shorter events, 2.2 us)
Async XLA Ops:
  1.9 7.3 %copy-start.4 = (f32[3,4,8,128]{3,2,1,0:T(8,128)S(1)}, f32[3,4,8,128]{3,2,1,0:T(8,128)}, u32[]{:S(2)}) copy-start(f32[3,4,8,128]{3,2,1,0:T(8,128)} %param.14) | copy-start | bytes 147460
  1.9 14.8 %all-to-all-start = ((f32[32,3,128]{2,1,0:T(4,128)}), f32[32,3,128]{2,1,0:T(4,128)S(1)}, u32[]{:S(2)}, u32[]{:S(2)}) async-start(f32[32,3,128]{2,1,0:T(4,128)} %broadcast_in_dim.4), calls=%async_computation | async-start | bytes 131072 | tf_op jit(solution)/shard_map/all_to_all | solution.py:497
  9.3 0.7 copy-start.3
  18.4 10.1 %all-to-all-start.1 = ((f32[32,3,128]{2,1,0:T(4,128)}), f32[32,3,128]{2,1,0:T(4,128)S(1)}, u32[]{:S(2)}, u32[]{:S(2)}) async-start(f32[32,3,128]{2,1,0:T(4,128)} %env.2), calls=%async_computation.1 | async-start | bytes 131072 | tf_op jit(solution)/shard_map/all_to_all | solution.py:497
  21.0 10.8 %collective-permute-start = (f32[2,8,4,128]{3,2,1,0:T(4,128)S(1)}, f32[2,8,4,128]{3,2,1,0:T(4,128)S(1)}, u32[]{:S(2)}, u32[]{:S(2)}) collective-permute-start(f32[2,8,4,128]{3,2,1,0:T(4,128)S(1)} %get-tuple-element.46), channel_id=1, source_target_pairs={{0,4},{4,8},{8,12},{12,16},{16,20},{20,24},{24,28},{28,0},{1,5},{5... | collective-permute-start | bytes 98312 | tf_op jit(solution)/shard_map/ppermute | solution.py:490
  21.2 10.6 %collective-permute-start.1 = (f32[2,8,4,128]{3,2,1,0:T(4,128)S(1)}, f32[2,8,4,128]{3,2,1,0:T(4,128)S(1)}, u32[]{:S(2)}, u32[]{:S(2)}) collective-permute-start(f32[2,8,4,128]{3,2,1,0:T(4,128)S(1)} %get-tuple-element.47), channel_id=1, source_target_pairs={{4,0},{8,4},{12,8},{16,12},{20,16},{24,20},{28,24},{0,28},{5,1},{9... | collective-permute-start | bytes 98312 | tf_op jit(solution)/shard_map/ppermute | solution.py:491
  23.7 4.8 %copy-start = (f32[4096]{0:T(1024)S(1)}, f32[4096]{0:T(1024)}, u32[]{:S(2)}) copy-start(f32[4096]{0:T(1024)} %param.11) | copy-start | bytes 49156
  23.7 4.8 %copy-start.1 = (f32[3,128]{1,0:T(4,128)S(1)}, f32[3,128]{1,0:T(4,128)}, u32[]{:S(2)}) copy-start(f32[3,128]{1,0:T(4,128)} %p_ref.1) | copy-start | bytes 4612
  23.7 4.8 %copy-start.2 = (f32[3,128]{1,0:T(4,128)S(1)}, f32[3,128]{1,0:T(4,128)}, u32[]{:S(2)}) copy-start(f32[3,128]{1,0:T(4,128)} %v_ref.1) | copy-start | bytes 4612
  29.2 10.4 %all-to-all-start.2 = ((f32[32,3,128]{2,1,0:T(4,128)}), f32[32,3,128]{2,1,0:T(4,128)S(1)}, u32[]{:S(2)}, u32[]{:S(2)}) async-start(f32[32,3,128]{2,1,0:T(4,128)} %get-tuple-element.25), calls=%async_computation.2 | async-start | bytes 131072 | tf_op jit(solution)/shard_map/all_to_all | solution.py:497
  31.8 3.9 %copy-start.5 = (s32[4,8,5]{1,0,2:T(4,128)S(1)}, s32[4,8,5]{1,0,2:T(4,128)}, u32[]{:S(2)}) copy-start(s32[4,8,5]{1,0,2:T(4,128)} %param.17) | copy-start | bytes 1924
  31.9 12.7 %collective-permute-start.2 = (f32[8,2,4,128]{3,2,1,0:T(4,128)S(1)}, f32[8,2,4,128]{3,2,1,0:T(4,128)S(1)}, u32[]{:S(2)}, u32[]{:S(2)}) collective-permute-start(f32[8,2,4,128]{3,2,1,0:T(4,128)S(1)} %get-tuple-element.42), channel_id=1, source_target_pairs={{0,1},{1,2},{2,3},{3,0},{4,5},{5,6},{6,7},{7,4},{8,9},{9,10},{10,1... | collective-permute-start | bytes 98312 | tf_op jit(solution)/shard_map/ppermute | solution.py:490
  33.6 10.9 %collective-permute-start.3 = (f32[8,2,4,128]{3,2,1,0:T(4,128)S(1)}, f32[8,2,4,128]{3,2,1,0:T(4,128)S(1)}, u32[]{:S(2)}, u32[]{:S(2)}) collective-permute-start(f32[8,2,4,128]{3,2,1,0:T(4,128)S(1)} %get-tuple-element.43), channel_id=1, source_target_pairs={{1,0},{2,1},{3,2},{0,3},{5,4},{6,5},{7,6},{4,7},{9,8},{10,9},{11,1... | collective-permute-start | bytes 98312 | tf_op jit(solution)/shard_map/ppermute | solution.py:491
  41.9 11.8 %all-to-all-start.3 = ((f32[32,3,128]{2,1,0:T(4,128)}), f32[32,3,128]{2,1,0:T(4,128)S(1)}, u32[]{:S(2)}, u32[]{:S(2)}) async-start(f32[32,3,128]{2,1,0:T(4,128)} %get-tuple-element.27), calls=%async_computation.3 | async-start | bytes 131072 | tf_op jit(solution)/shard_map/all_to_all | solution.py:497
  56.1 13.3 %all-to-all-start.4 = ((f32[32,3,128]{2,1,0:T(4,128)}), f32[32,3,128]{2,1,0:T(4,128)S(1)}, u32[]{:S(2)}, u32[]{:S(2)}) async-start(f32[32,3,128]{2,1,0:T(4,128)} %get-tuple-element.29), calls=%async_computation.4 | async-start | bytes 131072 | tf_op jit(solution)/shard_map/all_to_all | solution.py:497
  62.0 12.4 %collective-permute-start.4 = (f32[2,8,4,128]{3,2,1,0:T(4,128)S(1)}, f32[2,8,4,128]{3,2,1,0:T(4,128)S(1)}, u32[]{:S(2)}, u32[]{:S(2)}) collective-permute-start(f32[2,8,4,128]{3,2,1,0:T(4,128)S(1)} %bitcast.26), channel_id=1, source_target_pairs={{0,4},{4,8},{8,12},{12,16},{16,20},{20,24},{24,28},{28,0},{1,5},{5... | collective-permute-start | bytes 98312 | tf_op jit(solution)/shard_map/ppermute | solution.py:490
  62.3 12.1 %collective-permute-start.5 = (f32[2,8,4,128]{3,2,1,0:T(4,128)S(1)}, f32[2,8,4,128]{3,2,1,0:T(4,128)S(1)}, u32[]{:S(2)}, u32[]{:S(2)}) collective-permute-start(f32[2,8,4,128]{3,2,1,0:T(4,128)S(1)} %bitcast.25), channel_id=1, source_target_pairs={{4,0},{8,4},{12,8},{16,12},{20,16},{24,20},{28,24},{0,28},{5,1},{9... | collective-permute-start | bytes 98312 | tf_op jit(solution)/shard_map/ppermute | solution.py:491
  71.8 10.4 %all-to-all-start.5 = ((f32[32,3,128]{2,1,0:T(4,128)}), f32[32,3,128]{2,1,0:T(4,128)S(1)}, u32[]{:S(2)}, u32[]{:S(2)}) async-start(f32[32,3,128]{2,1,0:T(4,128)} %get-tuple-element.32), calls=%async_computation.5 | async-start | bytes 131072 | tf_op jit(solution)/shard_map/all_to_all | solution.py:497
  74.4 12.0 %collective-permute-start.6 = (f32[8,2,4,128]{3,2,1,0:T(4,128)S(1)}, f32[8,2,4,128]{3,2,1,0:T(4,128)S(1)}, u32[]{:S(2)}, u32[]{:S(2)}) collective-permute-start(f32[8,2,4,128]{3,2,1,0:T(4,128)S(1)} %get-tuple-element.40), channel_id=1, source_target_pairs={{0,1},{1,2},{2,3},{3,0},{4,5},{5,6},{6,7},{7,4},{8,9},{9,10},{10,1... | collective-permute-start | bytes 98312 | tf_op jit(solution)/shard_map/ppermute | solution.py:490
  76.1 10.3 %collective-permute-start.7 = (f32[8,2,4,128]{3,2,1,0:T(4,128)S(1)}, f32[8,2,4,128]{3,2,1,0:T(4,128)S(1)}, u32[]{:S(2)}, u32[]{:S(2)}) collective-permute-start(f32[8,2,4,128]{3,2,1,0:T(4,128)S(1)} %get-tuple-element.41), channel_id=1, source_target_pairs={{1,0},{2,1},{3,2},{0,3},{5,4},{6,5},{7,6},{4,7},{9,8},{10,9},{11,1... | collective-permute-start | bytes 98312 | tf_op jit(solution)/shard_map/ppermute | solution.py:491
  83.8 13.3 %all-to-all-start.6 = ((f32[32,3,128]{2,1,0:T(4,128)}), f32[32,3,128]{2,1,0:T(4,128)S(1)}, u32[]{:S(2)}, u32[]{:S(2)}) async-start(f32[32,3,128]{2,1,0:T(4,128)} %env.3), calls=%async_computation.6 | async-start | bytes 131072 | tf_op jit(solution)/shard_map/all_to_all | solution.py:497

commit v6 on v5

--- a/solution.py
+++ b/solution.py
@@ -22,7 +22,8 @@
 F32 = jnp.float32
 BF16 = jnp.bfloat16
 LANES = 128
-ENV_UNROLL = 4
+ENV_UNROLL = 8
+PARTS = 4
 
 
 def in_hbm(x):
@@ -72,13 +73,16 @@
     count = g_ref.shape[0]
     members = exm_ref.shape[0]
     zeros = jnp.zeros((5, LANES), F32)
-    for b in range(count):
-        y = jnp.concatenate([g_ref[b], zeros], axis=0) + table_ref[b]
-        atoms[b] = y
-        feat[:, LANES * b : LANES * (b + 1)] = right_rows(y, 1.0).astype(BF16)
-    me = atoms[own]
+    me = jnp.concatenate([g_ref[own], zeros], axis=0) + table_ref[own]
     left = jnp.transpose(left_rows(me)).astype(BF16)
-    dist[...] = jnp.dot(left, feat[...], preferred_element_type=F32)
+    part = max(1, count // PARTS)
+    for start in range(0, count, part):
+        for b in range(start, start + part):
+            y = jnp.concatenate([g_ref[b], zeros], axis=0) + table_ref[b]
+            atoms[b] = y
+            feat[:, LANES * b : LANES * (b + 1)] = right_rows(y, 1.0).astype(BF16)
+        at = slice(LANES * start, LANES * (start + part))
+        dist[:, at] = jnp.dot(left, feat[:, at], preferred_element_type=F32)
     unroll = 2
 
     def body(i, carry):
@@ -192,24 +196,18 @@
     row_bit = total_cols * cell_rows
     keep = -row_bit | (total_cols - cell_cols)
     here = lax.axis_index("row") * row_bit + lax.axis_index("col") * cell_cols
-    unroll = 16
-
-    def body(j, n):
+    first.wait()
+    n = jnp.int32(0)
+    batch = 16
+    for start in range(0, GROUPS, batch):
         found = []
-        row = lax.shift_right_logical(j * unroll, LANES.bit_length() - 1)
-        col = (j * unroll) & (LANES - 1)
-        for u in range(unroll):
-            i = j * unroll + u
-            cell = heads[row, col + u]
+        for i in range(start, start + batch):
+            cell = heads[i // LANES, i % LANES]
             other = (cell & keep) ^ here
             found.append((cell * GROUPS + i, lax.shift_right_logical(other - 1, 31)))
         for entry, inside in found:
             list_ref[n] = entry
             n = n + inside
-        return n
-
-    first.wait()
-    n = lax.fori_loop(0, GROUPS // unroll, body, jnp.int32(0))
     for k in range(ENV_UNROLL):
         list_ref[n + k] = -1
     list_ref[GROUPS + ENV_UNROLL] = n
@@ -352,9 +350,9 @@
 
 
 def slow_kernel(first, row0, nb_ref, tab_ref, vel_ref, *refs):
-    results = 3 if first else 1
-    if row0:
-        before, refs = refs[:results], refs[results:]
+    earlier = (2 if first else 1) if row0 else 0
+    results = 2 if first or row0 else 1
+    before, refs = refs[:earlier], refs[earlier:]
     outs, scratch = refs[:results], refs[results:]
     totals = scratch[8]
     if first:
@@ -362,7 +360,9 @@
         fetch.start()
     vel_out = outs[0]
     if first:
-        pos_out, cell_out = outs[1:]
+        cell_out = outs[1]
+    elif row0:
+        pos_out = outs[1]
     bufs = [tuple(scratch[0:4]), tuple(scratch[4:8])]
     cell_rows, cell_cols = vel_out.shape[1] - row0, vel_out.shape[2]
     slots = nb_ref.shape[1]
@@ -371,8 +371,7 @@
     if row0:
         vel_out[:, :row0] = before[0][...]
         if first:
-            pos_out[:, :row0] = before[1][...]
-            cell_out[:skip] = before[2][...]
+            cell_out[:skip] = before[1][...]
     row8 = lax.broadcasted_iota(jnp.int32, (8, CELL), 0)
 
     def place(n):
@@ -445,8 +444,9 @@
         vel_out[x, rows] = v
         if first:
             p = p + outer_dt * v.reshape(count, CELL)
-            pos_out[x, rows] = p.reshape(cell_rows, cell_cols, CELL)
             cell_out[skip:, x, :] = p
+        elif row0:
+            pos_out[x] = tab_ref[2 : 2 + row0 + cell_rows, inner[1], x, :]
     if first:
         cell_out[skip:, 3, :] = charge
 
@@ -457,7 +457,9 @@
     slots = nb.shape[1]
     out = (sds(shape),)
     if first:
-        out += (sds(shape), sds(((row0 + rows) * vel.shape[2], 4, CELL)))
+        out += (sds(((row0 + rows) * vel.shape[2], 4, CELL)),)
+    elif row0:
+        out += (sds(shape),)
     pairs = own * slots * CELL * CELL
     return pl.pallas_call(
         functools.partial(slow_kernel, first, row0),
@@ -526,12 +528,12 @@
     part = ()
     for r0 in (0, half):
         part = slow(True, r0, half, nb, tab, slow_vel, part)
-    slow_vel, slow_pos, cells2 = part
+    slow_vel, cells2 = part
     tab2 = with_halo(cells2.reshape(cells.shape), sides, 2)
     part = ()
     for r0 in (0, half):
         part = slow(False, r0, half, nb, tab2, slow_vel, part)
-    (slow_vel,) = part
+    slow_vel, slow_pos = part
 
     back = exchange(env(groups, g, cells.reshape(cells2.shape), grid))
     f = fast_only(g, table, exm)

time: 98.4 us -> 97.1 us (0.987)
  Pallas kernels: 36 us -> 34.3 us
  transfers between devices with their start and end apart: 15 -> 15, of which waited for: 5 -> 5; matrix products, arithmetic and copies ran while one was open for 0% -> 0% of each run, Pallas kernels for 32% -> 31%
where the time goes in v6:
time: 97.1 us; the launch traced here: 96.5 us
  starting transfers between devices  38.9 us (40%)
  Pallas kernels  34.3 us (35%)
  waiting for transfers between devices  20 us (21%)
  local copies, waits for them, and re-layouts  2.15 us (2%)
    all_to_all x7, starting transfers between devices, exchange(): return lax.all_to_all(x, BOTH, 0, 0)  25.8 us
    all_to_all x7, waiting for transfers between devices, exchange(): return lax.all_to_all(x, BOTH, 0, 0)  20 us
    pallas_call x4, Pallas kernels, slow(): pl.pallas_call(functools.partial(slow_kernel, first, row0), out_shape=out...  17.6 us
    ppermute x4, starting transfers between devices, with_halo(): after = lax.ppermute(initial, axis, down)  9.2 us
    pallas_call x3, Pallas kernels, fast_step(): pl.pallas_call(fast_step_kernel, out_shape=(sds((count, 3, LANES)), sds((...  6.92 us
    ppermute x4, starting transfers between devices, with_halo(): before = lax.ppermute(last, axis, up)  3.95 us
    pallas_call x2, Pallas kernels, fast_only(): pl.pallas_call(fast_only_kernel, out_shape=sds((3, LANES)), in_specs=[VME...  3.32 us
    pallas_call x2, Pallas kernels, env(): pl.pallas_call(functools.partial(env_kernel, grid), out_shape=sds((count,...  2.98 us
  transfers between devices with their start and end apart: 15, of which 5 were waited for; matrix products, arithmetic and copies ran while one was open for 0% of the time, Pallas kernels for 31%

profile of v6, /device:TPU:0, one launch (start us, length us, event | category | flops | bytes accessed | tf_op | source)
XLA Modules:
  0.0 96.5 jit_solution(10175264855367648647)
XLA Ops:
  0.6 1.3 %broadcast_in_dim.4 = f32[32,3,128]{2,1,0:T(4,128)} broadcast(f32[3,128]{1,0:T(4,128)} %p_ref.1), dimensions={1,2} | broadcast | bytes 50688 | tf_op jit(solution)/shard_map/broadcast_in_dim | solution.py:516
  1.9 7.3 %all-to-all-start = ((f32[32,3,128]{2,1,0:T(4,128)}), f32[32,3,128]{2,1,0:T(4,128)S(1)}, u32[]{:S(2)}, u32[]{:S(2)}) async-start(f32[32,3,128]{2,1,0:T(4,128)} %broadcast_in_dim.4), calls=%async_computation | async-start | bytes 131072 | tf_op jit(solution)/shard_map/all_to_all | solution.py:499
  10.0 2.2 %prep.1 = (f32[32,8,128]{2,1,0:T(8,128)S(1)}, f32[16,128]{1,0:T(8,128)S(1)}, s32[265]{0:T(512)S(1)}) custom-call(s32[32,128]{1,0:T(8,128)} %bitcast.27, f32[32,128]{1,0:T(8,128)} %bitcast.15, s32[4,4096]{1,0:T(4,128)} %bitcast.24), custom_call_target="tpu_custom_call" | custom-call | tf_op jit(solution)/shard_map/prep/pallas_call | solution.py:232
  12.3 4.5 %all-to-all-done.g_ref = f32[32,3,128]{2,1,0:T(4,128)S(1)} async-done(((f32[32,3,128]{2,1,0:T(4,128)}), f32[32,3,128]{2,1,0:T(4,128)S(1)}, u32[]{:S(2)}, u32[]{:S(2)}) %all-to-all-start) | async-done | bytes 49184 | tf_op jit(solution)/shard_map/all_to_all | solution.py:499
  16.8 1.5 %env.2 = f32[32,3,128]{2,1,0:T(4,128)} custom-call(s32[265]{0:T(512)S(1)} %get-tuple-element.22.list_ref, f32[32,3,128]{2,1,0:T(4,128)S(1)} %all-to-all-done.g_ref, f32[32,4,128]{2,1,0:T(4,128)S(1)} %bitcast.14), custom_call_target="tpu_custom_call" | custom-call | flops 2000000 | bytes 200000 | tf_op jit(solution)/shard_map/env/pallas_call | solution.py:293
  18.3 2.5 %all-to-all-start.1 = ((f32[32,3,128]{2,1,0:T(4,128)}), f32[32,3,128]{2,1,0:T(4,128)S(1)}, u32[]{:S(2)}, u32[]{:S(2)}) async-start(f32[32,3,128]{2,1,0:T(4,128)} %env.2), calls=%async_computation.1 | async-start | bytes 131072 | tf_op jit(solution)/shard_map/all_to_all | solution.py:499
  21.0 2.5 %collective-permute-start.1 = (f32[2,8,4,128]{3,2,1,0:T(4,128)S(1)}, f32[2,8,4,128]{3,2,1,0:T(4,128)S(1)}, u32[]{:S(2)}, u32[]{:S(2)}) collective-permute-start(f32[2,8,4,128]{3,2,1,0:T(4,128)S(1)} %get-tuple-element.47), channel_id=1, source_target_pairs={{4,0},{8,4},{12,8},{16,12},{20,16},{24,20},{28,24},{0,28},{5,1},{9... | collective-permute-start | bytes 98312 | tf_op jit(solution)/shard_map/ppermute | solution.py:493
  23.5 1.7 %fast_only.2.f_ref = f32[3,128]{1,0:T(4,128)S(1)} custom-call(f32[32,3,128]{2,1,0:T(4,128)S(1)} %all-to-all-done.g_ref, f32[32,8,128]{2,1,0:T(8,128)S(1)} %get-tuple-element.23.table_ref, f32[16,128]{1,0:T(8,128)S(1)} %get-tuple-element.24.exm_ref), custom_call_target="tpu_custom_call" | custom-call | flops 5242880 | bytes 131072 | tf_op jit(solution)/shard_map/fast_only/pallas_call | solution.py:154
  25.2 3.1 %all-to-all-done.1.e_ref = f32[32,3,128]{2,1,0:T(4,128)S(1)} async-done(((f32[32,3,128]{2,1,0:T(4,128)}), f32[32,3,128]{2,1,0:T(4,128)S(1)}, u32[]{:S(2)}, u32[]{:S(2)}) %all-to-all-start.1) | async-done | bytes 49184 | tf_op jit(solution)/shard_map/all_to_all | solution.py:499
  28.3 0.7 kick.1
  29.0 2.5 %all-to-all-start.2 = ((f32[32,3,128]{2,1,0:T(4,128)}), f32[32,3,128]{2,1,0:T(4,128)S(1)}, u32[]{:S(2)}, u32[]{:S(2)}) async-start(f32[32,3,128]{2,1,0:T(4,128)} %get-tuple-element.25), calls=%async_computation.2 | async-start | bytes 131072 | tf_op jit(solution)/shard_map/all_to_all | solution.py:499
  31.6 1.7 %collective-permute-start.2 = (f32[8,2,4,128]{3,2,1,0:T(4,128)S(1)}, f32[8,2,4,128]{3,2,1,0:T(4,128)S(1)}, u32[]{:S(2)}, u32[]{:S(2)}) collective-permute-start(f32[8,2,4,128]{3,2,1,0:T(4,128)S(1)} %get-tuple-element.42), channel_id=1, source_target_pairs={{0,1},{1,2},{2,3},{3,0},{4,5},{5,6},{6,7},{7,4},{8,9},{9,10},{10,1... | collective-permute-start | bytes 98312 | tf_op jit(solution)/shard_map/ppermute | solution.py:492
  33.3 2.1 %collective-permute-start.3 = (f32[8,2,4,128]{3,2,1,0:T(4,128)S(1)}, f32[8,2,4,128]{3,2,1,0:T(4,128)S(1)}, u32[]{:S(2)}, u32[]{:S(2)}) collective-permute-start(f32[8,2,4,128]{3,2,1,0:T(4,128)S(1)} %get-tuple-element.43), channel_id=1, source_target_pairs={{1,0},{2,1},{3,2},{0,3},{5,4},{6,5},{7,6},{4,7},{9,8},{10,9},{11,1... | collective-permute-start | bytes 98312 | tf_op jit(solution)/shard_map/ppermute | solution.py:493
  35.6 3.8 %all-to-all-done.2.g_ref = f32[32,3,128]{2,1,0:T(4,128)S(1)} async-done(((f32[32,3,128]{2,1,0:T(4,128)}), f32[32,3,128]{2,1,0:T(4,128)S(1)}, u32[]{:S(2)}, u32[]{:S(2)}) %all-to-all-start.2) | async-done | bytes 49184 | tf_op jit(solution)/shard_map/all_to_all | solution.py:499
  39.3 2.3 %fast_step.3 = (f32[32,3,128]{2,1,0:T(4,128)}, f32[3,128]{1,0:T(4,128)}, f32[3,128]{1,0:T(4,128)S(1)}) custom-call(f32[32,3,128]{2,1,0:T(4,128)S(1)} %all-to-all-done.2.g_ref, f32[32,8,128]{2,1,0:T(8,128)S(1)} %get-tuple-element.23.table_ref, f32[16,128]{1,0:T(8,128)S(1)} %get-tuple-element.24.exm_ref, f32[3,128]{1,0:T(4,128)S(1)} %get-tuple-element.26.v_ref), custom_call_target="tpu_custom_call" | custom-call | flops 5242880 | bytes 131072 | tf_op jit(solution)/shard_map/fast_step/pallas_call | solution.py:168
  41.6 2.5 %all-to-all-start.3 = ((f32[32,3,128]{2,1,0:T(4,128)}), f32[32,3,128]{2,1,0:T(4,128)S(1)}, u32[]{:S(2)}, u32[]{:S(2)}) async-start(f32[32,3,128]{2,1,0:T(4,128)} %get-tuple-element.27), calls=%async_computation.3 | async-start | bytes 131072 | tf_op jit(solution)/shard_map/all_to_all | solution.py:499
  44.2 4.3 %slow.4 = (f32[3,2,8,128]{3,2,1,0:T(8,128)S(1)}, f32[16,4,128]{2,1,0:T(4,128)S(1)}) custom-call(s32[32,5]{1,0:T(8,128)S(1)} %bitcast.18, f32[8,12,4,128]{3,2,1,0:T(4,128)S(1)} %pad_maximum_fusion.tab_ref, f32[3,4,8,128]{3,2,1,0:T(8,128)} %vel_ref.3), custom_call_target="tpu_custom_call" | custom-call | flops 13107200 | bytes 1000000 | tf_op jit(solution)/shard_map/slow/pallas_call | solution.py:464
  48.5 4.3 %slow.5 = (f32[3,4,8,128]{3,2,1,0:T(8,128)S(1)}, f32[32,4,128]{2,1,0:T(4,128)S(1)}) custom-call(s32[32,5]{1,0:T(8,128)S(1)} %bitcast.19, f32[8,12,4,128]{3,2,1,0:T(4,128)S(1)} %pad_maximum_fusion.tab_ref, f32[3,4,8,128]{3,2,1,0:T(8,128)} %vel_ref.3, f32[3,2,8,128]{3,2,1,0:T(8,128)S(1)} %get-tuple-element.33.refs_0_, f32[16,4,128]{2,1,0:T(4,128)S(1)} %get-tuple-element.34.refs_1_), custom_call_target="tpu_custom_call" | custom-call | flops 13107200 | bytes 1000000 | tf_op jit(solution)/shard_map/slow/pallas_call | solution.py:464
  52.8 2.3 %fast_step.4 = (f32[32,3,128]{2,1,0:T(4,128)}, f32[3,128]{1,0:T(4,128)}, f32[3,128]{1,0:T(4,128)S(1)}) custom-call(f32[32,3,128]{2,1,0:T(4,128)S(1)} %all-to-all-done.3.g_ref, f32[32,8,128]{2,1,0:T(8,128)S(1)} %get-tuple-element.23.table_ref, f32[16,128]{1,0:T(8,128)S(1)} %get-tuple-element.24.exm_ref, f32[3,128]{1,0:T(4,128)S(1)} %get-tuple-element.28.v_ref), custom_call_target="tpu_custom_call" | custom-call | flops 5242880 | bytes 131072 | tf_op jit(solution)/shard_map/fast_step/pallas_call | solution.py:168
  55.1 5.8 %all-to-all-start.4 = ((f32[32,3,128]{2,1,0:T(4,128)}), f32[32,3,128]{2,1,0:T(4,128)S(1)}, u32[]{:S(2)}, u32[]{:S(2)}) async-start(f32[32,3,128]{2,1,0:T(4,128)} %get-tuple-element.29), calls=%async_computation.4 | async-start | bytes 131072 | tf_op jit(solution)/shard_map/all_to_all | solution.py:499
  61.3 2.4 %collective-permute-start.5 = (f32[2,8,4,128]{3,2,1,0:T(4,128)S(1)}, f32[2,8,4,128]{3,2,1,0:T(4,128)S(1)}, u32[]{:S(2)}, u32[]{:S(2)}) collective-permute-start(f32[2,8,4,128]{3,2,1,0:T(4,128)S(1)} %bitcast.25), channel_id=1, source_target_pairs={{4,0},{8,4},{12,8},{16,12},{20,16},{24,20},{28,24},{0,28},{5,1},{9... | collective-permute-start | bytes 98312 | tf_op jit(solution)/shard_map/ppermute | solution.py:493
  63.7 4.8 %all-to-all-done.4.g_ref = f32[32,3,128]{2,1,0:T(4,128)S(1)} async-done(((f32[32,3,128]{2,1,0:T(4,128)}), f32[32,3,128]{2,1,0:T(4,128)S(1)}, u32[]{:S(2)}, u32[]{:S(2)}) %all-to-all-start.4) | async-done | bytes 49184 | tf_op jit(solution)/shard_map/all_to_all | solution.py:499
  68.5 2.3 %fast_step.5 = (f32[32,3,128]{2,1,0:T(4,128)}, f32[3,128]{1,0:T(4,128)}, f32[3,128]{1,0:T(4,128)S(1)}) custom-call(f32[32,3,128]{2,1,0:T(4,128)S(1)} %all-to-all-done.4.g_ref, f32[32,8,128]{2,1,0:T(8,128)S(1)} %get-tuple-element.23.table_ref, f32[16,128]{1,0:T(8,128)S(1)} %get-tuple-element.24.exm_ref, f32[3,128]{1,0:T(4,128)S(1)} %get-tuple-element.30.v_ref), custom_call_target="tpu_custom_call" | custom-call | flops 5242880 | bytes 131072 | tf_op jit(solution)/shard_map/fast_step/pallas_call | solution.py:168
  70.8 2.5 %all-to-all-start.5 = ((f32[32,3,128]{2,1,0:T(4,128)}), f32[32,3,128]{2,1,0:T(4,128)S(1)}, u32[]{:S(2)}, u32[]{:S(2)}) async-start(f32[32,3,128]{2,1,0:T(4,128)} %get-tuple-element.32), calls=%async_computation.5 | async-start | bytes 131072 | tf_op jit(solution)/shard_map/all_to_all | solution.py:499
  73.4 1.7 %collective-permute-start.6 = (f32[8,2,4,128]{3,2,1,0:T(4,128)S(1)}, f32[8,2,4,128]{3,2,1,0:T(4,128)S(1)}, u32[]{:S(2)}, u32[]{:S(2)}) collective-permute-start(f32[8,2,4,128]{3,2,1,0:T(4,128)S(1)} %get-tuple-element.40), channel_id=1, source_target_pairs={{0,1},{1,2},{2,3},{3,0},{4,5},{5,6},{6,7},{7,4},{8,9},{9,10},{10,1... | collective-permute-start | bytes 98312 | tf_op jit(solution)/shard_map/ppermute | solution.py:492
  75.1 2.1 %collective-permute-start.7 = (f32[8,2,4,128]{3,2,1,0:T(4,128)S(1)}, f32[8,2,4,128]{3,2,1,0:T(4,128)S(1)}, u32[]{:S(2)}, u32[]{:S(2)}) collective-permute-start(f32[8,2,4,128]{3,2,1,0:T(4,128)S(1)} %get-tuple-element.41), channel_id=1, source_target_pairs={{1,0},{2,1},{3,2},{0,3},{5,4},{6,5},{7,6},{4,7},{9,8},{10,9},{11,1... | collective-permute-start | bytes 98312 | tf_op jit(solution)/shard_map/ppermute | solution.py:493
  77.2 3.9 %all-to-all-done.5.g_ref = f32[32,3,128]{2,1,0:T(4,128)S(1)} async-done(((f32[32,3,128]{2,1,0:T(4,128)}), f32[32,3,128]{2,1,0:T(4,128)S(1)}, u32[]{:S(2)}, u32[]{:S(2)}) %all-to-all-start.5) | async-done | bytes 49184 | tf_op jit(solution)/shard_map/all_to_all | solution.py:499
  81.1 1.5 %env.3 = f32[32,3,128]{2,1,0:T(4,128)} custom-call(s32[265]{0:T(512)S(1)} %get-tuple-element.22.list_ref, f32[32,3,128]{2,1,0:T(4,128)S(1)} %all-to-all-done.5.g_ref, f32[32,4,128]{2,1,0:T(4,128)S(1)} %get-tuple-element.35.cells_ref), custom_call_target="tpu_custom_call" | custom-call | flops 2000000 | bytes 200000 | tf_op jit(solution)/shard_map/env/pallas_call | solution.py:293
  82.6 2.5 %all-to-all-start.6 = ((f32[32,3,128]{2,1,0:T(4,128)}), f32[32,3,128]{2,1,0:T(4,128)S(1)}, u32[]{:S(2)}, u32[]{:S(2)}) async-start(f32[32,3,128]{2,1,0:T(4,128)} %env.3), calls=%async_computation.6 | async-start | bytes 131072 | tf_op jit(solution)/shard_map/all_to_all | solution.py:499
  85.2 4.2 %slow.6.refs_0_ = f32[3,2,8,128]{3,2,1,0:T(8,128)S(1)} custom-call(s32[32,5]{1,0:T(8,128)S(1)} %bitcast.20, f32[8,12,4,128]{3,2,1,0:T(4,128)S(1)} %pad_maximum_fusion.1.tab_ref, f32[3,4,8,128]{3,2,1,0:T(8,128)S(1)} %get-tuple-element.37.vel_ref), custom_call_target="tpu_custom_call" | custom-call | flops 13107200 | bytes 1000000 | tf_op jit(solution)/shard_map/slow/pallas_call | solution.py:464
  89.4 4.8 %slow.7 = (f32[3,4,8,128]{3,2,1,0:T(8,128)}, f32[3,4,8,128]{3,2,1,0:T(8,128)}) custom-call(s32[32,5]{1,0:T(8,128)S(1)} %bitcast.21, f32[8,12,4,128]{3,2,1,0:T(4,128)S(1)} %pad_maximum_fusion.1.tab_ref, f32[3,4,8,128]{3,2,1,0:T(8,128)S(1)} %get-tuple-element.37.vel_ref, f32[3,2,8,128]{3,2,1,0:T(8,128)S(1)} %slow.6.refs_0_), custom_call_target="tpu_custom_call" | custom-call | flops 13107200 | bytes 1000000 | tf_op jit(solution)/shard_map/slow/pallas_call | solution.py:464
  94.2 1.7 %fast_only.3.f_ref = f32[3,128]{1,0:T(4,128)S(1)} custom-call(f32[32,3,128]{2,1,0:T(4,128)S(1)} %all-to-all-done.5.g_ref, f32[32,8,128]{2,1,0:T(8,128)S(1)} %get-tuple-element.23.table_ref, f32[16,128]{1,0:T(8,128)S(1)} %get-tuple-element.24.exm_ref), custom_call_target="tpu_custom_call" | custom-call | flops 5242880 | bytes 131072 | tf_op jit(solution)/shard_map/fast_only/pallas_call | solution.py:154
  (35 shorter events, 2.2 us)
Async XLA Ops:
  1.9 7.3 %copy-start.4 = (f32[3,4,8,128]{3,2,1,0:T(8,128)S(1)}, f32[3,4,8,128]{3,2,1,0:T(8,128)}, u32[]{:S(2)}) copy-start(f32[3,4,8,128]{3,2,1,0:T(8,128)} %param.14) | copy-start | bytes 147460
  1.9 14.8 %all-to-all-start = ((f32[32,3,128]{2,1,0:T(4,128)}), f32[32,3,128]{2,1,0:T(4,128)S(1)}, u32[]{:S(2)}, u32[]{:S(2)}) async-start(f32[32,3,128]{2,1,0:T(4,128)} %broadcast_in_dim.4), calls=%async_computation | async-start | bytes 131072 | tf_op jit(solution)/shard_map/all_to_all | solution.py:499
  9.3 0.7 copy-start.3
  18.3 10.0 %all-to-all-start.1 = ((f32[32,3,128]{2,1,0:T(4,128)}), f32[32,3,128]{2,1,0:T(4,128)S(1)}, u32[]{:S(2)}, u32[]{:S(2)}) async-start(f32[32,3,128]{2,1,0:T(4,128)} %env.2), calls=%async_computation.1 | async-start | bytes 131072 | tf_op jit(solution)/shard_map/all_to_all | solution.py:499
  20.8 10.7 %collective-permute-start = (f32[2,8,4,128]{3,2,1,0:T(4,128)S(1)}, f32[2,8,4,128]{3,2,1,0:T(4,128)S(1)}, u32[]{:S(2)}, u32[]{:S(2)}) collective-permute-start(f32[2,8,4,128]{3,2,1,0:T(4,128)S(1)} %get-tuple-element.46), channel_id=1, source_target_pairs={{0,4},{4,8},{8,12},{12,16},{16,20},{20,24},{24,28},{28,0},{1,5},{5... | collective-permute-start | bytes 98312 | tf_op jit(solution)/shard_map/ppermute | solution.py:492
  21.0 10.6 %collective-permute-start.1 = (f32[2,8,4,128]{3,2,1,0:T(4,128)S(1)}, f32[2,8,4,128]{3,2,1,0:T(4,128)S(1)}, u32[]{:S(2)}, u32[]{:S(2)}) collective-permute-start(f32[2,8,4,128]{3,2,1,0:T(4,128)S(1)} %get-tuple-element.47), channel_id=1, source_target_pairs={{4,0},{8,4},{12,8},{16,12},{20,16},{24,20},{28,24},{0,28},{5,1},{9... | collective-permute-start | bytes 98312 | tf_op jit(solution)/shard_map/ppermute | solution.py:493
  23.5 4.8 %copy-start = (f32[4096]{0:T(1024)S(1)}, f32[4096]{0:T(1024)}, u32[]{:S(2)}) copy-start(f32[4096]{0:T(1024)} %param.11) | copy-start | bytes 49156
  23.5 4.8 %copy-start.1 = (f32[3,128]{1,0:T(4,128)S(1)}, f32[3,128]{1,0:T(4,128)}, u32[]{:S(2)}) copy-start(f32[3,128]{1,0:T(4,128)} %p_ref.1) | copy-start | bytes 4612
  23.5 4.8 %copy-start.2 = (f32[3,128]{1,0:T(4,128)S(1)}, f32[3,128]{1,0:T(4,128)}, u32[]{:S(2)}) copy-start(f32[3,128]{1,0:T(4,128)} %v_ref.1) | copy-start | bytes 4612
  29.0 10.3 %all-to-all-start.2 = ((f32[32,3,128]{2,1,0:T(4,128)}), f32[32,3,128]{2,1,0:T(4,128)S(1)}, u32[]{:S(2)}, u32[]{:S(2)}) async-start(f32[32,3,128]{2,1,0:T(4,128)} %get-tuple-element.25), calls=%async_computation.2 | async-start | bytes 131072 | tf_op jit(solution)/shard_map/all_to_all | solution.py:499
  31.5 3.9 %copy-start.5 = (s32[4,8,5]{1,0,2:T(4,128)S(1)}, s32[4,8,5]{1,0,2:T(4,128)}, u32[]{:S(2)}) copy-start(s32[4,8,5]{1,0,2:T(4,128)} %param.17) | copy-start | bytes 1924
  31.6 12.6 %collective-permute-start.2 = (f32[8,2,4,128]{3,2,1,0:T(4,128)S(1)}, f32[8,2,4,128]{3,2,1,0:T(4,128)S(1)}, u32[]{:S(2)}, u32[]{:S(2)}) collective-permute-start(f32[8,2,4,128]{3,2,1,0:T(4,128)S(1)} %get-tuple-element.42), channel_id=1, source_target_pairs={{0,1},{1,2},{2,3},{3,0},{4,5},{5,6},{6,7},{7,4},{8,9},{9,10},{10,1... | collective-permute-start | bytes 98312 | tf_op jit(solution)/shard_map/ppermute | solution.py:492
  33.3 10.9 %collective-permute-start.3 = (f32[8,2,4,128]{3,2,1,0:T(4,128)S(1)}, f32[8,2,4,128]{3,2,1,0:T(4,128)S(1)}, u32[]{:S(2)}, u32[]{:S(2)}) collective-permute-start(f32[8,2,4,128]{3,2,1,0:T(4,128)S(1)} %get-tuple-element.43), channel_id=1, source_target_pairs={{1,0},{2,1},{3,2},{0,3},{5,4},{6,5},{7,6},{4,7},{9,8},{10,9},{11,1... | collective-permute-start | bytes 98312 | tf_op jit(solution)/shard_map/ppermute | solution.py:493
  41.6 11.2 %all-to-all-start.3 = ((f32[32,3,128]{2,1,0:T(4,128)}), f32[32,3,128]{2,1,0:T(4,128)S(1)}, u32[]{:S(2)}, u32[]{:S(2)}) async-start(f32[32,3,128]{2,1,0:T(4,128)} %get-tuple-element.27), calls=%async_computation.3 | async-start | bytes 131072 | tf_op jit(solution)/shard_map/all_to_all | solution.py:499
  55.1 13.3 %all-to-all-start.4 = ((f32[32,3,128]{2,1,0:T(4,128)}), f32[32,3,128]{2,1,0:T(4,128)S(1)}, u32[]{:S(2)}, u32[]{:S(2)}) async-start(f32[32,3,128]{2,1,0:T(4,128)} %get-tuple-element.29), calls=%async_computation.4 | async-start | bytes 131072 | tf_op jit(solution)/shard_map/all_to_all | solution.py:499
  61.0 12.3 %collective-permute-start.4 = (f32[2,8,4,128]{3,2,1,0:T(4,128)S(1)}, f32[2,8,4,128]{3,2,1,0:T(4,128)S(1)}, u32[]{:S(2)}, u32[]{:S(2)}) collective-permute-start(f32[2,8,4,128]{3,2,1,0:T(4,128)S(1)} %bitcast.26), channel_id=1, source_target_pairs={{0,4},{4,8},{8,12},{12,16},{16,20},{20,24},{24,28},{28,0},{1,5},{5... | collective-permute-start | bytes 98312 | tf_op jit(solution)/shard_map/ppermute | solution.py:492
  61.3 12.0 %collective-permute-start.5 = (f32[2,8,4,128]{3,2,1,0:T(4,128)S(1)}, f32[2,8,4,128]{3,2,1,0:T(4,128)S(1)}, u32[]{:S(2)}, u32[]{:S(2)}) collective-permute-start(f32[2,8,4,128]{3,2,1,0:T(4,128)S(1)} %bitcast.25), channel_id=1, source_target_pairs={{4,0},{8,4},{12,8},{16,12},{20,16},{24,20},{28,24},{0,28},{5,1},{9... | collective-permute-start | bytes 98312 | tf_op jit(solution)/shard_map/ppermute | solution.py:493
  70.8 10.3 %all-to-all-start.5 = ((f32[32,3,128]{2,1,0:T(4,128)}), f32[32,3,128]{2,1,0:T(4,128)S(1)}, u32[]{:S(2)}, u32[]{:S(2)}) async-start(f32[32,3,128]{2,1,0:T(4,128)} %get-tuple-element.32), calls=%async_computation.5 | async-start | bytes 131072 | tf_op jit(solution)/shard_map/all_to_all | solution.py:499
  73.4 11.8 %collective-permute-start.6 = (f32[8,2,4,128]{3,2,1,0:T(4,128)S(1)}, f32[8,2,4,128]{3,2,1,0:T(4,128)S(1)}, u32[]{:S(2)}, u32[]{:S(2)}) collective-permute-start(f32[8,2,4,128]{3,2,1,0:T(4,128)S(1)} %get-tuple-element.40), channel_id=1, source_target_pairs={{0,1},{1,2},{2,3},{3,0},{4,5},{5,6},{6,7},{7,4},{8,9},{9,10},{10,1... | collective-permute-start | bytes 98312 | tf_op jit(solution)/shard_map/ppermute | solution.py:492
  75.1 10.1 %collective-permute-start.7 = (f32[8,2,4,128]{3,2,1,0:T(4,128)S(1)}, f32[8,2,4,128]{3,2,1,0:T(4,128)S(1)}, u32[]{:S(2)}, u32[]{:S(2)}) collective-permute-start(f32[8,2,4,128]{3,2,1,0:T(4,128)S(1)} %get-tuple-element.41), channel_id=1, source_target_pairs={{1,0},{2,1},{3,2},{0,3},{5,4},{6,5},{7,6},{4,7},{9,8},{10,9},{11,1... | collective-permute-start | bytes 98312 | tf_op jit(solution)/shard_map/ppermute | solution.py:493
  82.6 13.3 %all-to-all-start.6 = ((f32[32,3,128]{2,1,0:T(4,128)}), f32[32,3,128]{2,1,0:T(4,128)S(1)}, u32[]{:S(2)}, u32[]{:S(2)}) async-start(f32[32,3,128]{2,1,0:T(4,128)} %env.3), calls=%async_computation.6 | async-start | bytes 131072 | tf_op jit(solution)/shard_map/all_to_all | solution.py:499

commit v7 on v6

--- a/solution.py
+++ b/solution.py
@@ -22,7 +22,7 @@
 F32 = jnp.float32
 BF16 = jnp.bfloat16
 LANES = 128
-ENV_UNROLL = 8
+ENV_UNROLL = 12
 PARTS = 4
 
 
@@ -83,7 +83,7 @@
             feat[:, LANES * b : LANES * (b + 1)] = right_rows(y, 1.0).astype(BF16)
         at = slice(LANES * start, LANES * (start + part))
         dist[:, at] = jnp.dot(left, feat[:, at], preferred_element_type=F32)
-    unroll = 2
+    unroll = 16
 
     def body(i, carry):
         at = [pl.ds(pl.multiple_of((i * unroll + u) * 8, 8), 8) for u in range(unroll)]
@@ -520,6 +520,7 @@
     grid = (total_cols, cell_rows, cell_cols)
     table, exm, groups = prep(fast_owner, q, exclusions, members, grid)
 
+    slow_charge, exm = lax.optimization_barrier((slow_charge, exm))
     cells = jnp.concatenate([slow_pos, slow_charge[None]], axis=0).transpose(1, 2, 0, 3)
     sides = (("row", 0), ("col", 1))
     nb = neighbours.reshape(cell_rows * cell_cols, -1)

time: 97.1 us -> 95.3 us (0.981)
  Pallas kernels: 34.3 us -> 32.1 us
  waiting for transfers between devices: 20 us -> 21.3 us
    pallas_call x3, Pallas kernels: 6.92 us -> 5.49 us  [fast_step(): pl.pallas_call(fast_step_kernel, out_shape=(sds((count, 3, LANES)), sds((...]
    all_to_all x7, waiting for transfers between devices: 20 us -> 21.3 us  [exchange(): return lax.all_to_all(x, BOTH, 0, 0)]
  transfers between devices with their start and end apart: 15 -> 15, of which waited for: 5 -> 5; matrix products, arithmetic and copies ran while one was open for 0% -> 0% of each run, Pallas kernels for 31% -> 30%
where the time goes in v7:
time: 95.3 us; the launch traced here: 94.8 us
  starting transfers between devices  38.8 us (41%)
  Pallas kernels  32.1 us (34%)
  waiting for transfers between devices  21.3 us (22%)
  local copies, waits for them, and re-layouts  1.49 us (2%)
    all_to_all x7, starting transfers between devices, exchange(): return lax.all_to_all(x, BOTH, 0, 0)  25.9 us
    all_to_all x7, waiting for transfers between devices, exchange(): return lax.all_to_all(x, BOTH, 0, 0)  21.3 us
    pallas_call x4, Pallas kernels, slow(): pl.pallas_call(functools.partial(slow_kernel, first, row0), out_shape=out...  17.6 us
    ppermute x4, starting transfers between devices, with_halo(): after = lax.ppermute(initial, axis, down)  9.25 us
    pallas_call x3, Pallas kernels, fast_step(): pl.pallas_call(fast_step_kernel, out_shape=(sds((count, 3, LANES)), sds((...  5.49 us
    ppermute x4, starting transfers between devices, with_halo(): before = lax.ppermute(last, axis, up)  3.65 us
    pallas_call x2, Pallas kernels, env(): pl.pallas_call(functools.partial(env_kernel, grid), out_shape=sds((count,...  3 us
    pallas_call x2, Pallas kernels, fast_only(): pl.pallas_call(fast_only_kernel, out_shape=sds((3, LANES)), in_specs=[VME...  2.38 us
  transfers between devices with their start and end apart: 15, of which 5 were waited for; matrix products, arithmetic and copies ran while one was open for 0% of the time, Pallas kernels for 30%

profile of v7, /device:TPU:0, one launch (start us, length us, event | category | flops | bytes accessed | tf_op | source)
XLA Modules:
  0.0 94.8 jit_solution(8471782261030550626)
XLA Ops:
  0.6 1.3 %broadcast_in_dim.4 = f32[32,3,128]{2,1,0:T(4,128)} broadcast(f32[3,128]{1,0:T(4,128)} %p_ref.1), dimensions={1,2} | broadcast | bytes 50688 | tf_op jit(solution)/shard_map/broadcast_in_dim | solution.py:516
  1.9 7.3 %all-to-all-start = ((f32[32,3,128]{2,1,0:T(4,128)}), f32[32,3,128]{2,1,0:T(4,128)S(1)}, u32[]{:S(2)}, u32[]{:S(2)}) async-start(f32[32,3,128]{2,1,0:T(4,128)} %broadcast_in_dim.4), calls=%async_computation | async-start | bytes 131072 | tf_op jit(solution)/shard_map/all_to_all | solution.py:499
  9.3 2.4 %prep.1 = (f32[32,8,128]{2,1,0:T(8,128)S(1)}, f32[16,128]{1,0:T(8,128)S(1)}, s32[269]{0:T(512)S(1)}) custom-call(s32[32,128]{1,0:T(8,128)} %bitcast.27, f32[32,128]{1,0:T(8,128)} %bitcast.15, s32[4,4096]{1,0:T(4,128)} %bitcast.24), custom_call_target="tpu_custom_call" | custom-call | tf_op jit(solution)/shard_map/prep/pallas_call | solution.py:232
  11.8 5.0 %all-to-all-done.g_ref = f32[32,3,128]{2,1,0:T(4,128)S(1)} async-done(((f32[32,3,128]{2,1,0:T(4,128)}), f32[32,3,128]{2,1,0:T(4,128)S(1)}, u32[]{:S(2)}, u32[]{:S(2)}) %all-to-all-start) | async-done | bytes 49184 | tf_op jit(solution)/shard_map/all_to_all | solution.py:499
  16.8 1.5 %env.2 = f32[32,3,128]{2,1,0:T(4,128)} custom-call(s32[269]{0:T(512)S(1)} %get-tuple-element.24.list_ref, f32[32,3,128]{2,1,0:T(4,128)S(1)} %all-to-all-done.g_ref, f32[32,4,128]{2,1,0:T(4,128)S(1)} %bitcast.14), custom_call_target="tpu_custom_call" | custom-call | flops 2000000 | bytes 200000 | tf_op jit(solution)/shard_map/env/pallas_call | solution.py:293
  18.3 2.5 %all-to-all-start.1 = ((f32[32,3,128]{2,1,0:T(4,128)}), f32[32,3,128]{2,1,0:T(4,128)S(1)}, u32[]{:S(2)}, u32[]{:S(2)}) async-start(f32[32,3,128]{2,1,0:T(4,128)} %env.2), calls=%async_computation.1 | async-start | bytes 131072 | tf_op jit(solution)/shard_map/all_to_all | solution.py:499
  21.0 2.5 %collective-permute-start.1 = (f32[2,8,4,128]{3,2,1,0:T(4,128)S(1)}, f32[2,8,4,128]{3,2,1,0:T(4,128)S(1)}, u32[]{:S(2)}, u32[]{:S(2)}) collective-permute-start(f32[2,8,4,128]{3,2,1,0:T(4,128)S(1)} %get-tuple-element.51), channel_id=1, source_target_pairs={{4,0},{8,4},{12,8},{16,12},{20,16},{24,20},{28,24},{0,28},{5,1},{9... | collective-permute-start | bytes 98312 | tf_op jit(solution)/shard_map/ppermute | solution.py:493
  23.5 1.2 %fast_only.2.f_ref = f32[3,128]{1,0:T(4,128)S(1)} custom-call(f32[32,3,128]{2,1,0:T(4,128)S(1)} %all-to-all-done.g_ref, f32[32,8,128]{2,1,0:T(8,128)S(1)} %get-tuple-element.27.table_ref, f32[16,128]{1,0:T(8,128)S(1)} %get-tuple-element.28.exm_ref), custom_call_target="tpu_custom_call" | custom-call | flops 5242880 | bytes 131072 | tf_op jit(solution)/shard_map/fast_only/pallas_call | solution.py:154
  24.7 3.6 %all-to-all-done.1.e_ref = f32[32,3,128]{2,1,0:T(4,128)S(1)} async-done(((f32[32,3,128]{2,1,0:T(4,128)}), f32[32,3,128]{2,1,0:T(4,128)S(1)}, u32[]{:S(2)}, u32[]{:S(2)}) %all-to-all-start.1) | async-done | bytes 49184 | tf_op jit(solution)/shard_map/all_to_all | solution.py:499
  28.3 0.7 kick.1
  29.0 2.5 %all-to-all-start.2 = ((f32[32,3,128]{2,1,0:T(4,128)}), f32[32,3,128]{2,1,0:T(4,128)S(1)}, u32[]{:S(2)}, u32[]{:S(2)}) async-start(f32[32,3,128]{2,1,0:T(4,128)} %get-tuple-element.29), calls=%async_computation.2 | async-start | bytes 131072 | tf_op jit(solution)/shard_map/all_to_all | solution.py:499
  31.6 1.7 %collective-permute-start.2 = (f32[8,2,4,128]{3,2,1,0:T(4,128)S(1)}, f32[8,2,4,128]{3,2,1,0:T(4,128)S(1)}, u32[]{:S(2)}, u32[]{:S(2)}) collective-permute-start(f32[8,2,4,128]{3,2,1,0:T(4,128)S(1)} %get-tuple-element.46), channel_id=1, source_target_pairs={{0,1},{1,2},{2,3},{3,0},{4,5},{5,6},{6,7},{7,4},{8,9},{9,10},{10,1... | collective-permute-start | bytes 98312 | tf_op jit(solution)/shard_map/ppermute | solution.py:492
  33.3 2.1 %collective-permute-start.3 = (f32[8,2,4,128]{3,2,1,0:T(4,128)S(1)}, f32[8,2,4,128]{3,2,1,0:T(4,128)S(1)}, u32[]{:S(2)}, u32[]{:S(2)}) collective-permute-start(f32[8,2,4,128]{3,2,1,0:T(4,128)S(1)} %get-tuple-element.47), channel_id=1, source_target_pairs={{1,0},{2,1},{3,2},{0,3},{5,4},{6,5},{7,6},{4,7},{9,8},{10,9},{11,1... | collective-permute-start | bytes 98312 | tf_op jit(solution)/shard_map/ppermute | solution.py:493
  35.6 3.8 %all-to-all-done.2.g_ref = f32[32,3,128]{2,1,0:T(4,128)S(1)} async-done(((f32[32,3,128]{2,1,0:T(4,128)}), f32[32,3,128]{2,1,0:T(4,128)S(1)}, u32[]{:S(2)}, u32[]{:S(2)}) %all-to-all-start.2) | async-done | bytes 49184 | tf_op jit(solution)/shard_map/all_to_all | solution.py:499
  39.3 1.8 %fast_step.3 = (f32[32,3,128]{2,1,0:T(4,128)}, f32[3,128]{1,0:T(4,128)}, f32[3,128]{1,0:T(4,128)S(1)}) custom-call(f32[32,3,128]{2,1,0:T(4,128)S(1)} %all-to-all-done.2.g_ref, f32[32,8,128]{2,1,0:T(8,128)S(1)} %get-tuple-element.27.table_ref, f32[16,128]{1,0:T(8,128)S(1)} %get-tuple-element.28.exm_ref, f32[3,128]{1,0:T(4,128)S(1)} %get-tuple-element.30.v_ref), custom_call_target="tpu_custom_call" | custom-call | flops 5242880 | bytes 131072 | tf_op jit(solution)/shard_map/fast_step/pallas_call | solution.py:168
  41.2 2.5 %all-to-all-start.3 = ((f32[32,3,128]{2,1,0:T(4,128)}), f32[32,3,128]{2,1,0:T(4,128)S(1)}, u32[]{:S(2)}, u32[]{:S(2)}) async-start(f32[32,3,128]{2,1,0:T(4,128)} %get-tuple-element.31), calls=%async_computation.3 | async-start | bytes 131072 | tf_op jit(solution)/shard_map/all_to_all | solution.py:499
  43.8 4.3 %slow.4 = (f32[3,2,8,128]{3,2,1,0:T(8,128)S(1)}, f32[16,4,128]{2,1,0:T(4,128)S(1)}) custom-call(s32[32,5]{1,0:T(8,128)S(1)} %bitcast.18, f32[8,12,4,128]{3,2,1,0:T(4,128)S(1)} %pad_maximum_fusion.tab_ref, f32[3,4,8,128]{3,2,1,0:T(8,128)} %vel_ref.3), custom_call_target="tpu_custom_call" | custom-call | flops 13107200 | bytes 1000000 | tf_op jit(solution)/shard_map/slow/pallas_call | solution.py:464
  48.1 4.3 %slow.5 = (f32[3,4,8,128]{3,2,1,0:T(8,128)S(1)}, f32[32,4,128]{2,1,0:T(4,128)S(1)}) custom-call(s32[32,5]{1,0:T(8,128)S(1)} %bitcast.19, f32[8,12,4,128]{3,2,1,0:T(4,128)S(1)} %pad_maximum_fusion.tab_ref, f32[3,4,8,128]{3,2,1,0:T(8,128)} %vel_ref.3, f32[3,2,8,128]{3,2,1,0:T(8,128)S(1)} %get-tuple-element.37.refs_0_, f32[16,4,128]{2,1,0:T(4,128)S(1)} %get-tuple-element.38.refs_1_), custom_call_target="tpu_custom_call" | custom-call | flops 13107200 | bytes 1000000 | tf_op jit(solution)/shard_map/slow/pallas_call | solution.py:464
  52.4 1.8 %fast_step.4 = (f32[32,3,128]{2,1,0:T(4,128)}, f32[3,128]{1,0:T(4,128)}, f32[3,128]{1,0:T(4,128)S(1)}) custom-call(f32[32,3,128]{2,1,0:T(4,128)S(1)} %all-to-all-done.3.g_ref, f32[32,8,128]{2,1,0:T(8,128)S(1)} %get-tuple-element.27.table_ref, f32[16,128]{1,0:T(8,128)S(1)} %get-tuple-element.28.exm_ref, f32[3,128]{1,0:T(4,128)S(1)} %get-tuple-element.32.v_ref), custom_call_target="tpu_custom_call" | custom-call | flops 5242880 | bytes 131072 | tf_op jit(solution)/shard_map/fast_step/pallas_call | solution.py:168
  54.2 5.8 %all-to-all-start.4 = ((f32[32,3,128]{2,1,0:T(4,128)}), f32[32,3,128]{2,1,0:T(4,128)S(1)}, u32[]{:S(2)}, u32[]{:S(2)}) async-start(f32[32,3,128]{2,1,0:T(4,128)} %get-tuple-element.33), calls=%async_computation.4 | async-start | bytes 131072 | tf_op jit(solution)/shard_map/all_to_all | solution.py:499
  60.0 2.4 %collective-permute-start.5 = (f32[2,8,4,128]{3,2,1,0:T(4,128)S(1)}, f32[2,8,4,128]{3,2,1,0:T(4,128)S(1)}, u32[]{:S(2)}, u32[]{:S(2)}) collective-permute-start(f32[2,8,4,128]{3,2,1,0:T(4,128)S(1)} %bitcast.26), channel_id=1, source_target_pairs={{4,0},{8,4},{12,8},{16,12},{20,16},{24,20},{28,24},{0,28},{5,1},{9... | collective-permute-start | bytes 98312 | tf_op jit(solution)/shard_map/ppermute | solution.py:493
  62.5 5.0 %all-to-all-done.4.g_ref = f32[32,3,128]{2,1,0:T(4,128)S(1)} async-done(((f32[32,3,128]{2,1,0:T(4,128)}), f32[32,3,128]{2,1,0:T(4,128)S(1)}, u32[]{:S(2)}, u32[]{:S(2)}) %all-to-all-start.4) | async-done | bytes 49184 | tf_op jit(solution)/shard_map/all_to_all | solution.py:499
  67.5 1.8 %fast_step.5 = (f32[32,3,128]{2,1,0:T(4,128)}, f32[3,128]{1,0:T(4,128)}, f32[3,128]{1,0:T(4,128)S(1)}) custom-call(f32[32,3,128]{2,1,0:T(4,128)S(1)} %all-to-all-done.4.g_ref, f32[32,8,128]{2,1,0:T(8,128)S(1)} %get-tuple-element.27.table_ref, f32[16,128]{1,0:T(8,128)S(1)} %get-tuple-element.28.exm_ref, f32[3,128]{1,0:T(4,128)S(1)} %get-tuple-element.34.v_ref), custom_call_target="tpu_custom_call" | custom-call | flops 5242880 | bytes 131072 | tf_op jit(solution)/shard_map/fast_step/pallas_call | solution.py:168
  69.3 2.5 %all-to-all-start.5 = ((f32[32,3,128]{2,1,0:T(4,128)}), f32[32,3,128]{2,1,0:T(4,128)S(1)}, u32[]{:S(2)}, u32[]{:S(2)}) async-start(f32[32,3,128]{2,1,0:T(4,128)} %get-tuple-element.36), calls=%async_computation.5 | async-start | bytes 131072 | tf_op jit(solution)/shard_map/all_to_all | solution.py:499
  71.9 1.7 %collective-permute-start.6 = (f32[8,2,4,128]{3,2,1,0:T(4,128)S(1)}, f32[8,2,4,128]{3,2,1,0:T(4,128)S(1)}, u32[]{:S(2)}, u32[]{:S(2)}) collective-permute-start(f32[8,2,4,128]{3,2,1,0:T(4,128)S(1)} %get-tuple-element.44), channel_id=1, source_target_pairs={{0,1},{1,2},{2,3},{3,0},{4,5},{5,6},{6,7},{7,4},{8,9},{9,10},{10,1... | collective-permute-start | bytes 98312 | tf_op jit(solution)/shard_map/ppermute | solution.py:492
  73.7 2.1 %collective-permute-start.7 = (f32[8,2,4,128]{3,2,1,0:T(4,128)S(1)}, f32[8,2,4,128]{3,2,1,0:T(4,128)S(1)}, u32[]{:S(2)}, u32[]{:S(2)}) collective-permute-start(f32[8,2,4,128]{3,2,1,0:T(4,128)S(1)} %get-tuple-element.45), channel_id=1, source_target_pairs={{1,0},{2,1},{3,2},{0,3},{5,4},{6,5},{7,6},{4,7},{9,8},{10,9},{11,1... | collective-permute-start | bytes 98312 | tf_op jit(solution)/shard_map/ppermute | solution.py:493
  75.8 3.9 %all-to-all-done.5.g_ref = f32[32,3,128]{2,1,0:T(4,128)S(1)} async-done(((f32[32,3,128]{2,1,0:T(4,128)}), f32[32,3,128]{2,1,0:T(4,128)S(1)}, u32[]{:S(2)}, u32[]{:S(2)}) %all-to-all-start.5) | async-done | bytes 49184 | tf_op jit(solution)/shard_map/all_to_all | solution.py:499
  79.7 1.5 %env.3 = f32[32,3,128]{2,1,0:T(4,128)} custom-call(s32[269]{0:T(512)S(1)} %get-tuple-element.24.list_ref, f32[32,3,128]{2,1,0:T(4,128)S(1)} %all-to-all-done.5.g_ref, f32[32,4,128]{2,1,0:T(4,128)S(1)} %get-tuple-element.39.cells_ref), custom_call_target="tpu_custom_call" | custom-call | flops 2000000 | bytes 200000 | tf_op jit(solution)/shard_map/env/pallas_call | solution.py:293
  81.2 2.7 %all-to-all-start.6 = ((f32[32,3,128]{2,1,0:T(4,128)}), f32[32,3,128]{2,1,0:T(4,128)S(1)}, u32[]{:S(2)}, u32[]{:S(2)}) async-start(f32[32,3,128]{2,1,0:T(4,128)} %env.3), calls=%async_computation.6 | async-start | bytes 131072 | tf_op jit(solution)/shard_map/all_to_all | solution.py:499
  84.0 4.2 %slow.6.refs_0_ = f32[3,2,8,128]{3,2,1,0:T(8,128)S(1)} custom-call(s32[32,5]{1,0:T(8,128)S(1)} %bitcast.20, f32[8,12,4,128]{3,2,1,0:T(4,128)S(1)} %pad_maximum_fusion.1.tab_ref, f32[3,4,8,128]{3,2,1,0:T(8,128)S(1)} %get-tuple-element.41.vel_ref), custom_call_target="tpu_custom_call" | custom-call | flops 13107200 | bytes 1000000 | tf_op jit(solution)/shard_map/slow/pallas_call | solution.py:464
  88.2 4.8 %slow.7 = (f32[3,4,8,128]{3,2,1,0:T(8,128)}, f32[3,4,8,128]{3,2,1,0:T(8,128)}) custom-call(s32[32,5]{1,0:T(8,128)S(1)} %bitcast.21, f32[8,12,4,128]{3,2,1,0:T(4,128)S(1)} %pad_maximum_fusion.1.tab_ref, f32[3,4,8,128]{3,2,1,0:T(8,128)S(1)} %get-tuple-element.41.vel_ref, f32[3,2,8,128]{3,2,1,0:T(8,128)S(1)} %slow.6.refs_0_), custom_call_target="tpu_custom_call" | custom-call | flops 13107200 | bytes 1000000 | tf_op jit(solution)/shard_map/slow/pallas_call | solution.py:464
  93.0 1.2 %fast_only.3.f_ref = f32[3,128]{1,0:T(4,128)S(1)} custom-call(f32[32,3,128]{2,1,0:T(4,128)S(1)} %all-to-all-done.5.g_ref, f32[32,8,128]{2,1,0:T(8,128)S(1)} %get-tuple-element.27.table_ref, f32[16,128]{1,0:T(8,128)S(1)} %get-tuple-element.28.exm_ref), custom_call_target="tpu_custom_call" | custom-call | flops 5242880 | bytes 131072 | tf_op jit(solution)/shard_map/fast_only/pallas_call | solution.py:154
  (35 shorter events, 1.2 us)
Async XLA Ops:
  1.9 7.3 %copy-start.4 = (f32[3,4,8,128]{3,2,1,0:T(8,128)S(1)}, f32[3,4,8,128]{3,2,1,0:T(8,128)}, u32[]{:S(2)}) copy-start(f32[3,4,8,128]{3,2,1,0:T(8,128)} %param.14) | copy-start | bytes 147460
  1.9 14.8 %all-to-all-start = ((f32[32,3,128]{2,1,0:T(4,128)}), f32[32,3,128]{2,1,0:T(4,128)S(1)}, u32[]{:S(2)}, u32[]{:S(2)}) async-start(f32[32,3,128]{2,1,0:T(4,128)} %broadcast_in_dim.4), calls=%async_computation | async-start | bytes 131072 | tf_op jit(solution)/shard_map/all_to_all | solution.py:499
  9.3 2.4 %copy-start.3 = (f32[4,8,128]{2,1,0:T(8,128)S(1)}, f32[4,8,128]{2,1,0:T(8,128)}, u32[]{:S(2)}) copy-start(f32[4,8,128]{2,1,0:T(8,128)} %param.16) | copy-start | bytes 49156
  18.3 10.0 %all-to-all-start.1 = ((f32[32,3,128]{2,1,0:T(4,128)}), f32[32,3,128]{2,1,0:T(4,128)S(1)}, u32[]{:S(2)}, u32[]{:S(2)}) async-start(f32[32,3,128]{2,1,0:T(4,128)} %env.2), calls=%async_computation.1 | async-start | bytes 131072 | tf_op jit(solution)/shard_map/all_to_all | solution.py:499
  20.8 10.7 %collective-permute-start = (f32[2,8,4,128]{3,2,1,0:T(4,128)S(1)}, f32[2,8,4,128]{3,2,1,0:T(4,128)S(1)}, u32[]{:S(2)}, u32[]{:S(2)}) collective-permute-start(f32[2,8,4,128]{3,2,1,0:T(4,128)S(1)} %get-tuple-element.50), channel_id=1, source_target_pairs={{0,4},{4,8},{8,12},{12,16},{16,20},{20,24},{24,28},{28,0},{1,5},{5... | collective-permute-start | bytes 98312 | tf_op jit(solution)/shard_map/ppermute | solution.py:492
  21.0 10.6 %collective-permute-start.1 = (f32[2,8,4,128]{3,2,1,0:T(4,128)S(1)}, f32[2,8,4,128]{3,2,1,0:T(4,128)S(1)}, u32[]{:S(2)}, u32[]{:S(2)}) collective-permute-start(f32[2,8,4,128]{3,2,1,0:T(4,128)S(1)} %get-tuple-element.51), channel_id=1, source_target_pairs={{4,0},{8,4},{12,8},{16,12},{20,16},{24,20},{28,24},{0,28},{5,1},{9... | collective-permute-start | bytes 98312 | tf_op jit(solution)/shard_map/ppermute | solution.py:493
  23.5 4.8 %copy-start = (f32[4096]{0:T(1024)S(1)}, f32[4096]{0:T(1024)}, u32[]{:S(2)}) copy-start(f32[4096]{0:T(1024)} %param.11) | copy-start | bytes 49156
  23.5 4.8 %copy-start.1 = (f32[3,128]{1,0:T(4,128)S(1)}, f32[3,128]{1,0:T(4,128)}, u32[]{:S(2)}) copy-start(f32[3,128]{1,0:T(4,128)} %p_ref.1) | copy-start | bytes 4612
  23.5 4.8 %copy-start.2 = (f32[3,128]{1,0:T(4,128)S(1)}, f32[3,128]{1,0:T(4,128)}, u32[]{:S(2)}) copy-start(f32[3,128]{1,0:T(4,128)} %v_ref.1) | copy-start | bytes 4612
  29.0 10.3 %all-to-all-start.2 = ((f32[32,3,128]{2,1,0:T(4,128)}), f32[32,3,128]{2,1,0:T(4,128)S(1)}, u32[]{:S(2)}, u32[]{:S(2)}) async-start(f32[32,3,128]{2,1,0:T(4,128)} %get-tuple-element.29), calls=%async_computation.2 | async-start | bytes 131072 | tf_op jit(solution)/shard_map/all_to_all | solution.py:499
  31.5 3.9 %copy-start.5 = (s32[4,8,5]{1,0,2:T(4,128)S(1)}, s32[4,8,5]{1,0,2:T(4,128)}, u32[]{:S(2)}) copy-start(s32[4,8,5]{1,0,2:T(4,128)} %param.17) | copy-start | bytes 1924
  31.6 12.1 %collective-permute-start.2 = (f32[8,2,4,128]{3,2,1,0:T(4,128)S(1)}, f32[8,2,4,128]{3,2,1,0:T(4,128)S(1)}, u32[]{:S(2)}, u32[]{:S(2)}) collective-permute-start(f32[8,2,4,128]{3,2,1,0:T(4,128)S(1)} %get-tuple-element.46), channel_id=1, source_target_pairs={{0,1},{1,2},{2,3},{3,0},{4,5},{5,6},{6,7},{7,4},{8,9},{9,10},{10,1... | collective-permute-start | bytes 98312 | tf_op jit(solution)/shard_map/ppermute | solution.py:492
  33.3 10.4 %collective-permute-start.3 = (f32[8,2,4,128]{3,2,1,0:T(4,128)S(1)}, f32[8,2,4,128]{3,2,1,0:T(4,128)S(1)}, u32[]{:S(2)}, u32[]{:S(2)}) collective-permute-start(f32[8,2,4,128]{3,2,1,0:T(4,128)S(1)} %get-tuple-element.47), channel_id=1, source_target_pairs={{1,0},{2,1},{3,2},{0,3},{5,4},{6,5},{7,6},{4,7},{9,8},{10,9},{11,1... | collective-permute-start | bytes 98312 | tf_op jit(solution)/shard_map/ppermute | solution.py:493
  41.2 11.2 %all-to-all-start.3 = ((f32[32,3,128]{2,1,0:T(4,128)}), f32[32,3,128]{2,1,0:T(4,128)S(1)}, u32[]{:S(2)}, u32[]{:S(2)}) async-start(f32[32,3,128]{2,1,0:T(4,128)} %get-tuple-element.31), calls=%async_computation.3 | async-start | bytes 131072 | tf_op jit(solution)/shard_map/all_to_all | solution.py:499
  54.2 13.3 %all-to-all-start.4 = ((f32[32,3,128]{2,1,0:T(4,128)}), f32[32,3,128]{2,1,0:T(4,128)S(1)}, u32[]{:S(2)}, u32[]{:S(2)}) async-start(f32[32,3,128]{2,1,0:T(4,128)} %get-tuple-element.33), calls=%async_computation.4 | async-start | bytes 131072 | tf_op jit(solution)/shard_map/all_to_all | solution.py:499
  60.0 11.8 %collective-permute-start.5 = (f32[2,8,4,128]{3,2,1,0:T(4,128)S(1)}, f32[2,8,4,128]{3,2,1,0:T(4,128)S(1)}, u32[]{:S(2)}, u32[]{:S(2)}) collective-permute-start(f32[2,8,4,128]{3,2,1,0:T(4,128)S(1)} %bitcast.26), channel_id=1, source_target_pairs={{4,0},{8,4},{12,8},{16,12},{20,16},{24,20},{28,24},{0,28},{5,1},{9... | collective-permute-start | bytes 98312 | tf_op jit(solution)/shard_map/ppermute | solution.py:493
  62.5 9.4 %collective-permute-start.4 = (f32[2,8,4,128]{3,2,1,0:T(4,128)S(1)}, f32[2,8,4,128]{3,2,1,0:T(4,128)S(1)}, u32[]{:S(2)}, u32[]{:S(2)}) collective-permute-start(f32[2,8,4,128]{3,2,1,0:T(4,128)S(1)} %bitcast.25), channel_id=1, source_target_pairs={{0,4},{4,8},{8,12},{12,16},{16,20},{20,24},{24,28},{28,0},{1,5},{5... | collective-permute-start | bytes 98312 | tf_op jit(solution)/shard_map/ppermute | solution.py:492
  69.3 10.3 %all-to-all-start.5 = ((f32[32,3,128]{2,1,0:T(4,128)}), f32[32,3,128]{2,1,0:T(4,128)S(1)}, u32[]{:S(2)}, u32[]{:S(2)}) async-start(f32[32,3,128]{2,1,0:T(4,128)} %get-tuple-element.36), calls=%async_computation.5 | async-start | bytes 131072 | tf_op jit(solution)/shard_map/all_to_all | solution.py:499
  71.9 12.0 %collective-permute-start.6 = (f32[8,2,4,128]{3,2,1,0:T(4,128)S(1)}, f32[8,2,4,128]{3,2,1,0:T(4,128)S(1)}, u32[]{:S(2)}, u32[]{:S(2)}) collective-permute-start(f32[8,2,4,128]{3,2,1,0:T(4,128)S(1)} %get-tuple-element.44), channel_id=1, source_target_pairs={{0,1},{1,2},{2,3},{3,0},{4,5},{5,6},{6,7},{7,4},{8,9},{9,10},{10,1... | collective-permute-start | bytes 98312 | tf_op jit(solution)/shard_map/ppermute | solution.py:492
  73.7 10.2 %collective-permute-start.7 = (f32[8,2,4,128]{3,2,1,0:T(4,128)S(1)}, f32[8,2,4,128]{3,2,1,0:T(4,128)S(1)}, u32[]{:S(2)}, u32[]{:S(2)}) collective-permute-start(f32[8,2,4,128]{3,2,1,0:T(4,128)S(1)} %get-tuple-element.45), channel_id=1, source_target_pairs={{1,0},{2,1},{3,2},{0,3},{5,4},{6,5},{7,6},{4,7},{9,8},{10,9},{11,1... | collective-permute-start | bytes 98312 | tf_op jit(solution)/shard_map/ppermute | solution.py:493
  81.2 13.0 %all-to-all-start.6 = ((f32[32,3,128]{2,1,0:T(4,128)}), f32[32,3,128]{2,1,0:T(4,128)S(1)}, u32[]{:S(2)}, u32[]{:S(2)}) async-start(f32[32,3,128]{2,1,0:T(4,128)} %env.3), calls=%async_computation.6 | async-start | bytes 131072 | tf_op jit(solution)/shard_map/all_to_all | solution.py:499
